TPU v7x, 32 devices: a whole 2x2x4 slice. The times are simulated.
32 devices in a mesh: dp: 4 (over z), mp: 8 (over y, x, core).
Axes of the slice: x: 2, y: 2, z: 4, core: 2. Of those that a mesh axis runs over, the one named last changes fastest.
Arguments:
- block_input: bfloat16 [10752, 2048], P('dp'), may hold values from -6 to 6
- cotangent: bfloat16 [10752, 2048], P(('dp', 'mp')), may hold values from -6 to 6
- prefix_len: int32 [12], P('dp'), may hold values from 1 to 896
- cluster_id: int32 [12], replicated, may hold values from 0 to 5
- positions: int32 [10752], P('dp'), may hold values from 0 to 1790, as said below
- step_count: int32 [1], replicated, may hold values from 2 to 20
- master_qkv: float32 [3, 2048, 2048], P(None, 'dp', 'mp'), may hold values from -0.125 to 0.125
- first_qkv: float32 [3, 2048, 2048], P(None, 'dp', 'mp')
- second_qkv: float32 [3, 2048, 2048], P(None, 'dp', 'mp'), as said below
- master_out: float32 [2048, 2048], P('mp', 'dp'), may hold values from -3 to 3
- first_out: float32 [2048, 2048], P('mp', 'dp')
- second_out: float32 [2048, 2048], P('mp', 'dp'), as said below
- master_gateup: float32 [2, 2048, 5632], P(None, 'dp', 'mp'), as said below
- first_gateup: float32 [2, 2048, 5632], P(None, 'dp', 'mp'), as said below
- second_gateup: float32 [2, 2048, 5632], P(None, 'dp', 'mp'), as said below
- master_down: float32 [5632, 2048], P('mp', 'dp'), as said below
- first_down: float32 [5632, 2048], P('mp', 'dp'), as said below
- second_down: float32 [5632, 2048], P('mp', 'dp'), as said below
- master_norm: float32 [4, 2048], replicated, as said below
- first_norm: float32 [4, 2048], replicated
- second_norm: float32 [4, 2048], replicated, as said below
Outputs:
- block_output: bfloat16 [10752, 2048], P(('dp', 'mp'))
- grad_input: bfloat16 [10752, 2048], P(('dp', 'mp'))
- grad_qkv: float32 [3, 2048, 2048], P(None, 'dp', 'mp')
- new_qkv: float32 [3, 2048, 2048], P(None, 'dp', 'mp')
- new_first_qkv: float32 [3, 2048, 2048], P(None, 'dp', 'mp')
- new_second_qkv: float32 [3, 2048, 2048], P(None, 'dp', 'mp')
- grad_out: float32 [2048, 2048], P('mp', 'dp')
- new_out: float32 [2048, 2048], P('mp', 'dp')
- new_first_out: float32 [2048, 2048], P('mp', 'dp')
- new_second_out: float32 [2048, 2048], P('mp', 'dp')
- grad_gateup: float32 [2, 2048, 5632], P(None, 'dp', 'mp')
- new_gateup: float32 [2, 2048, 5632], P(None, 'dp', 'mp')
- new_first_gateup: float32 [2, 2048, 5632], P(None, 'dp', 'mp')
- new_second_gateup: float32 [2, 2048, 5632], P(None, 'dp', 'mp')
- grad_down: float32 [5632, 2048], P('mp', 'dp')
- new_down: float32 [5632, 2048], P('mp', 'dp')
- new_first_down: float32 [5632, 2048], P('mp', 'dp')
- new_second_down: float32 [5632, 2048], P('mp', 'dp')
- grad_norm: float32 [4, 2048], replicated
- new_norm: float32 [4, 2048], replicated
- new_first_norm: float32 [4, 2048], replicated
- new_second_norm: float32 [4, 2048], replicated
Inputs may be any that keep to these rules, and one draw needn't show every extreme that they name: `positions`: within each protein of 896 tokens the first position is 0 and each next one is larger by 1 or 2; in one protein every step is 2. `master_gateup`: hidden units from 5461 on are zero. `master_down`: hidden units from 5461 on are zero. `first_gateup`: hidden units from 5461 on are zero. `second_gateup`: hidden units from 5461 on are zero, all others positive. `first_down`: hidden units from 5461 on are zero. `second_down`: hidden units from 5461 on are zero, all others positive. `second_qkv`: Positive. `second_out`: Positive. `second_norm`: Positive. `master_norm`: gains in rows 0 and 2 are positive.
All inputs are finite; a program needn't handle non-finite values.
Results may differ from a plain program's by a relative error of at most 0.022.
Values may be sent and summed in bfloat16 or wider, within the bound.
A program may use at most 256 MiB of HBM per device.

v0:
```python
import math

import jax
import jax.numpy as jnp
from jax import lax
from jax.sharding import PartitionSpec as P

D = 2048
HEADS = 16
HEAD_DIM = 128
FF = 5632
DEPTH = 24
LEN = 896


beta_one = 0.9
beta_two = 0.95
adam_epsilon = 1e-08
decay_weight = 0.1
norm_epsilon = 1e-05


def norm_forward(hidden_rows, gain, offset):
    centre = hidden_rows - jnp.mean(hidden_rows, axis=-1, keepdims=True)
    inv_std = lax.rsqrt(jnp.mean(centre * centre, axis=-1, keepdims=True) + norm_epsilon)
    normed = centre * inv_std
    return (normed * gain + offset, normed, inv_std)


def norm_backward(grad_rows, normed, inv_std, gain):
    grad_normed = grad_rows * gain
    first_term = jnp.mean(grad_normed, axis=-1, keepdims=True)
    second_term = jnp.mean(grad_normed * normed, axis=-1, keepdims=True)
    grad_hidden = inv_std * (grad_normed - first_term - normed * second_term)
    return (grad_hidden, jnp.sum(grad_rows * normed, axis=0), jnp.sum(grad_rows, axis=0))


def rotate_half(values):
    middle = values.shape[-1] // 2
    return jnp.concatenate([-values[..., middle:], values[..., :middle]], axis=-1)


def rotate_back(values):
    middle = values.shape[-1] // 2
    return jnp.concatenate([values[..., middle:], -values[..., :middle]], axis=-1)


def rope_tables(positions):
    ladder = jnp.arange(HEAD_DIM // 2, dtype=jnp.float32)
    inverse = jnp.exp(ladder * (-2.0 * math.log(10000.0) / HEAD_DIM))
    angles = positions.astype(jnp.float32)[:, None] * inverse[None, :]
    cos_half = jnp.cos(angles)
    sin_half = jnp.sin(angles)
    return (
        jnp.concatenate([cos_half, cos_half], axis=-1),
        jnp.concatenate([sin_half, sin_half], axis=-1),
    )


def apply_rope(values, cos_table, sin_table):
    return values * cos_table[:, None, :] + rotate_half(values) * sin_table[:, None, :]


def rope_back(grads, cos_table, sin_table):
    return grads * cos_table[:, None, :] + rotate_back(grads * sin_table[:, None, :])


def gelu_tanh(values):
    return jax.nn.gelu(values, approximate=True)


def adamw_step(old_master, old_first, old_second, grad_sum, learn_rate, step_value):
    first_new = beta_one * old_first + (1.0 - beta_one) * grad_sum
    second_new = beta_two * old_second + (1.0 - beta_two) * grad_sum * grad_sum
    fix_first = 1.0 - jnp.power(beta_one, step_value)
    fix_second = 1.0 - jnp.power(beta_two, step_value)
    update = (
        first_new / fix_first / (jnp.sqrt(second_new / fix_second) + adam_epsilon)
        + decay_weight * old_master
    )
    return (old_master - learn_rate * update, first_new, second_new)


def body(
    block_input,
    cotangent,
    prefix_len,
    cluster_id,
    positions,
    step_count,
    master_qkv,
    first_qkv,
    second_qkv,
    master_out,
    first_out,
    second_out,
    master_gateup,
    first_gateup,
    second_gateup,
    master_down,
    first_down,
    second_down,
    master_norm,
    first_norm,
    second_norm,
):
    w_qkv, w_out, w_gateup, w_down = (
        lax.all_gather(master_qkv.astype(jnp.bfloat16), "dp", axis=1, tiled=True),
        lax.all_gather(master_out.astype(jnp.bfloat16), "dp", axis=1, tiled=True),
        lax.all_gather(master_gateup.astype(jnp.bfloat16), "dp", axis=1, tiled=True),
        lax.all_gather(master_down.astype(jnp.bfloat16), "dp", axis=1, tiled=True),
    )
    w_norm = lax.optimization_barrier(master_norm.astype(jnp.bfloat16)).astype(jnp.float32)
    token_count = block_input.shape[0]
    protein_count = token_count // LEN
    share_rows = cotangent.shape[0]
    share_start = lax.axis_index("mp") * share_rows
    head_count = w_qkv.shape[2] // HEAD_DIM
    width_heads = head_count * HEAD_DIM
    deep_alpha = math.sqrt(2.0 * DEPTH)
    score_scale = 1.0 / math.sqrt(HEAD_DIM)
    cos_table, sin_table = rope_tables(positions)
    projected = jnp.einsum("td,jdc->jtc", block_input, w_qkv, preferred_element_type=jnp.float32)
    shaped = projected.reshape(3, token_count, head_count, HEAD_DIM)
    queries = (apply_rope(shaped[0], cos_table, sin_table) * score_scale).astype(jnp.bfloat16)
    key_rows = apply_rope(shaped[1], cos_table, sin_table).astype(jnp.bfloat16)
    value_rows = shaped[2].astype(jnp.bfloat16)
    row_ids = jnp.arange(LEN)[:, None]
    col_ids = jnp.arange(LEN)[None, :]
    attended_parts = []
    log_totals = []
    for protein in range(protein_count):
        row_slice = slice(protein * LEN, (protein + 1) * LEN)
        visible = (col_ids < prefix_len[protein]) | (col_ids <= row_ids)
        scores = jnp.einsum(
            "qhd,khd->hqk",
            queries[row_slice],
            key_rows[row_slice],
            preferred_element_type=jnp.float32,
        )
        scores = jnp.where(visible[None], scores, -1e30)
        row_peak = jnp.max(scores, axis=-1, keepdims=True)
        expo_rows = jnp.exp(scores - row_peak)
        totals = jnp.sum(expo_rows, axis=-1, keepdims=True)
        attn_probs = (expo_rows / totals).astype(jnp.bfloat16)
        attended_parts.append(
            jnp.einsum(
                "hqk,khd->qhd",
                attn_probs,
                value_rows[row_slice],
                preferred_element_type=jnp.float32,
            )
        )
        log_totals.append(row_peak + jnp.log(totals))
    attended = (
        jnp.concatenate(attended_parts, axis=0)
        .reshape(token_count, width_heads)
        .astype(jnp.bfloat16)
    )
    attn_part = jnp.dot(attended, w_out, preferred_element_type=jnp.float32)
    input_share = lax.dynamic_slice_in_dim(block_input, share_start, share_rows, 0).astype(
        jnp.float32
    )
    attn_share = lax.psum_scatter(
        attn_part.astype(jnp.bfloat16), "mp", scatter_dimension=0, tiled=True
    ).astype(jnp.float32)
    middle_share, normed_one, inv_one = norm_forward(
        deep_alpha * input_share + attn_share, w_norm[0], w_norm[1]
    )
    middle_low = lax.all_gather(middle_share.astype(jnp.bfloat16), "mp", axis=0, tiled=True)
    gateup = jnp.einsum("td,jdf->jtf", middle_low, w_gateup, preferred_element_type=jnp.float32)
    gate_rows = gateup[0]
    up_rows = gateup[1]
    activated, gelu_pull = jax.vjp(gelu_tanh, gate_rows)
    hidden = (activated * up_rows).astype(jnp.bfloat16)
    ffn_part = jnp.dot(hidden, w_down, preferred_element_type=jnp.float32)
    ffn_share = lax.psum_scatter(
        ffn_part.astype(jnp.bfloat16), "mp", scatter_dimension=0, tiled=True
    ).astype(jnp.float32)
    out_share, normed_two, inv_two = norm_forward(
        deep_alpha * middle_share + ffn_share, w_norm[2], w_norm[3]
    )
    block_output = out_share.astype(jnp.bfloat16)
    matches = (cluster_id[:, None] == cluster_id[None, :]).astype(jnp.float32)
    counts = jnp.sum(matches, axis=1)
    group_counts = lax.dynamic_slice_in_dim(
        counts, lax.axis_index("dp") * protein_count, protein_count, 0
    )
    row_protein = (share_start + jnp.arange(share_rows)) // LEN
    one_hot = (row_protein[:, None] == jnp.arange(protein_count)[None, :]).astype(jnp.float32)
    row_weight = jnp.sum(one_hot * (1.0 / group_counts)[None, :], axis=1)
    grad_output = cotangent.astype(jnp.float32) * row_weight[:, None]
    grad_h2, grad_gain_two, grad_bias_two = norm_backward(
        grad_output, normed_two, inv_two, w_norm[2]
    )
    ffn_grad_full = lax.all_gather(grad_h2.astype(jnp.bfloat16), "mp", axis=0, tiled=True)
    grad_down_part = jnp.einsum(
        "tf,td->fd", hidden, ffn_grad_full, preferred_element_type=jnp.float32
    )
    grad_hidden = jnp.einsum("td,fd->tf", ffn_grad_full, w_down, preferred_element_type=jnp.float32)
    grad_gate = gelu_pull(grad_hidden * up_rows)[0]
    grad_up = grad_hidden * activated
    grad_gateup_rows = jnp.stack([grad_gate, grad_up]).astype(jnp.bfloat16)
    grad_gateup_part = jnp.einsum(
        "td,jtf->jdf", middle_low, grad_gateup_rows, preferred_element_type=jnp.float32
    )
    middle_grad_part = jnp.einsum(
        "jtf,jdf->td", grad_gateup_rows, w_gateup, preferred_element_type=jnp.float32
    )
    middle_grad = (
        lax.psum_scatter(
            middle_grad_part.astype(jnp.bfloat16), "mp", scatter_dimension=0, tiled=True
        ).astype(jnp.float32)
        + deep_alpha * grad_h2
    )
    grad_h1, grad_gain_one, grad_bias_one = norm_backward(
        middle_grad, normed_one, inv_one, w_norm[0]
    )
    attn_grad_full = lax.all_gather(grad_h1.astype(jnp.bfloat16), "mp", axis=0, tiled=True)
    grad_out_part = jnp.einsum(
        "tc,td->cd", attended, attn_grad_full, preferred_element_type=jnp.float32
    )
    grad_attended = (
        jnp.einsum("td,cd->tc", attn_grad_full, w_out, preferred_element_type=jnp.float32)
        .astype(jnp.bfloat16)
        .reshape(token_count, head_count, HEAD_DIM)
    )
    query_grads = []
    key_grads = []
    value_grads = []
    for protein in range(protein_count):
        row_slice = slice(protein * LEN, (protein + 1) * LEN)
        visible = (col_ids < prefix_len[protein]) | (col_ids <= row_ids)
        scores = jnp.einsum(
            "qhd,khd->hqk",
            queries[row_slice],
            key_rows[row_slice],
            preferred_element_type=jnp.float32,
        )
        scores = jnp.where(visible[None], scores, -1e30)
        probs_full = jnp.exp(scores - log_totals[protein])
        probs_low = probs_full.astype(jnp.bfloat16)
        grad_slice = grad_attended[row_slice]
        value_grads.append(
            jnp.einsum("hqk,qhd->khd", probs_low, grad_slice, preferred_element_type=jnp.float32)
        )
        prob_grads = jnp.einsum(
            "qhd,khd->hqk", grad_slice, value_rows[row_slice], preferred_element_type=jnp.float32
        )
        centre_term = jnp.sum(probs_full * prob_grads, axis=-1, keepdims=True)
        score_grads = (probs_full * (prob_grads - centre_term)).astype(jnp.bfloat16)
        query_grads.append(
            jnp.einsum(
                "hqk,khd->qhd", score_grads, key_rows[row_slice], preferred_element_type=jnp.float32
            )
        )
        key_grads.append(
            jnp.einsum(
                "hqk,qhd->khd", score_grads, queries[row_slice], preferred_element_type=jnp.float32
            )
        )
    grad_query = rope_back(jnp.concatenate(query_grads, axis=0), cos_table, sin_table) * score_scale
    grad_key = rope_back(jnp.concatenate(key_grads, axis=0), cos_table, sin_table)
    grad_value = jnp.concatenate(value_grads, axis=0)
    grad_proj = (
        jnp.stack([grad_query, grad_key, grad_value])
        .reshape(3, token_count, width_heads)
        .astype(jnp.bfloat16)
    )
    grad_qkv_part = jnp.einsum(
        "td,jtc->jdc", block_input, grad_proj, preferred_element_type=jnp.float32
    )
    input_grad_part = jnp.einsum(
        "jtc,jdc->td", grad_proj, w_qkv, preferred_element_type=jnp.float32
    )
    input_grad = (
        lax.psum_scatter(
            input_grad_part.astype(jnp.bfloat16), "mp", scatter_dimension=0, tiled=True
        ).astype(jnp.float32)
        + deep_alpha * grad_h1
    )
    grad_input = input_grad.astype(jnp.bfloat16)
    norm_terms = jnp.stack([grad_gain_one, grad_bias_one, grad_gain_two, grad_bias_two])
    grad_norm = lax.psum(norm_terms, ("dp", "mp"))
    red_qkv, red_out, red_gateup, red_down = (
        lax.psum_scatter(
            grad_qkv_part.astype(jnp.bfloat16), "dp", scatter_dimension=1, tiled=True
        ).astype(jnp.float32),
        lax.psum_scatter(
            grad_out_part.astype(jnp.bfloat16), "dp", scatter_dimension=1, tiled=True
        ).astype(jnp.float32),
        lax.psum_scatter(
            grad_gateup_part.astype(jnp.bfloat16), "dp", scatter_dimension=1, tiled=True
        ).astype(jnp.float32),
        lax.psum_scatter(
            grad_down_part.astype(jnp.bfloat16), "dp", scatter_dimension=1, tiled=True
        ).astype(jnp.float32),
    )
    step_value = step_count[0].astype(jnp.float32)
    rate_qkv = D ** (-0.5)
    rate_out = max(HEADS * HEAD_DIM // 512, 1) ** (-0.5)
    rate_gateup = D ** (-0.5)
    rate_down = max(FF // 64, 1) ** (-0.5)
    rate_norm = 1.0
    new_qkv, new_first_qkv, new_second_qkv = adamw_step(
        master_qkv, first_qkv, second_qkv, red_qkv, rate_qkv, step_value
    )
    new_out, new_first_out, new_second_out = adamw_step(
        master_out, first_out, second_out, red_out, rate_out, step_value
    )
    new_gateup, new_first_gateup, new_second_gateup = adamw_step(
        master_gateup, first_gateup, second_gateup, red_gateup, rate_gateup, step_value
    )
    new_down, new_first_down, new_second_down = adamw_step(
        master_down, first_down, second_down, red_down, rate_down, step_value
    )
    new_norm, new_first_norm, new_second_norm = adamw_step(
        master_norm, first_norm, second_norm, grad_norm, rate_norm, step_value
    )
    return (
        block_output,
        grad_input,
        red_qkv,
        new_qkv,
        new_first_qkv,
        new_second_qkv,
        red_out,
        new_out,
        new_first_out,
        new_second_out,
        red_gateup,
        new_gateup,
        new_first_gateup,
        new_second_gateup,
        red_down,
        new_down,
        new_first_down,
        new_second_down,
        grad_norm,
        new_norm,
        new_first_norm,
        new_second_norm,
    )


def solution(mesh):
    placed = (
        P("dp", None),
        P(("dp", "mp"), None),
        P("dp"),
        P(),
        P("dp"),
        P(),
        P(None, "dp", "mp"),
        P(None, "dp", "mp"),
        P(None, "dp", "mp"),
        P("mp", "dp"),
        P("mp", "dp"),
        P("mp", "dp"),
        P(None, "dp", "mp"),
        P(None, "dp", "mp"),
        P(None, "dp", "mp"),
        P("mp", "dp"),
        P("mp", "dp"),
        P("mp", "dp"),
        P(),
        P(),
        P(),
    )
    return jax.shard_map(
        body,
        mesh=mesh,
        in_specs=placed,
        out_specs=(
            P(("dp", "mp"), None),
            P(("dp", "mp"), None),
            P(None, "dp", "mp"),
            P(None, "dp", "mp"),
            P(None, "dp", "mp"),
            P(None, "dp", "mp"),
            P("mp", "dp"),
            P("mp", "dp"),
            P("mp", "dp"),
            P("mp", "dp"),
            P(None, "dp", "mp"),
            P(None, "dp", "mp"),
            P(None, "dp", "mp"),
            P(None, "dp", "mp"),
            P("mp", "dp"),
            P("mp", "dp"),
            P("mp", "dp"),
            P("mp", "dp"),
            P(),
            P(),
            P(),
            P(),
        ),
        check_vma=False,
    )
```

profile of v0, /device:TPU:0, one launch (start us, length us, event | category | flops | bytes accessed | tf_op | source)
XLA Modules:
  0.0 1192.8 jit_solution(10545651134449470549)
XLA Ops:
  23.6 53.1 %all-gather.8.cloned.1.call-done = bf16[3,2048,256]{1,2,0:T(8,128)(2,1)} async-done(((bf16[3,512,256]{1,2,0:T(8,128)(2,1)}), bf16[3,2048,256]{1,2,0:T(8,128)(2,1)}) %all-gather.8.cloned.1.call-update) | async-done | bytes 3145744 | tf_op jit(solution)/shard_map/all_gather | solution.py:108
  76.7 15.9 %fusion.144 = (bf16[3,2688,256]{1,2,0:T(8,128)(2,1)S(1)}, f32[3,2688,256]{1,2,0:T(8,128)}) fusion(bf16[3,2048,256]{1,2,0:T(8,128)(2,1)} %all-gather.8.cloned.1.call-done, bf16[2688,2048]{1,0:T(8,128)(2,1)} %param.21), kind=kOutput, calls=%fused_computation.233 | convolution fusion | flops 8457781248 | bytes 26542080 | tf_op jit(solution)/shard_map/td,jdc->jtc/dot_general | solution.py:123
  104.7 8.5 slice_negate_fusion.2
  134.3 8.9 convolution_convert_fusion.1
  146.4 79.6 %reduce-scatter.9.cloned.1.call-done = bf16[336,2048]{1,0:T(8,128)(2,1)} async-done(((bf16[2688,2048]{1,0:T(8,128)(2,1)}), bf16[336,2048]{1,0:T(8,128)(2,1)}) %reduce-scatter.9.cloned.1.call-update) | async-done | bytes 1376272 | tf_op jit(solution)/shard_map/reduce_scatter | solution.py:164
  235.0 99.8 %all-gather.14.cloned.1.call-done = bf16[2,2048,704]{1,2,0:T(8,128)(2,1)} async-done(((bf16[2,512,704]{1,2,0:T(8,128)(2,1)}), bf16[2,2048,704]{1,2,0:T(8,128)(2,1)}) %all-gather.14.cloned.1.call-update) | async-done | bytes 5767184 | tf_op jit(solution)/shard_map/all_gather | solution.py:110
  334.8 66.1 %all-gather.12.cloned.1.call-done = bf16[2688,2048]{1,0:T(8,128)(2,1)} async-done(((bf16[336,2048]{1,0:T(8,128)(2,1)}), bf16[2688,2048]{1,0:T(8,128)(2,1)}) %all-gather.12.cloned.1.call-update) | async-done | bytes 11010064 | tf_op jit(solution)/shard_map/all_gather | solution.py:170
  400.9 22.5 %fusion.8 = f32[2,2688,704]{1,2,0:T(8,128)S(1)} fusion(bf16[2,2048,704]{1,2,0:T(8,128)(2,1)} %all-gather.14.cloned.1.call-done, bf16[2688,2048]{1,0:T(8,128)(2,1)} %all-gather.12.cloned.1.call-done), kind=kOutput, calls=%fused_computation.14 | convolution fusion | flops 15502147584 | bytes 31916032 | tf_op jit(solution)/shard_map/td,jdf->jtf/dot_general | solution.py:171
  432.5 29.5 %all-gather.16.cloned.1.call-done = bf16[704,2048]{1,0:T(8,128)(2,1)} async-done(((bf16[704,512]{1,0:T(8,128)(2,1)}), bf16[704,2048]{1,0:T(8,128)(2,1)}) %all-gather.16.cloned.1.call-update) | async-done | bytes 2883600 | tf_op jit(solution)/shard_map/all_gather | solution.py:111
  462.0 14.0 %convolution_convert_fusion = bf16[2688,2048]{1,0:T(8,128)(2,1)} fusion(bf16[2688,704]{0,1:T(8,128)(2,1)} %multiply_convert_fusion.1, bf16[704,2048]{1,0:T(8,128)(2,1)} %all-gather.16.cloned.1.call-done), kind=kOutput, calls=%fused_computation.2 | convolution fusion | flops 7756578816 | bytes 17678336 | tf_op jit(solution)/shard_map/dot_general | solution.py:176
  477.1 81.9 %reduce-scatter.11.cloned.1.call-done = bf16[336,2048]{1,0:T(8,128)(2,1)} async-done(((bf16[2688,2048]{1,0:T(8,128)(2,1)}), bf16[336,2048]{1,0:T(8,128)(2,1)}) %reduce-scatter.11.cloned.1.call-update) | async-done | bytes 1376272 | tf_op jit(solution)/shard_map/reduce_scatter | solution.py:177
  569.0 65.6 %all-gather.18.cloned.1.call-done = bf16[2688,2048]{1,0:T(8,128)(2,1)} async-done(((bf16[336,2048]{1,0:T(8,128)(2,1)}), bf16[2688,2048]{1,0:T(8,128)(2,1)}) %all-gather.18.cloned.1.call-update) | async-done | bytes 11010064 | tf_op jit(solution)/shard_map/all_gather | solution.py:196
  634.6 21.1 %fusion.30 = (bf16[1,2688,704]{1,2,0:T(8,128)(2,1)S(1)}, bf16[1,2688,704]{1,2,0:T(8,128)(2,1)S(1)}) fusion(f32[2,2688,704]{1,2,0:T(8,128)} %copy-done.19, bf16[2688,2048]{1,0:T(8,128)(2,1)} %all-gather.18.cloned.1.call-done, bf16[704,2048]{1,0:T(8,128)(2,1)} %all-gather.16.cloned.1.call-done), kind=kOutput, calls=%fused_computation.58 | convolution fusion | flops 7796490240 | bytes 36601856 | tf_op jit(solution)/shard_map/td,fd->tf/dot_general | solution.py:200
  658.7 21.0 %bitcast_convert_fusion.1 = bf16[2688,2048]{1,0:T(8,128)(2,1)} fusion(bf16[2,2048,704]{1,2,0:T(8,128)(2,1)} %all-gather.14.cloned.1.call-done, bf16[1,2688,704]{1,2,0:T(8,128)(2,1)S(1)} %get-tuple-element.121, bf16[1,2688,704]{1,2,0:T(8,128)(2,1)S(1)} %get-tuple-element.120), kind=kOutput, calls=%fused_computation.1 | convolution fusion | flops 15511437312 | bytes 24346624 | tf_op jit(solution)/shard_map/jtf,jdf->td/dot_general | solution.py:207
  679.9 84.0 %reduce-scatter.13.cloned.1.call-done = bf16[336,2048]{1,0:T(8,128)(2,1)} async-done(((bf16[2688,2048]{1,0:T(8,128)(2,1)}), bf16[336,2048]{1,0:T(8,128)(2,1)}) %reduce-scatter.13.cloned.1.call-update) | async-done | bytes 1376272 | tf_op jit(solution)/shard_map/reduce_scatter | solution.py:211
  773.7 13.3 %convolution_convert_fusion.3 = bf16[704,2048]{1,0:T(8,128)(2,1)} fusion(bf16[2688,704]{0,1:T(8,128)(2,1)} %multiply_convert_fusion.1, bf16[2688,2048]{1,0:T(8,128)(2,1)} %all-gather.18.cloned.1.call-done), kind=kOutput, calls=%fused_computation.60 | convolution fusion | flops 7752515584 | bytes 17678336 | tf_op jit(solution)/shard_map/tf,td->fd/dot_general | solution.py:197
  793.7 22.3 %convert_bitcast_fusion = bf16[2,2048,704]{1,2,0:T(8,128)(2,1)} fusion(bf16[2688,2048]{1,0:T(8,128)(2,1)} %all-gather.12.cloned.1.call-done, bf16[1,2688,704]{1,2,0:T(8,128)(2,1)} %copy-done.84, bf16[1,2688,704]{1,2,0:T(8,128)(2,1)} %copy-done.83), kind=kOutput, calls=%fused_computation.43 | convolution fusion | flops 15508815872 | bytes 24346624 | tf_op jit(solution)/shard_map/td,jtf->jdf/dot_general | solution.py:204
  816.4 22.9 %all-gather.20.cloned.1.call-done = bf16[2688,2048]{1,0:T(8,128)(2,1)} async-done(((bf16[336,2048]{1,0:T(8,128)(2,1)}), bf16[2688,2048]{1,0:T(8,128)(2,1)}) %all-gather.20.cloned.1.call-update) | async-done | bytes 11010064 | tf_op jit(solution)/shard_map/all_gather | solution.py:219
  958.1 8.9 convolution_convert_fusion.4
  973.5 13.4 %fusion.55 = bf16[3,2048,256]{1,2,0:T(8,128)(2,1)} fusion(bf16[2688,2048]{1,0:T(8,128)(2,1)} %param.21, bf16[1,2688,256]{2,1,0:T(8,128)(2,1)S(1)} %copy-done.53, bf16[1,2688,256]{2,1,0:T(8,128)(2,1)S(1)} %get-tuple-element.129, bf16[1,2688,256]{2,1,0:T(8,128)(2,1)S(1)} %get-tuple-element.128), kind=kOutput, calls=%fused_computation.80 | convolution fusion | flops 8461418496 | bytes 18284544 | tf_op jit(solution)/shard_map/td,jtc->jdc/dot_general | solution.py:270
  988.7 13.4 %bitcast_convert_fusion = bf16[2688,2048]{1,0:T(8,128)(2,1)} fusion(bf16[3,2048,256]{1,2,0:T(8,128)(2,1)} %all-gather.8.cloned.1.call-done, bf16[1,2688,256]{2,1,0:T(8,128)(2,1)S(1)} %copy-done.54, bf16[1,2688,256]{2,1,0:T(8,128)(2,1)} %copy-done.57, bf16[1,2688,256]{2,1,0:T(8,128)(2,1)S(1)} %copy-done.56), kind=kOutput, calls=%fused_computation | convolution fusion | flops 8465350656 | bytes 18284544 | tf_op jit(solution)/shard_map/jtc,jdc->td/dot_general | solution.py:273
  1019.8 41.7 %psum.7 = f32[4,2048]{1,0:T(4,128)S(1)} all-reduce(f32[4,2048]{1,0:T(4,128)S(1)} %pad_maximum_fusion.14), channel_id=1, replica_groups=mesh['dp'=4,'mp'=8] {'dp','mp'}, use_global_device_ids=true, to_apply=%region_31.32 | all-reduce | flops 8192 | bytes 65536 | tf_op jit(solution)/shard_map/psum | solution.py:284
  1065.2 29.5 %reduce-scatter.17.cloned.1.call-done = bf16[3,512,256]{1,2,0:T(8,128)(2,1)} async-done(((bf16[3,2048,256]{1,2,0:T(8,128)(2,1)}), bf16[3,512,256]{1,2,0:T(8,128)(2,1)}) %reduce-scatter.17.cloned.1.call-update) | async-done | bytes 786448 | tf_op jit(solution)/shard_map/reduce_scatter | solution.py:286
  1108.9 73.9 %reduce-scatter.15.cloned.1.call-done = bf16[336,2048]{1,0:T(8,128)(2,1)} async-done(((bf16[2688,2048]{1,0:T(8,128)(2,1)}), bf16[336,2048]{1,0:T(8,128)(2,1)}) %reduce-scatter.15.cloned.1.call-update) | async-done | bytes 1376272 | tf_op jit(solution)/shard_map/reduce_scatter | solution.py:277
  (339 shorter events, 265.2 us)
Async XLA Ops:
  7.2 69.5 %all-gather.8.cloned.1.call-start = ((), (), s32[]{:S(2)}) async-start(), calls=%async_computation.8 | async-start | bytes 3932160 | tf_op jit(solution)/shard_map/all_gather | solution.py:108
  10.3 124.0 %all-gather.10.cloned.1.call-start = ((), (), s32[]{:S(2)}) async-start(), calls=%async_computation.9 | async-start | bytes 1310720 | tf_op jit(solution)/shard_map/all_gather | solution.py:109
  11.2 214.9 %reduce-scatter.9.cloned.1.call-start = ((), (), s32[]{:S(2)}) async-start(), calls=%async_computation.10 | async-start | bytes 12386304 | tf_op jit(solution)/shard_map/reduce_scatter | solution.py:164
  16.4 115.0 %copy-start.11 = (pred[896,896]{0,1:T(8,128)(4,1)}, pred[896,896]{0,1:T(8,128)(4,1)S(1)}, u32[]{:S(2)}) copy-start(pred[896,896]{0,1:T(8,128)(4,1)S(1)} %fusion.48) | copy-start | bytes 2408452
  143.2 191.6 %all-gather.14.cloned.1.call-start = ((), (), s32[]{:S(2)}) async-start(), calls=%async_computation.12 | async-start | bytes 7208960 | tf_op jit(solution)/shard_map/all_gather | solution.py:110
  146.3 254.6 %all-gather.12.cloned.1.call-start = ((), (), s32[]{:S(2)}) async-start(), calls=%async_computation.11 | async-start | bytes 12386304 | tf_op jit(solution)/shard_map/all_gather | solution.py:170
  233.9 228.1 %all-gather.16.cloned.1.call-start = ((), (), s32[]{:S(2)}) async-start(), calls=%async_computation.13 | async-start | bytes 3604480 | tf_op jit(solution)/shard_map/all_gather | solution.py:111
  234.9 324.1 %reduce-scatter.11.cloned.1.call-start = ((), (), s32[]{:S(2)}) async-start(), calls=%async_computation.14 | async-start | bytes 12386304 | tf_op jit(solution)/shard_map/reduce_scatter | solution.py:177
  476.1 158.5 %all-gather.18.cloned.1.call-start = ((), (), s32[]{:S(2)}) async-start(), calls=%async_computation.15 | async-start | bytes 12386304 | tf_op jit(solution)/shard_map/all_gather | solution.py:196
  568.9 194.9 %reduce-scatter.13.cloned.1.call-start = ((), (), s32[]{:S(2)}) async-start(), calls=%async_computation.16 | async-start | bytes 12386304 | tf_op jit(solution)/shard_map/reduce_scatter | solution.py:211
  679.7 159.6 %all-gather.20.cloned.1.call-start = ((), (), s32[]{:S(2)}) async-start(), calls=%async_computation.17 | async-start | bytes 12386304 | tf_op jit(solution)/shard_map/all_gather | solution.py:219
  773.6 233.2 %reduce-scatter.23.cloned.1.call-start = ((), (), s32[]{:S(2)}) async-start(), calls=%async_computation.22 | async-start | bytes 3604480 | tf_op jit(solution)/shard_map/reduce_scatter | solution.py:295
  787.1 225.4 %reduce-scatter.21.cloned.1.call-start = ((), (), s32[]{:S(2)}) async-start(), calls=%async_computation.21 | async-start | bytes 7208960 | tf_op jit(solution)/shard_map/reduce_scatter | solution.py:292
  816.1 23.2 %copy-start.58 = (bf16[256,2048]{1,0:T(8,128)(2,1)S(1)}, bf16[256,2048]{1,0:T(8,128)(2,1)}, u32[]{:S(2)}) copy-start(bf16[256,2048]{1,0:T(8,128)(2,1)} %all-gather.10.cloned.1.call-done) | copy-start | bytes 3145732
  816.1 246.1 %reduce-scatter.19.cloned.1.call-start = ((), (), s32[]{:S(2)}) async-start(), calls=%async_computation.20 | async-start | bytes 1310720 | tf_op jit(solution)/shard_map/reduce_scatter | solution.py:289
  967.0 127.6 %reduce-scatter.17.cloned.1.call-start = ((), (), s32[]{:S(2)}) async-start(), calls=%async_computation.19 | async-start | bytes 3932160 | tf_op jit(solution)/shard_map/reduce_scatter | solution.py:286
  986.9 195.9 %reduce-scatter.15.cloned.1.call-start = ((), (), s32[]{:S(2)}) async-start(), calls=%async_computation.18 | async-start | bytes 12386304 | tf_op jit(solution)/shard_map/reduce_scatter | solution.py:277
  1012.4 49.1 %copy-start.60 = (f32[4,2048]{1,0:T(4,128)S(1)}, f32[4,2048]{1,0:T(4,128)}, u32[]{:S(2)}) copy-start(f32[4,2048]{1,0:T(4,128)} %param.39) | copy-start | bytes 98308
  1012.4 49.1 %copy-start.70 = (f32[4,2048]{1,0:T(4,128)S(1)}, f32[4,2048]{1,0:T(4,128)}, u32[]{:S(2)}) copy-start(f32[4,2048]{1,0:T(4,128)} %param.41) | copy-start | bytes 98308
  1012.4 49.1 %copy-start.71 = (f32[4,2048]{1,0:T(4,128)S(1)}, f32[4,2048]{1,0:T(4,128)}, u32[]{:S(2)}) copy-start(f32[4,2048]{1,0:T(4,128)} %param.40) | copy-start | bytes 98308
  1019.7 75.0 %copy-start.21 = (f32[3,512,256]{1,2,0:T(8,128)S(1)}, f32[3,512,256]{1,2,0:T(8,128)}, u32[]{:S(2)}) copy-start(f32[3,512,256]{1,2,0:T(8,128)} %copy-done.20) | copy-start | bytes 4718596
  1019.7 75.0 %copy-start.32 = (f32[3,512,256]{1,2,0:T(8,128)S(1)}, f32[3,512,256]{1,2,0:T(8,128)}, u32[]{:S(2)}) copy-start(f32[3,512,256]{1,2,0:T(8,128)} %copy.218) | copy-start | bytes 4718596
  1061.6 37.8 %copy-start.61 = (f32[4,2048]{1,0:T(4,128)}, f32[4,2048]{1,0:T(4,128)S(1)}, u32[]{:S(2)}) copy-start(f32[4,2048]{1,0:T(4,128)S(1)} %psum.7) | copy-start | bytes 98308
  1104.1 78.7 %copy-start.29 = (f32[336,2048]{1,0:T(8,128)S(1)}, f32[336,2048]{1,0:T(8,128)}, u32[]{:S(2)}) copy-start(f32[336,2048]{1,0:T(8,128)} %get-tuple-element.115) | copy-start | bytes 8257540
  (84 other events, 373.9 us)
Sparse Core Ops, SparseCore 0:
  10.5 66.1 all-gather.7
  78.8 26.6 all-gather.9
  143.3 82.6 reduce-scatter.8
  228.1 106.6 all-gather.13
  337.1 63.7 all-gather.11
  402.9 59.1 all-gather.15
  476.2 82.7 reduce-scatter.10
  569.1 65.4 all-gather.17
  679.8 84.0 reduce-scatter.12
  773.8 65.4 all-gather.19
  842.1 56.1 reduce-scatter.22
  900.5 102.0 reduce-scatter.20
  1005.5 27.6 reduce-scatter.18
  1035.5 59.1 reduce-scatter.16
  1098.5 84.2 reduce-scatter.14
where the time goes:
time: 1200 us; the launch traced here: 1190 us
  waiting for transfers between devices  686 us (57%)
  matrix products  241 us (20%)
  other arithmetic  109 us (9%)
  local copies, waits for them, and re-layouts  97.4 us (8%)
  blocking collectives  41.7 us (3%)
  between operations  16.6 us (1%)
    all_gather x1, waiting for transfers between devices, body(): lax.all_gather(master_gateup.astype(jnp.bfloat16), 'dp', axis=1, tiled=True)  99.8 us
    reduce_scatter x1, waiting for transfers between devices, body(): lax.psum_scatter(middle_grad_part.astype(jnp.bfloat16), 'mp', scatter_dim...  84 us
    reduce_scatter x1, waiting for transfers between devices, body(): lax.psum_scatter(ffn_part.astype(jnp.bfloat16), 'mp', scatter_dimension=0...  81.9 us
    reduce_scatter x1, waiting for transfers between devices, body(): lax.psum_scatter(attn_part.astype(jnp.bfloat16), 'mp', scatter_dimension=...  79.6 us
    reduce_scatter x1, waiting for transfers between devices, body(): lax.psum_scatter(input_grad_part.astype(jnp.bfloat16), 'mp', scatter_dime...  73.9 us
    all_gather x1, waiting for transfers between devices, body(): lax.all_gather(middle_share.astype(jnp.bfloat16), 'mp', axis=0, tiled=True)  66.1 us
    all_gather x1, waiting for transfers between devices, body(): lax.all_gather(grad_h2.astype(jnp.bfloat16), 'mp', axis=0, tiled=True)  65.6 us
    all_gather x1, waiting for transfers between devices, body(): lax.all_gather(master_qkv.astype(jnp.bfloat16), 'dp', axis=1, tiled=True)  53.1 us
  transfers between devices with their start and end apart: 15, of which 11 were waited for; matrix products, arithmetic and copies ran while one was open for 28% of the time, Pallas kernels for 0%

commit v1 on v0

--- a/solution.py
+++ b/solution.py
@@ -1,8 +1,11 @@
+import functools
 import math
 
 import jax
 import jax.numpy as jnp
 from jax import lax
+from jax.experimental import pallas as pl
+from jax.experimental.pallas import tpu as pltpu
 from jax.sharding import PartitionSpec as P
 
 D = 2048
@@ -81,7 +84,7 @@
     return (old_master - learn_rate * update, first_new, second_new)
 
 
-def body(
+def body_plain(
     block_input,
     cotangent,
     prefix_len,
@@ -343,6 +346,867 @@
     )
 
 
+MESH = pl.DeviceIdType.MESH
+VMEM_BYTES = 61 * 1024 * 1024
+BF16 = jnp.bfloat16
+F32 = jnp.float32
+NT = (((1,), (1,)), ((), ()))
+ANY = pl.BlockSpec(memory_space=pl.ANY)
+VM = pl.BlockSpec(memory_space=pltpu.VMEM)
+PLUS = [(0, 1), (1, 2), (2, 3), (3, 0)]
+MINUS = [(1, 0), (2, 1), (3, 2), (0, 3)]
+
+
+def nt_dot(left, right):
+    return lax.dot_general(left, right, NT, preferred_element_type=F32)
+
+
+def ring_gather(first, second):
+    left = (lax.ppermute(first, "dp", PLUS), lax.ppermute(second, "dp", PLUS))
+    right = (lax.ppermute(first, "dp", MINUS), lax.ppermute(second, "dp", MINUS))
+    far = (lax.ppermute(left[0], "dp", PLUS), lax.ppermute(right[1], "dp", MINUS))
+    return (first, second) + left + right + far
+
+
+def ring_scatter(shard_of):
+    here = lax.axis_index("dp")
+    far = shard_of((here + 2) % 4)
+    nxt = shard_of((here + 1) % 4)
+    prv = shard_of((here + 3) % 4)
+    own = shard_of(here)
+    plus_far = lax.ppermute(far[0], "dp", PLUS)
+    minus_far = lax.ppermute(far[1], "dp", MINUS)
+    plus_b = lax.ppermute(nxt[1], "dp", PLUS)
+    minus_a = lax.ppermute(prv[0], "dp", MINUS)
+    plus_a = lax.ppermute((nxt[0].astype(F32) + plus_far.astype(F32)).astype(BF16), "dp", PLUS)
+    minus_b = lax.ppermute((prv[1].astype(F32) + minus_far.astype(F32)).astype(BF16), "dp", MINUS)
+    return (
+        own[0].astype(F32) + plus_a.astype(F32) + minus_a.astype(F32),
+        own[1].astype(F32) + plus_b.astype(F32) + minus_b.astype(F32),
+    )
+
+
+class Square:
+    def __init__(self, send, recv, rows):
+        me = lax.axis_index("mp")
+        self.core = me % 2
+        self.x = (me // 2) % 2
+        self.y = me // 4
+        self.xn = (self.y * 2 + (1 - self.x)) * 2 + self.core
+        self.yn = ((1 - self.y) * 2 + self.x) * 2 + self.core
+        self.peer = (self.y * 2 + self.x) * 2 + (1 - self.core)
+        self.own = self.y * 2 + self.x
+        self.xc = self.y * 2 + (1 - self.x)
+        self.yc = (1 - self.y) * 2 + self.x
+        self.dc = (1 - self.y) * 2 + (1 - self.x)
+        self.send, self.recv = send, recv
+        cut = rows // 2 // 16 * 16
+        self.rows = rows
+        self.a = pl.ds(0, cut)
+        self.b = pl.ds(cut, rows - cut)
+        self.na, self.nb, self.cut = cut, rows - cut, cut
+
+    def barrier(self):
+        sem = pltpu.get_barrier_semaphore()
+        for other in (self.xn, self.yn, self.peer):
+            pl.semaphore_signal(sem, inc=1, device_id={"mp": other}, device_id_type=MESH)
+        pl.semaphore_wait(sem, 3)
+
+    def copy(self, k, src, dst, other):
+        return pltpu.make_async_remote_copy(
+            src_ref=src,
+            dst_ref=dst,
+            send_sem=self.send.at[k],
+            recv_sem=self.recv.at[k],
+            device_id={"mp": other},
+            device_id_type=MESH,
+        )
+
+
+def add_rows(dst, src, count):
+    def step(i, carry):
+        rows = pl.ds(pl.multiple_of(i * 16, 16), 16)
+        dst[rows, :] = (dst[rows, :].astype(F32) + src[rows, :].astype(F32)).astype(BF16)
+        return carry
+
+    lax.fori_loop(0, count // 16, step, 0)
+
+
+def square_kernel(rows, gather, scatter, compute, share, full, gbuf, pbuf, bufs, out, send, recv, lsem):
+    sq = Square(send, recv, rows)
+    core = sq.core
+    sq.barrier()
+    if gather:
+        c_own = sq.copy(0, share, gbuf.at[sq.own, core], sq.peer)
+        x_a = sq.copy(1, share.at[sq.a], gbuf.at[sq.own, core, sq.a], sq.xn)
+        y_b = sq.copy(2, share.at[sq.b], gbuf.at[sq.own, core, sq.b], sq.yn)
+        f_x = sq.copy(3, gbuf.at[sq.yc, core, sq.b], gbuf.at[sq.yc, core, sq.b], sq.xn)
+        f_y = sq.copy(4, gbuf.at[sq.xc, core, sq.a], gbuf.at[sq.xc, core, sq.a], sq.yn)
+        x_b = sq.copy(5, share.at[sq.b], gbuf.at[sq.own, core, sq.b], sq.xn)
+        y_a = sq.copy(6, share.at[sq.a], gbuf.at[sq.own, core, sq.a], sq.yn)
+        c_d = sq.copy(7, gbuf.at[sq.dc, core], gbuf.at[sq.dc, core], sq.peer)
+        c_x = sq.copy(8, gbuf.at[sq.xc, core], gbuf.at[sq.xc, core], sq.peer)
+        c_y = sq.copy(9, gbuf.at[sq.yc, core], gbuf.at[sq.yc, core], sq.peer)
+        local = pltpu.make_async_copy(share, gbuf.at[sq.own, core], lsem.at[8])
+        x_a.start()
+        y_b.start()
+        c_own.start()
+        local.start()
+    if scatter:
+        rcore, rxd, ryd, rx, ry = bufs
+        x_d = sq.copy(14, pbuf.at[sq.dc, core, sq.a], rxd, sq.xn)
+        y_d = sq.copy(15, pbuf.at[sq.dc, core, sq.b], ryd, sq.yn)
+        x_ra = sq.copy(16, pbuf.at[sq.xc, core, sq.a], rx.at[sq.a], sq.xn)
+        y_rb = sq.copy(17, pbuf.at[sq.yc, core, sq.b], ry.at[sq.b], sq.yn)
+        x_rb = sq.copy(18, pbuf.at[sq.xc, core, sq.b], rx.at[sq.b], sq.xn)
+        y_ra = sq.copy(19, pbuf.at[sq.yc, core, sq.a], ry.at[sq.a], sq.yn)
+
+    def step(t, carry):
+        unit = t // 2
+        turn = t % 2
+        rel = unit if gather else (unit + 1) % 4
+        chip_y = (sq.y + rel % 2) % 2
+        chip_x = (sq.x + ((rel + 1) // 2) % 2) % 2
+        chip = chip_y * 2 + chip_x
+        which = (1 - core + turn) % 2
+        if gather:
+
+            @pl.when(t == 0)
+            def _():
+                c_own.wait_recv()
+                local.wait()
+
+            @pl.when(t == 2)
+            def _():
+                x_a.wait_recv()
+                y_b.wait_recv()
+                f_x.start()
+                f_y.start()
+                x_b.start()
+                y_a.start()
+                f_x.wait_recv()
+                f_y.wait_recv()
+                c_d.start()
+                c_d.wait_recv()
+
+            @pl.when(t == 4)
+            def _():
+                x_b.wait_recv()
+                y_a.wait_recv()
+                c_x.start()
+                c_y.start()
+                c_x.wait_recv()
+                c_y.wait_recv()
+
+            if full is not None:
+                pltpu.make_async_copy(gbuf.at[chip, which], full.at[chip, which], lsem.at[t]).start()
+        compute(t, chip, which)
+        if scatter:
+
+            @pl.when(turn == 0)
+            def _():
+                sq.copy(10 + rel, pbuf.at[chip, which], rcore.at[chip], sq.peer).start()
+
+            @pl.when(turn == 1)
+            def _():
+                sq.copy(10 + rel, pbuf.at[chip, which], rcore.at[chip], sq.peer).wait_recv()
+                add_rows(pbuf.at[chip, which], rcore.at[chip], rows)
+
+            @pl.when((turn == 1) & (rel == 1))
+            def _():
+                x_d.start()
+                y_d.start()
+
+            @pl.when((turn == 1) & (rel == 2))
+            def _():
+                x_ra.start()
+
+            @pl.when((turn == 1) & (rel == 3))
+            def _():
+                y_rb.start()
+
+        return carry
+
+    lax.fori_loop(0, 8, step, 0)
+    if scatter:
+        x_d.wait_recv()
+        add_rows(pbuf.at[sq.yc, core, sq.a], rxd, sq.na)
+        y_ra.start()
+        y_d.wait_recv()
+        add_rows(pbuf.at[sq.xc, core, sq.b], ryd, sq.nb)
+        x_rb.start()
+        x_ra.wait_recv()
+        y_rb.wait_recv()
+        y_ra.wait_recv()
+        x_rb.wait_recv()
+
+        def last(i, carry):
+            part = pl.ds(pl.multiple_of(i * 16, 16), 16)
+            out[part, :] = (
+                pbuf[sq.own, core, part, :].astype(F32)
+                + rx[part, :].astype(F32)
+                + ry[part, :].astype(F32)
+            )
+            return carry
+
+        lax.fori_loop(0, rows // 16, last, 0)
+        for k in range(4):
+            sq.copy(10 + k, pbuf.at[0, 0], rcore.at[0], sq.peer).wait_send()
+        for copy in (x_d, y_d, x_ra, y_rb, x_rb, y_ra):
+            copy.wait_send()
+    if gather:
+        for copy in (c_own, x_a, y_b, f_x, f_y, x_b, y_a, c_d, c_x, c_y):
+            copy.wait_send()
+        if full is not None:
+            for t in range(8):
+                pltpu.make_async_copy(gbuf.at[0, 0], full.at[0, 0], lsem.at[t]).wait()
+
+
+def scatter_scratch(rows, width):
+    cut = rows // 2 // 16 * 16
+    return [
+        pltpu.VMEM((4, 2, rows, width), BF16),
+        pltpu.VMEM((4, rows, width), BF16),
+        pltpu.VMEM((cut, width), BF16),
+        pltpu.VMEM((rows - cut, width), BF16),
+        pltpu.VMEM((rows, width), BF16),
+        pltpu.VMEM((rows, width), BF16),
+    ]
+
+
+SEMS = [
+    pltpu.SemaphoreType.DMA((20,)),
+    pltpu.SemaphoreType.DMA((20,)),
+    pltpu.SemaphoreType.DMA((9,)),
+]
+
+
+def params(collective_id):
+    return pltpu.CompilerParams(
+        collective_id=collective_id, has_side_effects=True, vmem_limit_bytes=VMEM_BYTES
+    )
+
+
+def weight_copies(pieces, place, sem):
+    here = lax.axis_index("dp")
+    owners = (here, (here + 3) % 4, (here + 1) % 4, (here + 2) % 4)
+    copies = []
+    for k, piece in enumerate(pieces):
+        copies.append(pltpu.make_async_copy(piece, place(owners[k // 2], k % 2), sem.at[k]))
+    return copies
+
+
+def row_place(buf, depth):
+    half = depth // 2
+
+    def place(owner, part):
+        return buf.at[:, pl.ds(pl.multiple_of(owner * depth + part * half, half), half), :]
+
+    return place
+
+
+def plane_place(buf, depth):
+    def place(owner, part):
+        return buf.at[part, pl.ds(pl.multiple_of(owner * depth, depth), depth), :]
+
+    return place
+
+
+def column_place(buf, depth):
+    half = buf.shape[0] // 2
+
+    def place(owner, part):
+        return buf.at[pl.ds(part * half, half), pl.ds(pl.multiple_of(owner * depth, depth), depth)]
+
+    return place
+
+
+def qkv_call(block_input, pieces, cos_table, sin_table):
+    tokens, width = block_input.shape
+    cols = pieces[0].shape[2]
+    depth = pieces[0].shape[1] * 2
+    rows = 336
+    heads = cols // HEAD_DIM
+    scale = 1.0 / math.sqrt(HEAD_DIM)
+
+    def kernel(x_ref, cos_ref, sin_ref, *rest):
+        piece_refs, (q_ref, k_ref, v_ref, w_buf, sem) = rest[:8], rest[8:]
+
+        @pl.when(pl.program_id(0) == 0)
+        def _():
+            copies = weight_copies(piece_refs, row_place(w_buf, depth), sem)
+            for copy in copies:
+                copy.start()
+            for copy in copies:
+                copy.wait()
+
+        x = x_ref[...]
+        for j, ref in enumerate((q_ref, k_ref)):
+            a = jnp.dot(x, w_buf[j], preferred_element_type=F32)
+            for h in range(heads):
+                part = a[:, h * HEAD_DIM : (h + 1) * HEAD_DIM]
+                turned = part * cos_ref[...] + pltpu.roll(part, HEAD_DIM // 2, 1) * sin_ref[...]
+                if j == 0:
+                    turned = turned * scale
+                ref[:, h * HEAD_DIM : (h + 1) * HEAD_DIM] = turned.astype(BF16)
+        v_ref[...] = jnp.dot(x, w_buf[2], preferred_element_type=F32).astype(BF16)
+
+    tile = lambda n: pl.BlockSpec((rows, n), lambda i: (i, 0))
+    return pl.pallas_call(
+        kernel,
+        grid=(tokens // rows,),
+        out_shape=[jax.ShapeDtypeStruct((tokens, cols), BF16)] * 3,
+        in_specs=[tile(width), tile(HEAD_DIM), tile(HEAD_DIM)] + [ANY] * 8,
+        out_specs=[tile(cols)] * 3,
+        scratch_shapes=[pltpu.VMEM((3, width, cols), BF16), pltpu.SemaphoreType.DMA((8,))],
+        compiler_params=pltpu.CompilerParams(vmem_limit_bytes=VMEM_BYTES),
+        cost_estimate=pl.CostEstimate(
+            flops=6 * tokens * width * cols, bytes_accessed=20 << 20, transcendentals=0
+        ),
+        name="qkv",
+    )(block_input, cos_table, sin_table, *pieces)
+
+
+BLOCK = 128
+
+
+def attention_call(queries, key_rows, value_rows, prefix_len):
+    tokens, cols = queries.shape
+    proteins = tokens // LEN
+    heads = cols // HEAD_DIM
+
+    def kernel(pre_ref, q_ref, k_ref, v_ref, o_ref, p_ref):
+        prefix = pre_ref[pl.program_id(0)]
+
+        def step(i, carry):
+            rows = pl.ds(pl.multiple_of(i * BLOCK, BLOCK), BLOCK)
+            s = nt_dot(q_ref[rows, :], k_ref[...])
+            col = lax.broadcasted_iota(jnp.int32, s.shape, 1)
+            row = lax.broadcasted_iota(jnp.int32, s.shape, 0) + i * BLOCK
+            s = jnp.where(col < jnp.maximum(prefix, row + 1), s, -1e30)
+            e = jnp.exp(s - jnp.max(s, axis=-1, keepdims=True))
+            p = (e / jnp.sum(e, axis=-1, keepdims=True)).astype(BF16)
+            p_ref[0, 0, rows, :] = p
+            o_ref[rows, :] = jnp.dot(p, v_ref[...], preferred_element_type=F32).astype(BF16)
+            return carry
+
+        lax.fori_loop(0, LEN // BLOCK, step, 0)
+
+    tile = pl.BlockSpec((LEN, HEAD_DIM), lambda p, h, *_: (p, h))
+    return pl.pallas_call(
+        kernel,
+        grid_spec=pltpu.PrefetchScalarGridSpec(
+            num_scalar_prefetch=1,
+            grid=(proteins, heads),
+            in_specs=[tile] * 3,
+            out_specs=[tile, pl.BlockSpec((1, 1, LEN, LEN), lambda p, h, *_: (p, h, 0, 0))],
+        ),
+        out_shape=[
+            jax.ShapeDtypeStruct((tokens, cols), BF16),
+            jax.ShapeDtypeStruct((proteins, heads, LEN, LEN), BF16),
+        ],
+        compiler_params=pltpu.CompilerParams(vmem_limit_bytes=VMEM_BYTES),
+        cost_estimate=pl.CostEstimate(
+            flops=4 * tokens * LEN * cols, bytes_accessed=16 << 20, transcendentals=tokens * LEN * heads
+        ),
+        name="attention",
+    )(prefix_len, queries, key_rows, value_rows)
+
+
+def attention_back_call(queries, key_rows, value_rows, probs, attended, grad_attended, cos_table, sin_table):
+    tokens, cols = queries.shape
+    proteins = tokens // LEN
+    heads = cols // HEAD_DIM
+    scale = 1.0 / math.sqrt(HEAD_DIM)
+    TN = (((0,), (0,)), ((), ()))
+
+    def kernel(q_ref, k_ref, v_ref, p_ref, o_ref, do_ref, cos_ref, sin_ref, da_ref, dk_acc, dv_acc):
+        dk_acc[...] = jnp.zeros_like(dk_acc)
+        dv_acc[...] = jnp.zeros_like(dv_acc)
+
+        def step(i, carry):
+            rows = pl.ds(pl.multiple_of(i * BLOCK, BLOCK), BLOCK)
+            do = do_ref[rows, :]
+            p = p_ref[0, 0, rows, :]
+            delta = jnp.sum(do.astype(F32) * o_ref[rows, :].astype(F32), axis=-1, keepdims=True)
+            dp = nt_dot(do, v_ref[...])
+            ds = (p.astype(F32) * (dp - delta)).astype(BF16)
+            dv_acc[...] += lax.dot_general(p, do, TN, preferred_element_type=F32)
+            dk_acc[...] += lax.dot_general(ds, q_ref[rows, :], TN, preferred_element_type=F32)
+            dq = jnp.dot(ds, k_ref[...], preferred_element_type=F32)
+            turned = dq * cos_ref[rows, :] - pltpu.roll(dq, HEAD_DIM // 2, 1) * sin_ref[rows, :]
+            da_ref[0, rows, :] = (turned * scale).astype(BF16)
+            return carry
+
+        lax.fori_loop(0, LEN // BLOCK, step, 0)
+        dk = dk_acc[...]
+        turned = dk * cos_ref[...] - pltpu.roll(dk, HEAD_DIM // 2, 1) * sin_ref[...]
+        da_ref[1] = turned.astype(BF16)
+        da_ref[2] = dv_acc[...].astype(BF16)
+
+    tile = pl.BlockSpec((LEN, HEAD_DIM), lambda p, h: (p, h))
+    table = pl.BlockSpec((LEN, HEAD_DIM), lambda p, h: (p, 0))
+    return pl.pallas_call(
+        kernel,
+        grid=(proteins, heads),
+        in_specs=[tile] * 3
+        + [pl.BlockSpec((1, 1, LEN, LEN), lambda p, h: (p, h, 0, 0)), tile, tile, table, table],
+        out_specs=pl.BlockSpec((3, LEN, HEAD_DIM), lambda p, h: (0, p, h)),
+        out_shape=jax.ShapeDtypeStruct((3, tokens, cols), BF16),
+        scratch_shapes=[pltpu.VMEM((LEN, HEAD_DIM), F32), pltpu.VMEM((LEN, HEAD_DIM), F32)],
+        compiler_params=pltpu.CompilerParams(vmem_limit_bytes=VMEM_BYTES),
+        cost_estimate=pl.CostEstimate(
+            flops=8 * tokens * LEN * cols, bytes_accessed=20 << 20, transcendentals=0
+        ),
+        name="attention_back",
+    )(queries, key_rows, value_rows, probs, attended, grad_attended, cos_table, sin_table)
+
+
+def out_call(attended, pieces, rows):
+    cols = attended.shape[1]
+    depth = pieces[0].shape[1]
+
+    def kernel(o_ref, *rest):
+        piece_refs, (out, w_buf, pbuf, rcore, rxd, ryd, rx, ry, wsem, send, recv, lsem) = rest[:8], rest[8:]
+        copies = weight_copies(piece_refs, column_place(w_buf, depth), wsem)
+        for copy in copies:
+            copy.start()
+        for copy in copies:
+            copy.wait()
+
+        def compute(t, chip, which):
+            part = jnp.dot(o_ref[chip, which], w_buf[...], preferred_element_type=F32)
+            pbuf[chip, which] = part.astype(BF16)
+
+        square_kernel(
+            rows, False, True, compute, None, None, None, pbuf, (rcore, rxd, ryd, rx, ry), out, send, recv, lsem
+        )
+
+    return pl.pallas_call(
+        kernel,
+        out_shape=jax.ShapeDtypeStruct((rows, D), F32),
+        in_specs=[VM] + [ANY] * 8,
+        out_specs=VM,
+        scratch_shapes=[pltpu.VMEM((cols, D), BF16)]
+        + scatter_scratch(rows, D)
+        + [pltpu.SemaphoreType.DMA((8,))]
+        + SEMS,
+        compiler_params=params(0),
+        cost_estimate=pl.CostEstimate(flops=40 << 30, bytes_accessed=100 << 20, transcendentals=0),
+        name="out_reduce",
+    )(attended.reshape(4, 2, rows, cols), *pieces)
+
+
+def ffn_call(middle_low, gateup_pieces, down_pieces):
+    rows = middle_low.shape[0]
+    live = gateup_pieces[0].shape[-1]
+    depth = gateup_pieces[0].shape[0]
+    curve = math.sqrt(2.0 / math.pi)
+
+    def kernel(share, *rest):
+        g_refs, d_refs = rest[:8], rest[8:16]
+        (out, full, hid_ref, act_ref, pull_ref) = rest[16:21]
+        (w_g, w_d, gbuf, stage, pbuf, rcore, rxd, ryd, rx, ry, gsem, dsem, osem, send, recv, lsem) = rest[21:]
+        copies = weight_copies(g_refs, plane_place(w_g, depth), gsem)
+        copies += weight_copies(d_refs, column_place(w_d, depth), dsem)
+        for copy in copies:
+            copy.start()
+        outs = (hid_ref, act_ref, pull_ref)
+
+        def compute(t, chip, which):
+            slot = t % 2
+
+            @pl.when(t == 0)
+            def _():
+                for copy in copies:
+                    copy.wait()
+
+            @pl.when(t >= 2)
+            def _():
+                for k, ref in enumerate(outs):
+                    pltpu.make_async_copy(stage.at[slot, k], ref.at[chip, which], osem.at[slot, k]).wait()
+
+            tile = gbuf[chip, which]
+            gate = jnp.dot(tile, w_g[0], preferred_element_type=F32)
+            up = jnp.dot(tile, w_g[1], preferred_element_type=F32)
+            square = gate * gate
+            bent = jnp.tanh(curve * gate * (1.0 + 0.044715 * square))
+            half = 0.5 * (1.0 + bent)
+            act = gate * half
+            slope = half + 0.5 * curve * gate * (1.0 - bent * bent) * (1.0 + 3.0 * 0.044715 * square)
+            hid = (act * up).astype(BF16)
+            stage[slot, 0] = hid
+            stage[slot, 1] = act.astype(BF16)
+            stage[slot, 2] = (slope * up).astype(BF16)
+            for k, ref in enumerate(outs):
+                pltpu.make_async_copy(stage.at[slot, k], ref.at[chip, which], osem.at[slot, k]).start()
+            pbuf[chip, which] = jnp.dot(hid, w_d[...], preferred_element_type=F32).astype(BF16)
+
+        square_kernel(
+            rows, True, True, compute, share, full, gbuf, pbuf, (rcore, rxd, ryd, rx, ry), out, send, recv, lsem
+        )
+        for slot in range(2):
+            for k, ref in enumerate(outs):
+                pltpu.make_async_copy(stage.at[slot, k], ref.at[0, 0], osem.at[slot, k]).wait()
+
+    kept = jax.ShapeDtypeStruct((4, 2, rows, live), BF16)
+    return pl.pallas_call(
+        kernel,
+        out_shape=[
+            jax.ShapeDtypeStruct((rows, D), F32),
+            jax.ShapeDtypeStruct((4, 2, rows, D), BF16),
+            kept,
+            kept,
+            kept,
+        ],
+        in_specs=[ANY] * 17,
+        out_specs=[VM, ANY, ANY, ANY, ANY],
+        scratch_shapes=[
+            pltpu.VMEM((2, D, live), BF16),
+            pltpu.VMEM((live, D), BF16),
+            pltpu.VMEM((4, 2, rows, D), BF16),
+            pltpu.VMEM((2, 3, rows, live), BF16),
+        ]
+        + scatter_scratch(rows, D)
+        + [pltpu.SemaphoreType.DMA((8,)), pltpu.SemaphoreType.DMA((8,)), pltpu.SemaphoreType.DMA((2, 3))]
+        + SEMS,
+        compiler_params=params(1),
+        cost_estimate=pl.CostEstimate(flops=100 << 30, bytes_accessed=300 << 20, transcendentals=0),
+        name="ffn",
+    )(middle_low, *gateup_pieces, *down_pieces)
+
+
+def ffn_back_call(ffn_grad, act, pull, gateup_pieces, down_pieces):
+    rows = ffn_grad.shape[0]
+    live = gateup_pieces[0].shape[-1]
+    depth = gateup_pieces[0].shape[0]
+
+    def kernel(share, act_ref, pull_ref, *rest):
+        g_refs, d_refs = rest[:8], rest[8:16]
+        (out, full, dg_ref) = rest[16:19]
+        (w_g, w_d, gbuf, load, stage, pbuf, rcore, rxd, ryd, rx, ry, gsem, dsem, isem, osem, send, recv, lsem) = rest[
+            19:
+        ]
+        copies = weight_copies(g_refs, plane_place(w_g, depth), gsem)
+        copies += weight_copies(d_refs, column_place(w_d, depth), dsem)
+        for copy in copies:
+            copy.start()
+
+        def compute(t, chip, which):
+            slot = t % 2
+
+            @pl.when(t == 0)
+            def _():
+                for copy in copies:
+                    copy.wait()
+
+            loads = [
+                pltpu.make_async_copy(ref.at[chip, which], load.at[k], isem.at[k])
+                for k, ref in enumerate((act_ref, pull_ref))
+            ]
+            stores = [
+                pltpu.make_async_copy(stage.at[slot, k], dg_ref.at[k, chip, which], osem.at[slot, k])
+                for k in range(2)
+            ]
+            for copy in loads:
+                copy.start()
+
+            @pl.when(t >= 2)
+            def _():
+                for copy in stores:
+                    copy.wait()
+
+            dh = nt_dot(gbuf[chip, which], w_d[...])
+            for copy in loads:
+                copy.wait()
+            d_gate = (dh * load[1].astype(F32)).astype(BF16)
+            d_up = (dh * load[0].astype(F32)).astype(BF16)
+            stage[slot, 0] = d_gate
+            stage[slot, 1] = d_up
+            for copy in stores:
+                copy.start()
+            pbuf[chip, which] = (nt_dot(d_gate, w_g[0]) + nt_dot(d_up, w_g[1])).astype(BF16)
+
+        square_kernel(
+            rows, True, True, compute, share, full, gbuf, pbuf, (rcore, rxd, ryd, rx, ry), out, send, recv, lsem
+        )
+        for slot in range(2):
+            for k in range(2):
+                pltpu.make_async_copy(stage.at[slot, k], dg_ref.at[k, 0, 0], osem.at[slot, k]).wait()
+
+    return pl.pallas_call(
+        kernel,
+        out_shape=[
+            jax.ShapeDtypeStruct((rows, D), F32),
+            jax.ShapeDtypeStruct((4, 2, rows, D), BF16),
+            jax.ShapeDtypeStruct((2, 4, 2, rows, live), BF16),
+        ],
+        in_specs=[ANY] * 19,
+        out_specs=[VM, ANY, ANY],
+        scratch_shapes=[
+            pltpu.VMEM((2, D, live), BF16),
+            pltpu.VMEM((live, D), BF16),
+            pltpu.VMEM((4, 2, rows, D), BF16),
+            pltpu.VMEM((2, rows, live), BF16),
+            pltpu.VMEM((2, 2, rows, live), BF16),
+        ]
+        + scatter_scratch(rows, D)
+        + [
+            pltpu.SemaphoreType.DMA((8,)),
+            pltpu.SemaphoreType.DMA((8,)),
+            pltpu.SemaphoreType.DMA((2,)),
+            pltpu.SemaphoreType.DMA((2, 2)),
+        ]
+        + SEMS,
+        compiler_params=params(2),
+        cost_estimate=pl.CostEstimate(flops=100 << 30, bytes_accessed=300 << 20, transcendentals=0),
+        name="ffn_back",
+    )(ffn_grad, act, pull, *gateup_pieces, *down_pieces)
+
+
+def out_back_call(attn_grad, pieces):
+    rows = attn_grad.shape[0]
+    cols = pieces[0].shape[0] * 2
+    depth = pieces[0].shape[1]
+
+    def kernel(share, *rest):
+        piece_refs, (full, dout, w_buf, gbuf, wsem, send, recv, lsem) = rest[:8], rest[8:]
+        copies = weight_copies(piece_refs, column_place(w_buf, depth), wsem)
+        for copy in copies:
+            copy.start()
+        for copy in copies:
+            copy.wait()
+
+        def compute(t, chip, which):
+            dout[chip, which] = nt_dot(gbuf[chip, which], w_buf[...]).astype(BF16)
+
+        square_kernel(rows, True, False, compute, share, full, gbuf, None, None, None, send, recv, lsem)
+
+    return pl.pallas_call(
+        kernel,
+        out_shape=[
+            jax.ShapeDtypeStruct((4, 2, rows, D), BF16),
+            jax.ShapeDtypeStruct((4, 2, rows, cols), BF16),
+        ],
+        in_specs=[ANY] * 9,
+        out_specs=[ANY, VM],
+        scratch_shapes=[
+            pltpu.VMEM((cols, D), BF16),
+            pltpu.VMEM((4, 2, rows, D), BF16),
+            pltpu.SemaphoreType.DMA((8,)),
+        ]
+        + SEMS,
+        compiler_params=params(3),
+        cost_estimate=pl.CostEstimate(flops=40 << 30, bytes_accessed=100 << 20, transcendentals=0),
+        name="out_back",
+    )(attn_grad, *pieces)
+
+
+def input_back_call(grad_proj, pieces, rows):
+    cols = grad_proj.shape[2]
+    depth = pieces[0].shape[1] * 2
+
+    def kernel(da_ref, *rest):
+        piece_refs, (out, w_buf, pbuf, rcore, rxd, ryd, rx, ry, wsem, send, recv, lsem) = rest[:8], rest[8:]
+        copies = weight_copies(piece_refs, row_place(w_buf, depth), wsem)
+        for copy in copies:
+            copy.start()
+        for copy in copies:
+            copy.wait()
+
+        def compute(t, chip, which):
+            part = nt_dot(da_ref[0, chip, which], w_buf[0])
+            part += nt_dot(da_ref[1, chip, which], w_buf[1])
+            part += nt_dot(da_ref[2, chip, which], w_buf[2])
+            pbuf[chip, which] = part.astype(BF16)
+
+        square_kernel(
+            rows, False, True, compute, None, None, None, pbuf, (rcore, rxd, ryd, rx, ry), out, send, recv, lsem
+        )
+
+    return pl.pallas_call(
+        kernel,
+        out_shape=jax.ShapeDtypeStruct((rows, D), F32),
+        in_specs=[VM] + [ANY] * 8,
+        out_specs=VM,
+        scratch_shapes=[pltpu.VMEM((3, D, cols), BF16)]
+        + scatter_scratch(rows, D)
+        + [pltpu.SemaphoreType.DMA((8,))]
+        + SEMS,
+        compiler_params=params(4),
+        cost_estimate=pl.CostEstimate(flops=50 << 30, bytes_accessed=100 << 20, transcendentals=0),
+        name="input_back",
+    )(grad_proj.reshape(3, 4, 2, rows, cols), *pieces)
+
+
+def body_ring(
+    block_input,
+    cotangent,
+    prefix_len,
+    cluster_id,
+    positions,
+    step_count,
+    master_qkv,
+    first_qkv,
+    second_qkv,
+    master_out,
+    first_out,
+    second_out,
+    master_gateup,
+    first_gateup,
+    second_gateup,
+    master_down,
+    first_down,
+    second_down,
+    master_norm,
+    first_norm,
+    second_norm,
+):
+    token_count = block_input.shape[0]
+    protein_count = token_count // LEN
+    share_rows = cotangent.shape[0]
+    share_start = lax.axis_index("mp") * share_rows
+    deep_alpha = math.sqrt(2.0 * DEPTH)
+    depth = master_qkv.shape[1]
+    half = depth // 2
+
+    low_qkv = master_qkv.astype(BF16)
+    qkv_pieces = ring_gather(low_qkv[:, :half], low_qkv[:, half:])
+    low_out = master_out.astype(BF16)
+    out_half = low_out.shape[0] // 2
+    out_pieces = ring_gather(low_out[:out_half], low_out[out_half:])
+    low_gateup = master_gateup.astype(BF16)
+    gateup_pieces = ring_gather(low_gateup[0], low_gateup[1])
+    low_down = master_down.astype(BF16)
+    down_half = low_down.shape[0] // 2
+    down_pieces = ring_gather(low_down[:down_half], low_down[down_half:])
+    w_norm = lax.optimization_barrier(master_norm.astype(BF16)).astype(F32)
+
+    cos_table, sin_table = rope_tables(positions)
+    sign = jnp.where(jnp.arange(HEAD_DIM) < HEAD_DIM // 2, -1.0, 1.0).astype(F32)
+    sin_table = sin_table * sign[None, :]
+    queries, key_rows, value_rows = qkv_call(block_input, qkv_pieces, cos_table, sin_table)
+    attended, probs = attention_call(queries, key_rows, value_rows, prefix_len)
+    attn_share = out_call(attended, out_pieces, share_rows)
+    input_share = lax.dynamic_slice_in_dim(block_input, share_start, share_rows, 0).astype(F32)
+    middle_share, normed_one, inv_one = norm_forward(
+        deep_alpha * input_share + attn_share, w_norm[0], w_norm[1]
+    )
+    ffn_share, middle_low, hidden, act, pull = ffn_call(
+        middle_share.astype(BF16), gateup_pieces, down_pieces
+    )
+    out_share, normed_two, inv_two = norm_forward(
+        deep_alpha * middle_share + ffn_share, w_norm[2], w_norm[3]
+    )
+    block_output = out_share.astype(BF16)
+    matches = (cluster_id[:, None] == cluster_id[None, :]).astype(F32)
+    counts = jnp.sum(matches, axis=1)
+    group_counts = lax.dynamic_slice_in_dim(
+        counts, lax.axis_index("dp") * protein_count, protein_count, 0
+    )
+    row_protein = (share_start + jnp.arange(share_rows)) // LEN
+    one_hot = (row_protein[:, None] == jnp.arange(protein_count)[None, :]).astype(F32)
+    row_weight = jnp.sum(one_hot * (1.0 / group_counts)[None, :], axis=1)
+    grad_output = cotangent.astype(F32) * row_weight[:, None]
+    grad_h2, grad_gain_two, grad_bias_two = norm_backward(
+        grad_output, normed_two, inv_two, w_norm[2]
+    )
+    middle_grad, ffn_grad, grad_gateup_rows = ffn_back_call(
+        grad_h2.astype(BF16), act, pull, gateup_pieces, down_pieces
+    )
+    hidden = hidden.reshape(token_count, -1)
+    middle_low = middle_low.reshape(token_count, D)
+    ffn_grad = ffn_grad.reshape(token_count, D)
+    grad_gateup_rows = grad_gateup_rows.reshape(2, token_count, -1)
+    grad_down_part = jnp.einsum("tf,td->fd", hidden, ffn_grad, preferred_element_type=F32).astype(BF16)
+    grad_gateup_part = jnp.einsum(
+        "td,jtf->jdf", middle_low, grad_gateup_rows, preferred_element_type=F32
+    ).astype(BF16)
+    middle_grad = middle_grad + deep_alpha * grad_h2
+    grad_h1, grad_gain_one, grad_bias_one = norm_backward(
+        middle_grad, normed_one, inv_one, w_norm[0]
+    )
+    attn_grad, grad_attended = out_back_call(grad_h1.astype(BF16), out_pieces)
+    attn_grad = attn_grad.reshape(token_count, D)
+    grad_attended = grad_attended.reshape(token_count, -1)
+    grad_out_part = jnp.einsum("tc,td->cd", attended, attn_grad, preferred_element_type=F32).astype(BF16)
+    grad_proj = attention_back_call(
+        queries, key_rows, value_rows, probs, attended, grad_attended, cos_table, sin_table
+    )
+    grad_qkv_part = jnp.einsum("td,jtc->jdc", block_input, grad_proj, preferred_element_type=F32).astype(BF16)
+    input_share_grad = input_back_call(grad_proj, qkv_pieces, share_rows)
+    grad_input = (input_share_grad + deep_alpha * grad_h1).astype(BF16)
+    norm_terms = jnp.stack([grad_gain_one, grad_bias_one, grad_gain_two, grad_bias_two])
+    grad_norm = lax.psum(norm_terms, ("dp", "mp"))
+
+    def down_shard(owner):
+        part = lax.dynamic_slice_in_dim(grad_down_part, owner * depth, depth, 1)
+        return part[:down_half], part[down_half:]
+
+    def gateup_shard(owner):
+        part = lax.dynamic_slice_in_dim(grad_gateup_part, owner * depth, depth, 1)
+        return part[0], part[1]
+
+    def out_shard(owner):
+        part = lax.dynamic_slice_in_dim(grad_out_part, owner * depth, depth, 1)
+        return part[:out_half], part[out_half:]
+
+    def qkv_shard(owner):
+        part = lax.dynamic_slice_in_dim(grad_qkv_part, owner * depth, depth, 1)
+        return part[:, :half], part[:, half:]
+
+    red_down = jnp.concatenate(ring_scatter(down_shard), axis=0)
+    red_gateup = jnp.stack(ring_scatter(gateup_shard))
+    red_out = jnp.concatenate(ring_scatter(out_shard), axis=0)
+    red_qkv = jnp.concatenate(ring_scatter(qkv_shard), axis=1)
+
+    step_value = step_count[0].astype(F32)
+    rate_qkv = D ** (-0.5)
+    rate_out = max(HEADS * HEAD_DIM // 512, 1) ** (-0.5)
+    rate_gateup = D ** (-0.5)
+    rate_down = max(FF // 64, 1) ** (-0.5)
+    rate_norm = 1.0
+    new_qkv, new_first_qkv, new_second_qkv = adamw_step(
+        master_qkv, first_qkv, second_qkv, red_qkv, rate_qkv, step_value
+    )
+    new_out, new_first_out, new_second_out = adamw_step(
+        master_out, first_out, second_out, red_out, rate_out, step_value
+    )
+    new_gateup, new_first_gateup, new_second_gateup = adamw_step(
+        master_gateup, first_gateup, second_gateup, red_gateup, rate_gateup, step_value
+    )
+    new_down, new_first_down, new_second_down = adamw_step(
+        master_down, first_down, second_down, red_down, rate_down, step_value
+    )
+    new_norm, new_first_norm, new_second_norm = adamw_step(
+        master_norm, first_norm, second_norm, grad_norm, rate_norm, step_value
+    )
+    return (
+        block_output,
+        grad_input,
+        red_qkv,
+        new_qkv,
+        new_first_qkv,
+        new_second_qkv,
+        red_out,
+        new_out,
+        new_first_out,
+        new_second_out,
+        red_gateup,
+        new_gateup,
+        new_first_gateup,
+        new_second_gateup,
+        red_down,
+        new_down,
+        new_first_down,
+        new_second_down,
+        grad_norm,
+        new_norm,
+        new_first_norm,
+        new_second_norm,
+    )
+
+
 def solution(mesh):
     placed = (
         P("dp", None),
@@ -367,8 +1231,9 @@
         P(),
         P(),
     )
+    ring = mesh.shape["dp"] == 4 and mesh.shape["mp"] == 8
     return jax.shard_map(
-        body,
+        body_ring if ring else body_plain,
         mesh=mesh,
         in_specs=placed,
         out_specs=(

time: 1200 us -> 990 us (0.82)
  Pallas kernels: 0 us -> 466 us
  waiting for transfers between devices: 686 us -> 225 us
  matrix products: 241 us -> 53.6 us
  starting transfers between devices: 1.41 us -> 70.2 us
  other arithmetic: 109 us -> 61.4 us
  local copies, waits for them, and re-layouts: 97.4 us -> 51.6 us
  between operations: 16.6 us -> 2.65 us
    pallas_call x0 -> x8, Pallas kernels: none -> 466 us  [the longest x1 108 us: ffn_back_call(): pl.pallas_call(kernel, out_shape=[jax.ShapeDtypeStruct((rows, D), F32), j...]
    reduce_scatter x8 -> x0, waiting for transfers between devices: 349 us -> none  [the longest x1 84 us: body(): lax.psum_scatter(middle_grad_part.astype(jnp.bfloat16), 'mp', scatter_dim...]
    all_gather x7 -> x0, waiting for transfers between devices: 337 us -> none  [the longest x1 99.8 us: body(): lax.all_gather(master_gateup.astype(jnp.bfloat16), 'dp', axis=1, tiled=True)]
    ppermute x0 -> x48, waiting for transfers between devices: none -> 225 us  [the longest x4 50.1 us: ring_scatter(): lax.ppermute((prv[1].astype(F32) + minus_far.astype(F32)).astype(BF16), '...]
    dot_general x30 -> x4, matrix products: 241 us -> 53.6 us  [the longest x1 19.3 us: body_ring(): jnp.einsum('td,jtf->jdf', middle_low, grad_gateup_rows, preferred_element...]
    ppermute x0 -> x48, starting transfers between devices: none -> 70.2 us  [the longest x4 12.6 us: ring_gather(): lax.ppermute(right[1], 'dp', MINUS)]
    concatenate x10 -> x0, local copies, waits for them, and re-layouts: 23.4 us -> none  [the longest x4 12.5 us: rotate_back(): jnp.concatenate([values[..., middle:], -values[..., :middle]], axis=-1)]
    convert_element_type x14, other arithmetic: 34 us -> 16.2 us  [the longest x1 3.58 us: body_ring(): grad_input = (input_share_grad + deep_alpha * grad_h1).astype(BF16)]
  transfers between devices with their start and end apart: 15 -> 48, of which waited for: 11 -> 18; matrix products, arithmetic and copies ran while one was open for 28% -> 12% of each run, Pallas kernels for 0% -> 26%
where the time goes in v1:
time: 990 us; the launch traced here: 980 us
  Pallas kernels  466 us (47%)
  waiting for transfers between devices  225 us (23%)
  starting transfers between devices  70.2 us (7%)
  other arithmetic  61.4 us (6%)
  matrix products  53.6 us (5%)
  local copies, waits for them, and re-layouts  51.6 us (5%)
  blocking collectives  49.3 us (5%)
    pallas_call x1, Pallas kernels, ffn_back_call(): pl.pallas_call(kernel, out_shape=[jax.ShapeDtypeStruct((rows, D), F32), j...  108 us
    pallas_call x1, Pallas kernels, ffn_call(): pl.pallas_call(kernel, out_shape=[jax.ShapeDtypeStruct((rows, D), F32), j...  106 us
    pallas_call x1, Pallas kernels, out_back_call(): pl.pallas_call(kernel, out_shape=[jax.ShapeDtypeStruct((4, 2, rows, D), B...  61.7 us
    pallas_call x1, Pallas kernels, input_back_call(): pl.pallas_call(kernel, out_shape=jax.ShapeDtypeStruct((rows, D), F32), in...  59.5 us
    pallas_call x1, Pallas kernels, out_call(): pl.pallas_call(kernel, out_shape=jax.ShapeDtypeStruct((rows, D), F32), in...  56.5 us
    ppermute x4, waiting for transfers between devices, ring_scatter(): lax.ppermute((prv[1].astype(F32) + minus_far.astype(F32)).astype(BF16), '...  50.1 us
    psum x1, blocking collectives, body_ring(): grad_norm = lax.psum(norm_terms, ('dp', 'mp'))  49.3 us
    ppermute x4, waiting for transfers between devices, ring_gather(): lax.ppermute(second, 'dp', MINUS)  46.3 us
  transfers between devices with their start and end apart: 48, of which 18 were waited for; matrix products, arithmetic and copies ran while one was open for 12% of the time, Pallas kernels for 26%

profile of v1, /device:TPU:0, one launch (start us, length us, event | category | flops | bytes accessed | tf_op | source)
XLA Modules:
  0.0 980.3 jit_solution(17849350156224356316)
XLA Ops:
  26.4 29.4 %collective-permute-done.6.rest_2_ = bf16[128,512]{1,0:T(8,128)(2,1)} collective-permute-done((bf16[128,512]{1,0:T(8,128)(2,1)}, bf16[128,512]{1,0:T(8,128)(2,1)}, u32[]{:S(2)}, u32[]{:S(2)}) %collective-permute-start.6) | collective-permute-done | bytes 131104 | tf_op jit(solution)/shard_map/ppermute | solution.py:365
  62.1 31.9 %collective-permute-done.3.rest_5_ = bf16[3,256,256]{2,1,0:T(8,128)(2,1)} collective-permute-done((bf16[3,256,256]{2,1,0:T(8,128)(2,1)S(1)}, bf16[3,256,256]{2,1,0:T(8,128)(2,1)}, u32[]{:S(2)}, u32[]{:S(2)}) %collective-permute-start.3) | collective-permute-done | bytes 393248 | tf_op jit(solution)/shard_map/ppermute | solution.py:366
  119.4 14.4 %collective-permute-done.9.rest_5_ = bf16[128,512]{1,0:T(8,128)(2,1)} collective-permute-done((bf16[128,512]{1,0:T(8,128)(2,1)}, bf16[128,512]{1,0:T(8,128)(2,1)}, u32[]{:S(2)}, u32[]{:S(2)}) %collective-permute-start.9) | collective-permute-done | bytes 131104 | tf_op jit(solution)/shard_map/ppermute | solution.py:366
  141.7 15.5 %qkv.1 = (bf16[2688,256]{1,0:T(8,128)(2,1)}, bf16[2688,256]{1,0:T(8,128)(2,1)}, bf16[2688,256]{1,0:T(8,128)(2,1)}) custom-call(bf16[2688,2048]{1,0:T(8,128)(2,1)} %x_ref.1, f32[2688,128]{1,0:T(8,128)} %get-tuple-element.195.cos_ref, f32[2688,128]{1,0:T(8,128)} %get-tuple-element.196.sin_ref, bf16[3,256,256]{2,1,0:T(8,128)(2,1)} %get-tuple-element.184.rest_0_, ...), custom_call_target="tpu_custom_call" | custom-call | flops 8455716864 | bytes 20971520 | tf_op jit(solution)/shard_map/qkv/pallas_call | solution.py:655
  157.3 29.0 %attention.1 = (bf16[2688,256]{1,0:T(8,128)(2,1)}, bf16[3,2,896,896]{3,2,1,0:T(8,128)(2,1)}) custom-call(s32[3]{0:T(128)} %pre_ref.1, bf16[2688,256]{1,0:T(8,128)(2,1)} %get-tuple-element.37.q_ref, bf16[2688,256]{1,0:T(8,128)(2,1)} %get-tuple-element.38.k_ref, bf16[2688,256]{1,0:T(8,128)(2,1)} %get-tuple-element.39.v_ref), custom_call_target="tpu_custom_call" | custom-call | flops 2466250752 | bytes 16777216 | tf_op jit(solution)/shard_map/attention/pallas_call | solution.py:696
  190.5 56.5 %out_reduce.1 = f32[336,2048]{1,0:T(8,128)} custom-call(bf16[4,2,336,256]{3,2,1,0:T(8,128)(2,1)} %bitcast.97, bf16[128,512]{1,0:T(8,128)(2,1)} %get-tuple-element.188.rest_0_, bf16[128,512]{1,0:T(8,128)(2,1)} %get-tuple-element.187.rest_1_, bf16[128,512]{1,0:T(8,128)(2,1)} %collective-permute-done.6.rest_2_, bf16[128,512]{1,0:T(8,128)(2,1)} %copy-done.48, ...), custom_call_target="tpu_custom_call" | custom-call | flops 42949672960 | bytes 104857600 | tf_op jit(solution)/shard_map/out_reduce/pallas_call | solution.py:785
  262.1 9.1 collective-permute-done.22.rest_14_
  276.8 105.9 %ffn.1 = (f32[336,2048]{1,0:T(8,128)}, bf16[4,2,336,2048]{3,2,1,0:T(8,128)(2,1)}, bf16[4,2,336,704]{3,2,1,0:T(8,128)(2,1)}, bf16[4,2,336,704]{3,2,1,0:T(8,128)(2,1)}, bf16[4,2,336,704]{3,2,1,0:T(8,128)(2,1)}) custom-call(bf16[336,2048]{1,0:T(8,128)(2,1)} %fusion.13.share, bf16[512,704]{1,0:T(8,128)(2,1)} %get-tuple-element.168.rest_0_, ...), custom_call_target="tpu_custom_call" | custom-call | flops 107374182400 | bytes 314572800 | tf_op jit(solution)/shard_map/ffn/pallas_call | solution.py:853
  391.1 107.8 %ffn_back.1 = (f32[336,2048]{1,0:T(8,128)}, bf16[4,2,336,2048]{3,2,1,0:T(8,128)(2,1)}, bf16[2,4,2,336,704]{4,3,2,1,0:T(8,128)(2,1)}) custom-call(bf16[336,2048]{1,0:T(8,128)(2,1)} %fusion.25.share, bf16[4,2,336,704]{3,2,1,0:T(8,128)(2,1)} %get-tuple-element.43.act_ref, bf16[4,2,336,704]{3,2,1,0:T(8,128)(2,1)} %get-tuple-element.44.pull_ref, ...), custom_call_target="tpu_custom_call" | custom-call | flops 107374182400 | bytes 314572800 | tf_op jit(solution)/shard_map/ffn_back/pallas_call | solution.py:937
  505.0 49.3 %psum.7 = f32[4,2048]{1,0:T(4,128)} all-reduce(f32[4,2048]{1,0:T(4,128)S(1)} %pad_maximum_fusion.5), channel_id=1, replica_groups=mesh['dp'=4,'mp'=8] {'dp','mp'}, use_global_device_ids=true, to_apply=%region_14.15 | all-reduce | flops 8192 | bytes 65536 | tf_op jit(solution)/shard_map/psum | solution.py:1140
  554.3 12.6 %bitcast_convert_fusion.1 = bf16[704,2048]{1,0:T(8,128)(2,1)S(1)} fusion(bf16[4,2,336,704]{3,2,1,0:T(8,128)(2,1)} %get-tuple-element.50, bf16[4,2,336,2048]{3,2,1,0:T(8,128)(2,1)} %get-tuple-element.51), kind=kOutput, calls=%fused_computation.5 | convolution fusion | flops 7752515584 | bytes 17678336 | tf_op jit(solution)/shard_map/tf,td->fd/dot_general | solution.py:1121
  572.0 19.3 %bitcast_convert_fusion = bf16[2,704,2048]{2,1,0:T(8,128)(2,1)S(1)} fusion(bf16[2,4,2,336,704]{4,3,2,1,0:T(8,128)(2,1)S(1)} %copy-done.52, bf16[4,2,336,2048]{3,2,1,0:T(8,128)(2,1)} %get-tuple-element.49), kind=kOutput, calls=%fused_computation | convolution fusion | flops 15505031168 | bytes 24346624 | tf_op jit(solution)/shard_map/td,jtf->jdf/dot_general | solution.py:1122
  599.8 61.7 %out_back.1 = (bf16[4,2,336,2048]{3,2,1,0:T(8,128)(2,1)}, bf16[4,2,336,256]{3,2,1,0:T(8,128)(2,1)}) custom-call(bf16[336,2048]{1,0:T(8,128)(2,1)} %get-tuple-element.144.share, bf16[128,512]{1,0:T(8,128)(2,1)} %get-tuple-element.188.rest_0_, bf16[128,512]{1,0:T(8,128)(2,1)} %get-tuple-element.187.rest_1_, bf16[128,512]{1,0:T(8,128)(2,1)} %collective-permute-done.6.rest_2_, ...), custom_call_target="tpu_custom_call" | custom-call | flops 42949672960 | bytes 104857600 | tf_op jit(solution)/shard_map/out_back/pallas_call | solution.py:985
  674.5 30.2 %attention_back.1 = bf16[3,2688,256]{2,1,0:T(8,128)(2,1)} custom-call(bf16[2688,256]{1,0:T(8,128)(2,1)} %get-tuple-element.37.q_ref, bf16[2688,256]{1,0:T(8,128)(2,1)} %get-tuple-element.38.k_ref, bf16[2688,256]{1,0:T(8,128)(2,1)} %get-tuple-element.39.v_ref, bf16[3,2,896,896]{3,2,1,0:T(8,128)(2,1)} %get-tuple-element.42.p_ref, ...), custom_call_target="tpu_custom_call" | custom-call | flops 4932501504 | bytes 20971520 | tf_op jit(solution)/shard_map/attention_back/pallas_call | solution.py:749
  704.6 14.4 %fusion.6 = bf16[3,256,2048]{2,1,0:T(8,128)(2,1)} fusion(bf16[3,2688,256]{2,1,0:T(8,128)(2,1)} %attention_back.1, bf16[2688,2048]{1,0:T(8,128)(2,1)} %x_ref.1), kind=kOutput, calls=%fused_computation.7 | convolution fusion | flops 8457289728 | bytes 18284544 | tf_op jit(solution)/shard_map/td,jtc->jdc/dot_general | solution.py:1136
  719.1 59.5 %input_back.1 = f32[336,2048]{1,0:T(8,128)} custom-call(bf16[3,4,2,336,256]{4,3,2,1,0:T(8,128)(2,1)} %bitcast.98, bf16[3,256,256]{2,1,0:T(8,128)(2,1)} %get-tuple-element.184.rest_0_, bf16[3,256,256]{2,1,0:T(8,128)(2,1)} %copy-done.33, bf16[3,256,256]{2,1,0:T(8,128)(2,1)} %collective-permute-done.rest_2_, ...), custom_call_target="tpu_custom_call" | custom-call | flops 53687091200 | bytes 104857600 | tf_op jit(solution)/shard_map/input_back/pallas_call | solution.py:1027
  798.6 20.8 %collective-permute-done.33 = bf16[128,512]{1,0:T(8,128)(2,1)S(1)} collective-permute-done((bf16[128,512]{1,0:T(8,128)(2,1)S(1)}, bf16[128,512]{1,0:T(8,128)(2,1)S(1)}, u32[]{:S(2)}, u32[]{:S(2)}) %collective-permute-start.33) | collective-permute-done | bytes 131104 | tf_op jit(solution)/shard_map/ppermute | solution.py:379
  831.3 7.8 collective-permute-done.24
  846.2 8.3 collective-permute-done.36
  856.3 14.5 %collective-permute-done.43 = bf16[352,512]{1,0:T(8,128)(2,1)S(1)} collective-permute-done((bf16[352,512]{1,0:T(8,128)(2,1)S(1)}, bf16[352,512]{1,0:T(8,128)(2,1)S(1)}, u32[]{:S(2)}, u32[]{:S(2)}) %collective-permute-start.43) | collective-permute-done | bytes 360480 | tf_op jit(solution)/shard_map/ppermute | solution.py:381
  879.9 7.8 collective-permute-done.29
  910.8 30.0 %collective-permute-done.47 = bf16[352,512]{1,0:T(8,128)(2,1)} collective-permute-done((bf16[352,512]{1,0:T(8,128)(2,1)}, bf16[352,512]{1,0:T(8,128)(2,1)}, u32[]{:S(2)}, u32[]{:S(2)}) %collective-permute-start.47) | collective-permute-done | bytes 360480 | tf_op jit(solution)/shard_map/ppermute | solution.py:382
  946.9 10.7 %collective-permute-done.41 = bf16[512,704]{0,1:T(8,128)(2,1)} collective-permute-done((bf16[512,704]{0,1:T(8,128)(2,1)}, bf16[512,704]{0,1:T(8,128)(2,1)}, u32[]{:S(2)}, u32[]{:S(2)}) %collective-permute-start.41) | collective-permute-done | bytes 720928 | tf_op jit(solution)/shard_map/ppermute | solution.py:382
  957.6 13.5 %collective-permute-done.37 = bf16[512,704]{0,1:T(8,128)(2,1)S(1)} collective-permute-done((bf16[512,704]{0,1:T(8,128)(2,1)}, bf16[512,704]{0,1:T(8,128)(2,1)S(1)}, u32[]{:S(2)}, u32[]{:S(2)}) %collective-permute-start.37) | collective-permute-done | bytes 720928 | tf_op jit(solution)/shard_map/ppermute | solution.py:381
  (271 shorter events, 217.7 us)
Async XLA Ops:
  6.3 91.5 %collective-permute-start.15 = (bf16[512,704]{0,1:T(8,128)(2,1)}, bf16[512,704]{0,1:T(8,128)(2,1)}, u32[]{:S(2)}, u32[]{:S(2)}) collective-permute-start(bf16[512,704]{0,1:T(8,128)(2,1)} %copy.81), channel_id=1, source_target_pairs={{8,0},{16,8},{24,16},{0,24},{9,1},{17,9},{25,17},{1,25},{10,2},{18... | collective-permute-start | bytes 2162696 | tf_op jit(solution)/shard_map/ppermute | solution.py:366
  11.4 86.5 %collective-permute-start.13 = (bf16[512,704]{0,1:T(8,128)(2,1)}, bf16[512,704]{0,1:T(8,128)(2,1)}, u32[]{:S(2)}, u32[]{:S(2)}) collective-permute-start(bf16[512,704]{0,1:T(8,128)(2,1)} %copy.81), channel_id=1, source_target_pairs={{0,8},{8,16},{16,24},{24,0},{1,9},{9,17},{17,25},{25,1},{2,10},{10... | collective-permute-start | bytes 2162696 | tf_op jit(solution)/shard_map/ppermute | solution.py:365
  15.8 78.8 %collective-permute-start.12 = (bf16[512,704]{0,1:T(8,128)(2,1)}, bf16[512,704]{0,1:T(8,128)(2,1)}, u32[]{:S(2)}, u32[]{:S(2)}) collective-permute-start(bf16[512,704]{0,1:T(8,128)(2,1)} %copy.80), channel_id=1, source_target_pairs={{0,8},{8,16},{16,24},{24,0},{1,9},{9,17},{17,25},{25,1},{2,10},{10... | collective-permute-start | bytes 2162696 | tf_op jit(solution)/shard_map/ppermute | solution.py:365
  133.7 52.6 %collective-permute-start.7 = (bf16[128,512]{1,0:T(8,128)(2,1)S(1)}, bf16[128,512]{1,0:T(8,128)(2,1)S(1)}, u32[]{:S(2)}, u32[]{:S(2)}) collective-permute-start(bf16[128,512]{1,0:T(8,128)(2,1)S(1)} %copy-done.38), channel_id=1, source_target_pairs={{0,8},{8,16},{16,24},{24,0},{1,9},{9,17},{17,25},{25,1},{2,10},{10... | collective-permute-start | bytes 393224 | tf_op jit(solution)/shard_map/ppermute | solution.py:365
  135.0 51.6 %collective-permute-start.8 = (bf16[128,512]{1,0:T(8,128)(2,1)}, bf16[128,512]{1,0:T(8,128)(2,1)S(1)}, u32[]{:S(2)}, u32[]{:S(2)}) collective-permute-start(bf16[128,512]{1,0:T(8,128)(2,1)} %get-tuple-element.188.rest_0_), channel_id=1, source_target_pairs={{8,0},{16,8},{24,16},{0,24},{9,1},{17,9},{25,17},{1,25},{10,2},{18... | collective-permute-start | bytes 393224 | tf_op jit(solution)/shard_map/ppermute | solution.py:366
  137.6 114.5 %collective-permute-start.21 = (bf16[352,512]{1,0:T(8,128)(2,1)}, bf16[352,512]{1,0:T(8,128)(2,1)}, u32[]{:S(2)}, u32[]{:S(2)}) collective-permute-start(bf16[352,512]{1,0:T(8,128)(2,1)} %get-tuple-element.185.rest_9_), channel_id=1, source_target_pairs={{8,0},{16,8},{24,16},{0,24},{9,1},{17,9},{25,17},{1,25},{10,2},{18... | collective-permute-start | bytes 1081352 | tf_op jit(solution)/shard_map/ppermute | solution.py:366
  137.7 48.9 %collective-permute-start.10 = (bf16[128,512]{1,0:T(8,128)(2,1)}, bf16[128,512]{1,0:T(8,128)(2,1)S(1)}, u32[]{:S(2)}, u32[]{:S(2)}) collective-permute-start(bf16[128,512]{1,0:T(8,128)(2,1)} %collective-permute-done.6.rest_2_), channel_id=1, source_target_pairs={{0,8},{8,16},{16,24},{24,0},{1,9},{9,17},{17,25},{25,1},{2,10},{10... | collective-permute-start | bytes 393224 | tf_op jit(solution)/shard_map/ppermute | solution.py:367
  139.6 48.0 %collective-permute-start.11 = (bf16[128,512]{1,0:T(8,128)(2,1)}, bf16[128,512]{1,0:T(8,128)(2,1)S(1)}, u32[]{:S(2)}, u32[]{:S(2)}) collective-permute-start(bf16[128,512]{1,0:T(8,128)(2,1)} %collective-permute-done.9.rest_5_), channel_id=1, source_target_pairs={{8,0},{16,8},{24,16},{0,24},{9,1},{17,9},{25,17},{1,25},{10,2},{18... | collective-permute-start | bytes 393224 | tf_op jit(solution)/shard_map/ppermute | solution.py:367
  186.4 75.7 %collective-permute-start.19 = (bf16[352,512]{1,0:T(8,128)(2,1)}, bf16[352,512]{1,0:T(8,128)(2,1)}, u32[]{:S(2)}, u32[]{:S(2)}) collective-permute-start(bf16[352,512]{1,0:T(8,128)(2,1)} %get-tuple-element.185.rest_9_), channel_id=1, source_target_pairs={{0,8},{8,16},{16,24},{24,0},{1,9},{9,17},{17,25},{25,1},{2,10},{10... | collective-permute-start | bytes 1081352 | tf_op jit(solution)/shard_map/ppermute | solution.py:365
  186.5 63.5 %collective-permute-start.18 = (bf16[352,512]{1,0:T(8,128)(2,1)}, bf16[352,512]{1,0:T(8,128)(2,1)}, u32[]{:S(2)}, u32[]{:S(2)}) collective-permute-start(bf16[352,512]{1,0:T(8,128)(2,1)} %get-tuple-element.186.rest_8_), channel_id=1, source_target_pairs={{0,8},{8,16},{16,24},{24,0},{1,9},{9,17},{17,25},{25,1},{2,10},{10... | collective-permute-start | bytes 1081352 | tf_op jit(solution)/shard_map/ppermute | solution.py:365
  186.6 65.5 %collective-permute-start.16 = (bf16[512,704]{0,1:T(8,128)(2,1)}, bf16[512,704]{0,1:T(8,128)(2,1)}, u32[]{:S(2)}, u32[]{:S(2)}) collective-permute-start(bf16[512,704]{0,1:T(8,128)(2,1)} %collective-permute-done.12), channel_id=1, source_target_pairs={{0,8},{8,16},{16,24},{24,0},{1,9},{9,17},{17,25},{25,1},{2,10},{10... | collective-permute-start | bytes 2162696 | tf_op jit(solution)/shard_map/ppermute | solution.py:367
  187.6 72.2 %collective-permute-start.17 = (bf16[512,704]{0,1:T(8,128)(2,1)}, bf16[512,704]{0,1:T(8,128)(2,1)}, u32[]{:S(2)}, u32[]{:S(2)}) collective-permute-start(bf16[512,704]{0,1:T(8,128)(2,1)} %collective-permute-done.15), channel_id=1, source_target_pairs={{8,0},{16,8},{24,16},{0,24},{9,1},{17,9},{25,17},{1,25},{10,2},{18... | collective-permute-start | bytes 2162696 | tf_op jit(solution)/shard_map/ppermute | solution.py:367
  568.1 225.6 %collective-permute-start.42 = (bf16[352,512]{1,0:T(8,128)(2,1)}, bf16[352,512]{1,0:T(8,128)(2,1)}, u32[]{:S(2)}, u32[]{:S(2)}) collective-permute-start(bf16[352,512]{1,0:T(8,128)(2,1)} %get-tuple-element.161), channel_id=1, source_target_pairs={{0,8},{8,16},{16,24},{24,0},{1,9},{9,17},{17,25},{25,1},{2,10},{10... | collective-permute-start | bytes 1081352 | tf_op jit(solution)/shard_map/ppermute | solution.py:377
  570.2 272.2 %collective-permute-start.44 = (bf16[352,512]{1,0:T(8,128)(2,1)}, bf16[352,512]{1,0:T(8,128)(2,1)}, u32[]{:S(2)}, u32[]{:S(2)}) collective-permute-start(bf16[352,512]{1,0:T(8,128)(2,1)} %get-tuple-element.162), channel_id=1, source_target_pairs={{8,0},{16,8},{24,16},{0,24},{9,1},{17,9},{25,17},{1,25},{10,2},{18... | collective-permute-start | bytes 1081352 | tf_op jit(solution)/shard_map/ppermute | solution.py:380
  670.6 112.8 %collective-permute-start.30 = (bf16[128,512]{1,0:T(8,128)(2,1)}, bf16[128,512]{1,0:T(8,128)(2,1)}, u32[]{:S(2)}, u32[]{:S(2)}) collective-permute-start(bf16[128,512]{1,0:T(8,128)(2,1)} %get-tuple-element.175), channel_id=1, source_target_pairs={{0,8},{8,16},{16,24},{24,0},{1,9},{9,17},{17,25},{25,1},{2,10},{10... | collective-permute-start | bytes 393224 | tf_op jit(solution)/shard_map/ppermute | solution.py:377
  670.6 116.7 %collective-permute-start.32 = (bf16[128,512]{1,0:T(8,128)(2,1)}, bf16[128,512]{1,0:T(8,128)(2,1)S(1)}, u32[]{:S(2)}, u32[]{:S(2)}) collective-permute-start(bf16[128,512]{1,0:T(8,128)(2,1)} %get-tuple-element.176), channel_id=1, source_target_pairs={{8,0},{16,8},{24,16},{0,24},{9,1},{17,9},{25,17},{1,25},{10,2},{18... | collective-permute-start | bytes 393224 | tf_op jit(solution)/shard_map/ppermute | solution.py:380
  674.4 114.8 %collective-permute-start.34 = (bf16[128,512]{1,0:T(8,128)(2,1)}, bf16[128,512]{1,0:T(8,128)(2,1)S(1)}, u32[]{:S(2)}, u32[]{:S(2)}) collective-permute-start(bf16[128,512]{1,0:T(8,128)(2,1)} %get-tuple-element.177), channel_id=1, source_target_pairs={{8,0},{16,8},{24,16},{0,24},{9,1},{17,9},{25,17},{1,25},{10,2},{18... | collective-permute-start | bytes 393224 | tf_op jit(solution)/shard_map/ppermute | solution.py:378
  787.3 55.8 %collective-permute-start.46 = (bf16[352,512]{1,0:T(8,128)(2,1)S(1)}, bf16[352,512]{1,0:T(8,128)(2,1)S(1)}, u32[]{:S(2)}, u32[]{:S(2)}) collective-permute-start(bf16[352,512]{1,0:T(8,128)(2,1)S(1)} %copy-done.35), channel_id=1, source_target_pairs={{8,0},{16,8},{24,16},{0,24},{9,1},{17,9},{25,17},{1,25},{10,2},{18... | collective-permute-start | bytes 1081352 | tf_op jit(solution)/shard_map/ppermute | solution.py:378
  789.2 50.2 %collective-permute-start.40 = (bf16[512,704]{0,1:T(8,128)(2,1)S(1)}, bf16[512,704]{0,1:T(8,128)(2,1)S(1)}, u32[]{:S(2)}, u32[]{:S(2)}) collective-permute-start(bf16[512,704]{0,1:T(8,128)(2,1)S(1)} %copy-done.30), channel_id=1, source_target_pairs={{8,0},{16,8},{24,16},{0,24},{9,1},{17,9},{25,17},{1,25},{10,2},{18... | collective-permute-start | bytes 2162696 | tf_op jit(solution)/shard_map/ppermute | solution.py:378
  874.3 72.6 %collective-permute-start.38 = (bf16[512,704]{0,1:T(8,128)(2,1)}, bf16[512,704]{0,1:T(8,128)(2,1)}, u32[]{:S(2)}, u32[]{:S(2)}) collective-permute-start(bf16[512,704]{0,1:T(8,128)(2,1)} %slice_bitcast_fusion.6), channel_id=1, source_target_pairs={{8,0},{16,8},{24,16},{0,24},{9,1},{17,9},{25,17},{1,25},{10,2},{18... | collective-permute-start | bytes 2162696 | tf_op jit(solution)/shard_map/ppermute | solution.py:380
  879.2 67.8 %collective-permute-start.39 = (bf16[512,704]{0,1:T(8,128)(2,1)}, bf16[512,704]{0,1:T(8,128)(2,1)}, u32[]{:S(2)}, u32[]{:S(2)}) collective-permute-start(bf16[512,704]{0,1:T(8,128)(2,1)} %slice_bitcast_fusion.4), channel_id=1, source_target_pairs={{0,8},{8,16},{16,24},{24,0},{1,9},{9,17},{17,25},{25,1},{2,10},{10... | collective-permute-start | bytes 2162696 | tf_op jit(solution)/shard_map/ppermute | solution.py:379
  887.7 53.2 %collective-permute-start.47 = (bf16[352,512]{1,0:T(8,128)(2,1)}, bf16[352,512]{1,0:T(8,128)(2,1)}, u32[]{:S(2)}, u32[]{:S(2)}) collective-permute-start(bf16[352,512]{1,0:T(8,128)(2,1)} %get-tuple-element.160), channel_id=1, source_target_pairs={{8,0},{16,8},{24,16},{0,24},{9,1},{17,9},{25,17},{1,25},{10,2},{18... | collective-permute-start | bytes 1081352 | tf_op jit(solution)/shard_map/ppermute | solution.py:382
  896.2 61.4 %collective-permute-start.41 = (bf16[512,704]{0,1:T(8,128)(2,1)}, bf16[512,704]{0,1:T(8,128)(2,1)}, u32[]{:S(2)}, u32[]{:S(2)}) collective-permute-start(bf16[512,704]{0,1:T(8,128)(2,1)} %fusion.16), channel_id=1, source_target_pairs={{8,0},{16,8},{24,16},{0,24},{9,1},{17,9},{25,17},{1,25},{10,2},{18... | collective-permute-start | bytes 2162696 | tf_op jit(solution)/shard_map/ppermute | solution.py:382
  908.8 62.3 %collective-permute-start.37 = (bf16[512,704]{0,1:T(8,128)(2,1)}, bf16[512,704]{0,1:T(8,128)(2,1)S(1)}, u32[]{:S(2)}, u32[]{:S(2)}) collective-permute-start(bf16[512,704]{0,1:T(8,128)(2,1)} %fusion.19), channel_id=1, source_target_pairs={{0,8},{8,16},{16,24},{24,0},{1,9},{9,17},{17,25},{25,1},{2,10},{10... | collective-permute-start | bytes 2162696 | tf_op jit(solution)/shard_map/ppermute | solution.py:381
  (77 other events, 1763.8 us)

commit v2 on v1

--- a/solution.py
+++ b/solution.py
@@ -353,37 +353,205 @@
 NT = (((1,), (1,)), ((), ()))
 ANY = pl.BlockSpec(memory_space=pl.ANY)
 VM = pl.BlockSpec(memory_space=pltpu.VMEM)
-PLUS = [(0, 1), (1, 2), (2, 3), (3, 0)]
-MINUS = [(1, 0), (2, 1), (3, 2), (0, 3)]
+
+
+LIGHT = pl.CostEstimate(flops=1 << 20, bytes_accessed=1 << 16, transcendentals=0)
 
 
 def nt_dot(left, right):
     return lax.dot_general(left, right, NT, preferred_element_type=F32)
 
 
-def ring_gather(first, second):
-    left = (lax.ppermute(first, "dp", PLUS), lax.ppermute(second, "dp", PLUS))
-    right = (lax.ppermute(first, "dp", MINUS), lax.ppermute(second, "dp", MINUS))
-    far = (lax.ppermute(left[0], "dp", PLUS), lax.ppermute(right[1], "dp", MINUS))
-    return (first, second) + left + right + far
-
-
-def ring_scatter(shard_of):
-    here = lax.axis_index("dp")
-    far = shard_of((here + 2) % 4)
-    nxt = shard_of((here + 1) % 4)
-    prv = shard_of((here + 3) % 4)
-    own = shard_of(here)
-    plus_far = lax.ppermute(far[0], "dp", PLUS)
-    minus_far = lax.ppermute(far[1], "dp", MINUS)
-    plus_b = lax.ppermute(nxt[1], "dp", PLUS)
-    minus_a = lax.ppermute(prv[0], "dp", MINUS)
-    plus_a = lax.ppermute((nxt[0].astype(F32) + plus_far.astype(F32)).astype(BF16), "dp", PLUS)
-    minus_b = lax.ppermute((prv[1].astype(F32) + minus_far.astype(F32)).astype(BF16), "dp", MINUS)
-    return (
-        own[0].astype(F32) + plus_a.astype(F32) + minus_a.astype(F32),
-        own[1].astype(F32) + plus_b.astype(F32) + minus_b.astype(F32),
-    )
+class Ring:
+    def __init__(self, send, recv, local):
+        self.here = lax.axis_index("dp")
+        self.right = (self.here + 1) % 4
+        self.left = (self.here + 3) % 4
+        self.far = (self.here + 2) % 4
+        self.send, self.recv, self.local = send, recv, local
+
+    def copy(self, k, src, dst, other):
+        return pltpu.make_async_remote_copy(
+            src_ref=src,
+            dst_ref=dst,
+            send_sem=self.send.at[k],
+            recv_sem=self.recv.at[k],
+            device_id={"dp": other},
+            device_id_type=MESH,
+        )
+
+
+class RingGather:
+    def __init__(self, ring, first, half_of, place):
+        self.plus_0 = ring.copy(first, half_of(0), place(ring.here, 0), ring.right)
+        self.minus_1 = ring.copy(first + 1, half_of(1), place(ring.here, 1), ring.left)
+        self.plus_1 = ring.copy(first + 2, half_of(1), place(ring.here, 1), ring.right)
+        self.minus_0 = ring.copy(first + 3, half_of(0), place(ring.here, 0), ring.left)
+        self.far_0 = ring.copy(first + 4, place(ring.left, 0), place(ring.left, 0), ring.right)
+        self.far_1 = ring.copy(first + 5, place(ring.right, 1), place(ring.right, 1), ring.left)
+        self.own = [
+            pltpu.make_async_copy(half_of(h), place(ring.here, h), ring.local.at[first + h])
+            for h in range(2)
+        ]
+        self.remote = (self.plus_0, self.minus_1, self.plus_1, self.minus_0, self.far_0, self.far_1)
+
+    def start(self):
+        for copy in self.remote[:4]:
+            copy.start()
+        for copy in self.own:
+            copy.start()
+
+    def forward(self):
+        self.plus_0.wait_recv()
+        self.far_0.start()
+        self.minus_1.wait_recv()
+        self.far_1.start()
+
+    def near(self):
+        self.plus_1.wait_recv()
+        self.minus_0.wait_recv()
+
+    def far(self):
+        self.far_0.wait_recv()
+        self.far_1.wait_recv()
+
+    def drain(self):
+        for copy in self.remote:
+            copy.wait_send()
+
+    def finish(self):
+        for copy in self.own:
+            copy.wait()
+        self.near()
+        self.far()
+        self.drain()
+
+
+class RingScatter:
+    def __init__(self, ring, first, half_at, buf, out):
+        self.buf, self.out = buf, out
+        self.plus_far = ring.copy(first, half_at(ring.far, 0), buf.at[0], ring.right)
+        self.minus_far = ring.copy(first + 1, half_at(ring.far, 1), buf.at[1], ring.left)
+        self.plus_near = ring.copy(first + 2, half_at(ring.right, 1), buf.at[2], ring.right)
+        self.minus_near = ring.copy(first + 3, half_at(ring.left, 0), buf.at[3], ring.left)
+        self.plus_sum = ring.copy(first + 4, buf.at[6], buf.at[4], ring.right)
+        self.minus_sum = ring.copy(first + 5, buf.at[7], buf.at[5], ring.left)
+        places = ((ring.right, 0), (ring.left, 1), (ring.here, 0), (ring.here, 1))
+        self.loads = [
+            pltpu.make_async_copy(half_at(*place), buf.at[6 + k], ring.local.at[first + k])
+            for k, place in enumerate(places)
+        ]
+        self.remote = (
+            self.plus_far,
+            self.minus_far,
+            self.plus_near,
+            self.minus_near,
+            self.plus_sum,
+            self.minus_sum,
+        )
+
+    def start(self):
+        for copy in self.remote[:4]:
+            copy.start()
+        for copy in self.loads:
+            copy.start()
+
+    def forward(self):
+        for copy in self.loads:
+            copy.wait()
+        self.plus_far.wait_recv()
+        for_rows(self.buf.shape[1:], lambda at: add_at(self.buf, 6, 0, at))
+        self.plus_sum.start()
+        self.minus_far.wait_recv()
+        for_rows(self.buf.shape[1:], lambda at: add_at(self.buf, 7, 1, at))
+        self.minus_sum.start()
+
+    def finish(self):
+        for copy in self.remote[2:]:
+            copy.wait_recv()
+        buf = self.buf
+        for half, terms in enumerate(((8, 3, 4), (9, 2, 5))):
+            out = self.out(half)
+
+            def total(at, out=out, terms=terms):
+                out[at] = sum(buf[(k,) + at].astype(F32) for k in terms)
+
+            for_rows(buf.shape[1:], total)
+        for copy in self.remote:
+            copy.wait_send()
+
+
+def add_at(buf, dst, src, at):
+    buf[(dst,) + at] = (buf[(dst,) + at].astype(F32) + buf[(src,) + at].astype(F32)).astype(BF16)
+
+
+def for_rows(shape, visit):
+    def step(i, carry):
+        rows = pl.ds(pl.multiple_of(i * 16, 16), 16)
+        if len(shape) == 2:
+            visit((rows, slice(None)))
+        else:
+            for j in range(shape[0]):
+                visit((j, rows, slice(None)))
+        return carry
+
+    lax.fori_loop(0, shape[-2] // 16, step, 0)
+
+
+def ring_sems(count):
+    return [pltpu.SemaphoreType.DMA((count,)) for _ in range(3)]
+
+
+def row_halves(depth):
+    half = depth // 2
+
+    def place(ref):
+        def at(owner, part):
+            return ref.at[:, pl.ds(pl.multiple_of(owner * depth + part * half, half), half), :]
+
+        return at
+
+    return place
+
+
+def plane_columns(depth):
+    def place(ref):
+        def at(owner, part):
+            return ref.at[part, :, pl.ds(pl.multiple_of(owner * depth, depth), depth)]
+
+        return at
+
+    return place
+
+
+def column_halves(depth):
+    def place(ref):
+        half = ref.shape[0] // 2
+
+        def at(owner, part):
+            columns = pl.ds(pl.multiple_of(owner * depth, depth), depth)
+            return ref.at[pl.ds(part * half, half), columns]
+
+        return at
+
+    return place
+
+
+def span_scatter(ring, first, ref, span, buf, out):
+    at = plane_columns(ref.shape[2] // 4)(ref.at[:, pl.ds(*span), :])
+    return RingScatter(ring, first, at, buf, lambda h: out.at[h])
+
+
+def each(items, name):
+    for item in items:
+        getattr(item, name)()
+
+
+def greet(others):
+    sem = pltpu.get_barrier_semaphore()
+    for other in others:
+        pl.semaphore_signal(sem, inc=1, device_id=other, device_id_type=MESH)
+    pl.semaphore_wait(sem, len(others))
 
 
 class Square:
@@ -406,11 +574,7 @@
         self.b = pl.ds(cut, rows - cut)
         self.na, self.nb, self.cut = cut, rows - cut, cut
 
-    def barrier(self):
-        sem = pltpu.get_barrier_semaphore()
-        for other in (self.xn, self.yn, self.peer):
-            pl.semaphore_signal(sem, inc=1, device_id={"mp": other}, device_id_type=MESH)
-        pl.semaphore_wait(sem, 3)
+        self.others = [{"mp": self.xn}, {"mp": self.yn}, {"mp": self.peer}]
 
     def copy(self, k, src, dst, other):
         return pltpu.make_async_remote_copy(
@@ -432,11 +596,36 @@
     lax.fori_loop(0, count // 16, step, 0)
 
 
-def square_kernel(rows, gather, scatter, compute, share, full, gbuf, pbuf, bufs, out, send, recv, lsem):
+def nothing():
+    pass
+
+
+def square_kernel(
+    rows,
+    sems,
+    gather=None,
+    scatter=None,
+    ring=None,
+    start=nothing,
+    first=nothing,
+    early=nothing,
+    later=nothing,
+    between=nothing,
+    middle=nothing,
+    end=nothing,
+):
+    send, recv, lsem = sems
     sq = Square(send, recv, rows)
     core = sq.core
-    sq.barrier()
-    if gather:
+    greet(sq.others + ([{"dp": ring.left}, {"dp": ring.right}] if ring is not None else []))
+
+    def place(rel, turn):
+        chip_y = (sq.y + rel % 2) % 2
+        chip_x = (sq.x + ((rel + 1) // 2) % 2) % 2
+        return chip_y * 2 + chip_x, (1 - core + turn) % 2
+
+    if gather is not None:
+        compute, share, full, gbuf = gather
         c_own = sq.copy(0, share, gbuf.at[sq.own, core], sq.peer)
         x_a = sq.copy(1, share.at[sq.a], gbuf.at[sq.own, core, sq.a], sq.xn)
         y_b = sq.copy(2, share.at[sq.b], gbuf.at[sq.own, core, sq.b], sq.yn)
@@ -452,29 +641,17 @@
         y_b.start()
         c_own.start()
         local.start()
-    if scatter:
-        rcore, rxd, ryd, rx, ry = bufs
-        x_d = sq.copy(14, pbuf.at[sq.dc, core, sq.a], rxd, sq.xn)
-        y_d = sq.copy(15, pbuf.at[sq.dc, core, sq.b], ryd, sq.yn)
-        x_ra = sq.copy(16, pbuf.at[sq.xc, core, sq.a], rx.at[sq.a], sq.xn)
-        y_rb = sq.copy(17, pbuf.at[sq.yc, core, sq.b], ry.at[sq.b], sq.yn)
-        x_rb = sq.copy(18, pbuf.at[sq.xc, core, sq.b], rx.at[sq.b], sq.xn)
-        y_ra = sq.copy(19, pbuf.at[sq.yc, core, sq.a], ry.at[sq.a], sq.yn)
-
-    def step(t, carry):
-        unit = t // 2
-        turn = t % 2
-        rel = unit if gather else (unit + 1) % 4
-        chip_y = (sq.y + rel % 2) % 2
-        chip_x = (sq.x + ((rel + 1) // 2) % 2) % 2
-        chip = chip_y * 2 + chip_x
-        which = (1 - core + turn) % 2
-        if gather:
+    start()
+    if gather is not None:
+
+        def gather_step(t, carry):
+            chip, which = place(t // 2, t % 2)
 
             @pl.when(t == 0)
             def _():
                 c_own.wait_recv()
                 local.wait()
+                first()
 
             @pl.when(t == 2)
             def _():
@@ -484,6 +661,7 @@
                 f_y.start()
                 x_b.start()
                 y_a.start()
+                early()
                 f_x.wait_recv()
                 f_y.wait_recv()
                 c_d.start()
@@ -495,46 +673,64 @@
                 y_a.wait_recv()
                 c_x.start()
                 c_y.start()
+                later()
                 c_x.wait_recv()
                 c_y.wait_recv()
 
-            if full is not None:
-                pltpu.make_async_copy(gbuf.at[chip, which], full.at[chip, which], lsem.at[t]).start()
-        compute(t, chip, which)
-        if scatter:
+            pltpu.make_async_copy(gbuf.at[chip, which], full.at[chip, which], lsem.at[t]).start()
+            compute(t, chip, which)
+            return carry
+
+        lax.fori_loop(0, 8, gather_step, 0)
+    between()
+    if scatter is not None:
+        finish_tile, pbuf, (rcore, rxd, ryd, rx, ry), out = scatter
+        x_d = sq.copy(14, pbuf.at[sq.dc, core, sq.a], rxd, sq.xn)
+        y_d = sq.copy(15, pbuf.at[sq.dc, core, sq.b], ryd, sq.yn)
+        x_ra = sq.copy(16, pbuf.at[sq.xc, core, sq.a], rx.at[sq.a], sq.xn)
+        y_rb = sq.copy(17, pbuf.at[sq.yc, core, sq.b], ry.at[sq.b], sq.yn)
+        x_rb = sq.copy(18, pbuf.at[sq.xc, core, sq.b], rx.at[sq.b], sq.xn)
+        y_ra = sq.copy(19, pbuf.at[sq.yc, core, sq.a], ry.at[sq.a], sq.yn)
+
+        def scatter_step(t, carry):
+            turn = t % 2
+            rel = (t // 2 + 1) % 4
+            chip, which = place(rel, turn)
+            finish_tile(t, chip, which)
+            to_peer = sq.copy(10 + rel, pbuf.at[chip, which], rcore.at[chip], sq.peer)
 
             @pl.when(turn == 0)
             def _():
-                sq.copy(10 + rel, pbuf.at[chip, which], rcore.at[chip], sq.peer).start()
+                to_peer.start()
 
             @pl.when(turn == 1)
             def _():
-                sq.copy(10 + rel, pbuf.at[chip, which], rcore.at[chip], sq.peer).wait_recv()
+                to_peer.wait_recv()
                 add_rows(pbuf.at[chip, which], rcore.at[chip], rows)
 
-            @pl.when((turn == 1) & (rel == 1))
+            @pl.when(t == 1)
             def _():
                 x_d.start()
                 y_d.start()
 
-            @pl.when((turn == 1) & (rel == 2))
+            @pl.when(t == 3)
             def _():
                 x_ra.start()
 
-            @pl.when((turn == 1) & (rel == 3))
+            @pl.when(t == 5)
             def _():
                 y_rb.start()
 
-        return carry
-
-    lax.fori_loop(0, 8, step, 0)
-    if scatter:
+            return carry
+
+        lax.fori_loop(0, 8, scatter_step, 0)
         x_d.wait_recv()
         add_rows(pbuf.at[sq.yc, core, sq.a], rxd, sq.na)
         y_ra.start()
         y_d.wait_recv()
         add_rows(pbuf.at[sq.xc, core, sq.b], ryd, sq.nb)
         x_rb.start()
+        middle()
         x_ra.wait_recv()
         y_rb.wait_recv()
         y_ra.wait_recv()
@@ -554,12 +750,12 @@
             sq.copy(10 + k, pbuf.at[0, 0], rcore.at[0], sq.peer).wait_send()
         for copy in (x_d, y_d, x_ra, y_rb, x_rb, y_ra):
             copy.wait_send()
-    if gather:
+    end()
+    if gather is not None:
         for copy in (c_own, x_a, y_b, f_x, f_y, x_b, y_a, c_d, c_x, c_y):
             copy.wait_send()
-        if full is not None:
-            for t in range(8):
-                pltpu.make_async_copy(gbuf.at[0, 0], full.at[0, 0], lsem.at[t]).wait()
+        for t in range(8):
+            pltpu.make_async_copy(gbuf.at[0, 0], full.at[0, 0], lsem.at[t]).wait()
 
 
 def scatter_scratch(rows, width):
@@ -587,110 +783,173 @@
     )
 
 
-def weight_copies(pieces, place, sem):
-    here = lax.axis_index("dp")
-    owners = (here, (here + 3) % 4, (here + 1) % 4, (here + 2) % 4)
-    copies = []
-    for k, piece in enumerate(pieces):
-        copies.append(pltpu.make_async_copy(piece, place(owners[k // 2], k % 2), sem.at[k]))
-    return copies
-
-
-def row_place(buf, depth):
-    half = depth // 2
-
-    def place(owner, part):
-        return buf.at[:, pl.ds(pl.multiple_of(owner * depth + part * half, half), half), :]
-
-    return place
-
-
-def plane_place(buf, depth):
-    def place(owner, part):
-        return buf.at[part, pl.ds(pl.multiple_of(owner * depth, depth), depth), :]
-
-    return place
-
-
-def column_place(buf, depth):
-    half = buf.shape[0] // 2
-
-    def place(owner, part):
-        return buf.at[pl.ds(part * half, half), pl.ds(pl.multiple_of(owner * depth, depth), depth)]
-
-    return place
-
-
-def qkv_call(block_input, pieces, cos_table, sin_table):
+def whole(shape):
+    return pl.BlockSpec(shape, lambda *_: (0,) * len(shape))
+
+
+def qkv_call(block_input, low_qkv, positions, rows):
     tokens, width = block_input.shape
-    cols = pieces[0].shape[2]
-    depth = pieces[0].shape[1] * 2
-    rows = 336
+    depth, cols = low_qkv.shape[1:]
+    tiles = tokens // rows
     heads = cols // HEAD_DIM
     scale = 1.0 / math.sqrt(HEAD_DIM)
-
-    def kernel(x_ref, cos_ref, sin_ref, *rest):
-        piece_refs, (q_ref, k_ref, v_ref, w_buf, sem) = rest[:8], rest[8:]
-
-        @pl.when(pl.program_id(0) == 0)
-        def _():
-            copies = weight_copies(piece_refs, row_place(w_buf, depth), sem)
-            for copy in copies:
-                copy.start()
-            for copy in copies:
-                copy.wait()
-
-        x = x_ref[...]
-        for j, ref in enumerate((q_ref, k_ref)):
-            a = jnp.dot(x, w_buf[j], preferred_element_type=F32)
-            for h in range(heads):
-                part = a[:, h * HEAD_DIM : (h + 1) * HEAD_DIM]
-                turned = part * cos_ref[...] + pltpu.roll(part, HEAD_DIM // 2, 1) * sin_ref[...]
-                if j == 0:
-                    turned = turned * scale
-                ref[:, h * HEAD_DIM : (h + 1) * HEAD_DIM] = turned.astype(BF16)
-        v_ref[...] = jnp.dot(x, w_buf[2], preferred_element_type=F32).astype(BF16)
-
-    tile = lambda n: pl.BlockSpec((rows, n), lambda i: (i, 0))
+    half = depth // 2
+
+    def kernel(
+        x_ref, low_ref, pos_ref, q_ref, k_ref, v_ref, cos_ref, sin_ref, w_ref,
+        x_buf, w_buf, acc, xsem, osem, send, recv, local,
+    ):
+        ring = Ring(send, recv, local)
+        gather = RingGather(
+            ring, 0, lambda h: low_ref.at[:, pl.ds(h * half, half), :], row_halves(depth)(w_buf)
+        )
+
+        def x_copy(t, k):
+            return pltpu.make_async_copy(
+                x_ref.at[t, :, pl.ds(k * depth, depth)], x_buf.at[t, k], xsem.at[t, k]
+            )
+
+        def start_tile(t, carry):
+            for k in range(4):
+                x_copy(t, k).start()
+            return carry
+
+        lax.fori_loop(0, tiles, start_tile, 0)
+        greet([{"dp": ring.left}, {"dp": ring.right}])
+        gather.start()
+        for copy in gather.own:
+            copy.wait()
+
+        def part(t, j, owner):
+            depths = pl.ds(pl.multiple_of(owner * depth, depth), depth)
+            return jnp.dot(x_buf[t, owner], w_buf[j, depths, :], preferred_element_type=F32)
+
+        def own_tile(t, carry):
+            for k in range(4):
+                x_copy(t, k).wait()
+            for j in range(3):
+                acc[t, j] = part(t, j, ring.here)
+            return carry
+
+        lax.fori_loop(0, tiles, own_tile, 0)
+        lane = lax.broadcasted_iota(jnp.int32, (1, HEAD_DIM), 1)
+        ladder = (lane % (HEAD_DIM // 2)).astype(F32)
+        inverse = jnp.exp(ladder * (-2.0 * math.log(10000.0) / HEAD_DIM))
+        sign = jnp.where(lane < HEAD_DIM // 2, -1.0, 1.0)
+
+        def table_tile(t, carry):
+            angles = pos_ref[t].astype(F32) * inverse
+            cos_ref[t] = jnp.cos(angles)
+            sin_ref[t] = jnp.sin(angles) * sign
+            return carry
+
+        lax.fori_loop(0, tiles // 2, table_tile, 0)
+        gather.forward()
+        lax.fori_loop(tiles // 2, tiles, table_tile, 0)
+        gather.near()
+
+        def near_tile(t, carry):
+            for j in range(3):
+                acc[t, j] += part(t, j, ring.left) + part(t, j, ring.right)
+            return carry
+
+        lax.fori_loop(0, tiles, near_tile, 0)
+        gather.far()
+        keep = pltpu.make_async_copy(w_buf, w_ref, osem.at[0])
+        keep.start()
+
+        def far_tile(t, carry):
+            for j, ref in enumerate((q_ref, k_ref)):
+                a = acc[t, j] + part(t, j, ring.far)
+                for h in range(heads):
+                    cut = slice(h * HEAD_DIM, (h + 1) * HEAD_DIM)
+                    turned = a[:, cut] * cos_ref[t] + pltpu.roll(a[:, cut], HEAD_DIM // 2, 1) * sin_ref[t]
+                    if j == 0:
+                        turned = turned * scale
+                    ref[t, :, cut] = turned.astype(BF16)
+            v_ref[t] = (acc[t, 2] + part(t, 2, ring.far)).astype(BF16)
+            return carry
+
+        lax.fori_loop(0, tiles, far_tile, 0)
+        keep.wait()
+        gather.drain()
+
+    tile = jax.ShapeDtypeStruct((tiles, rows, cols), BF16)
     return pl.pallas_call(
         kernel,
-        grid=(tokens // rows,),
-        out_shape=[jax.ShapeDtypeStruct((tokens, cols), BF16)] * 3,
-        in_specs=[tile(width), tile(HEAD_DIM), tile(HEAD_DIM)] + [ANY] * 8,
-        out_specs=[tile(cols)] * 3,
-        scratch_shapes=[pltpu.VMEM((3, width, cols), BF16), pltpu.SemaphoreType.DMA((8,))],
-        compiler_params=pltpu.CompilerParams(vmem_limit_bytes=VMEM_BYTES),
-        cost_estimate=pl.CostEstimate(
-            flops=6 * tokens * width * cols, bytes_accessed=20 << 20, transcendentals=0
-        ),
+        out_shape=[tile] * 3
+        + [jax.ShapeDtypeStruct((tiles, rows, HEAD_DIM), F32)] * 2
+        + [jax.ShapeDtypeStruct((3, width, cols), BF16)],
+        in_specs=[ANY, ANY, VM],
+        out_specs=[VM] * 5 + [ANY],
+        scratch_shapes=[
+            pltpu.VMEM((tiles, 4, rows, depth), BF16),
+            pltpu.VMEM((3, width, cols), BF16),
+            pltpu.VMEM((tiles, 3, rows, cols), F32),
+            pltpu.SemaphoreType.DMA((tiles, 4)),
+            pltpu.SemaphoreType.DMA((1,)),
+        ]
+        + ring_sems(6),
+        compiler_params=params(5),
+        cost_estimate=LIGHT,
         name="qkv",
-    )(block_input, cos_table, sin_table, *pieces)
+    )(
+        block_input.reshape(tiles, rows, width),
+        low_qkv,
+        positions.reshape(tiles, rows, 1),
+    )
 
 
 BLOCK = 128
 
 
-def attention_call(queries, key_rows, value_rows, prefix_len):
+def attention_call(queries, key_rows, value_rows, prefix_len, low_out, low_unit):
     tokens, cols = queries.shape
     proteins = tokens // LEN
     heads = cols // HEAD_DIM
-
-    def kernel(pre_ref, q_ref, k_ref, v_ref, o_ref, p_ref):
+    depth = low_out.shape[1]
+    last = proteins * heads - 1
+
+    def kernel(pre_ref, q_ref, k_ref, v_ref, lo_ref, lu_ref, o_ref, p_ref, wo_ref, wu_ref, send, recv, local):
         prefix = pre_ref[pl.program_id(0)]
-
-        def step(i, carry):
-            rows = pl.ds(pl.multiple_of(i * BLOCK, BLOCK), BLOCK)
+        step = pl.program_id(0) * heads + pl.program_id(1)
+        ring = Ring(send, recv, local)
+        half = lo_ref.shape[0] // 2
+        gathers = [
+            RingGather(ring, 0, lambda h: lo_ref.at[pl.ds(h * half, half), :], column_halves(depth)(wo_ref)),
+            RingGather(ring, 6, lambda h: lu_ref.at[h], plane_columns(depth)(wu_ref)),
+        ]
+
+        @pl.when(step == 0)
+        def _():
+            greet([{"dp": ring.left}, {"dp": ring.right}])
+            for gather in gathers:
+                gather.start()
+
+        for i in range(LEN // BLOCK):
+            rows = slice(i * BLOCK, (i + 1) * BLOCK)
             s = nt_dot(q_ref[rows, :], k_ref[...])
             col = lax.broadcasted_iota(jnp.int32, s.shape, 1)
-            row = lax.broadcasted_iota(jnp.int32, s.shape, 0) + i * BLOCK
+            row = lax.broadcasted_iota(jnp.int32, (BLOCK, 1), 0) + i * BLOCK
             s = jnp.where(col < jnp.maximum(prefix, row + 1), s, -1e30)
             e = jnp.exp(s - jnp.max(s, axis=-1, keepdims=True))
-            p = (e / jnp.sum(e, axis=-1, keepdims=True)).astype(BF16)
+            p = (e * (1.0 / jnp.sum(e, axis=-1, keepdims=True))).astype(BF16)
             p_ref[0, 0, rows, :] = p
             o_ref[rows, :] = jnp.dot(p, v_ref[...], preferred_element_type=F32).astype(BF16)
-            return carry
-
-        lax.fori_loop(0, LEN // BLOCK, step, 0)
+
+        @pl.when(step == last // 2)
+        def _():
+            for gather in gathers:
+                gather.forward()
+
+        @pl.when(step == last)
+        def _():
+            for gather in gathers:
+                for copy in gather.own:
+                    copy.wait()
+                gather.near()
+                gather.far()
+                gather.drain()
 
     tile = pl.BlockSpec((LEN, HEAD_DIM), lambda p, h, *_: (p, h))
     return pl.pallas_call(
@@ -698,51 +957,112 @@
         grid_spec=pltpu.PrefetchScalarGridSpec(
             num_scalar_prefetch=1,
             grid=(proteins, heads),
-            in_specs=[tile] * 3,
-            out_specs=[tile, pl.BlockSpec((1, 1, LEN, LEN), lambda p, h, *_: (p, h, 0, 0))],
+            in_specs=[tile] * 3 + [ANY, ANY],
+            out_specs=[tile, pl.BlockSpec((1, 1, LEN, LEN), lambda p, h, *_: (p, h, 0, 0)), ANY, ANY],
+            scratch_shapes=ring_sems(12),
         ),
         out_shape=[
             jax.ShapeDtypeStruct((tokens, cols), BF16),
             jax.ShapeDtypeStruct((proteins, heads, LEN, LEN), BF16),
+            jax.ShapeDtypeStruct((low_out.shape[0], 4 * depth), BF16),
+            jax.ShapeDtypeStruct(low_unit.shape[:2] + (4 * depth,), BF16),
         ],
-        compiler_params=pltpu.CompilerParams(vmem_limit_bytes=VMEM_BYTES),
-        cost_estimate=pl.CostEstimate(
-            flops=4 * tokens * LEN * cols, bytes_accessed=16 << 20, transcendentals=tokens * LEN * heads
-        ),
+        compiler_params=params(6),
+        cost_estimate=LIGHT,
         name="attention",
-    )(prefix_len, queries, key_rows, value_rows)
-
-
-def attention_back_call(queries, key_rows, value_rows, probs, attended, grad_attended, cos_table, sin_table):
+    )(prefix_len, queries, key_rows, value_rows, low_out, low_unit)
+
+
+TN = (((0,), (0,)), ((), ()))
+
+
+def attention_back_call(
+    queries, key_rows, value_rows, probs, attended, grad_attended, cos_table, sin_table, norm_terms,
+    grad_gateup_part, span,
+):
     tokens, cols = queries.shape
     proteins = tokens // LEN
     heads = cols // HEAD_DIM
     scale = 1.0 / math.sqrt(HEAD_DIM)
-    TN = (((0,), (0,)), ((), ()))
-
-    def kernel(q_ref, k_ref, v_ref, p_ref, o_ref, do_ref, cos_ref, sin_ref, da_ref, dk_acc, dv_acc):
-        dk_acc[...] = jnp.zeros_like(dk_acc)
-        dv_acc[...] = jnp.zeros_like(dv_acc)
-
-        def step(i, carry):
-            rows = pl.ds(pl.multiple_of(i * BLOCK, BLOCK), BLOCK)
+    last = proteins * heads - 1
+    depth = grad_gateup_part.shape[2] // 4
+
+    def kernel(
+        q_ref, k_ref, v_ref, p_ref, o_ref, do_ref, cos_ref, sin_ref, nt_ref, gg_ref,
+        da_ref, norm_ref, red_ref,
+        dk_acc, dv_acc, sums, got, nsend, nrecv, buf, send, recv, local,
+    ):
+        step = pl.program_id(0) * heads + pl.program_id(1)
+        ring = Ring(send, recv, local)
+        side = span_scatter(ring, 0, gg_ref, span, buf, red_ref)
+        sq = Square(nsend, nrecv, 32)
+        partners = [
+            {"mp": sq.peer},
+            {"mp": sq.xn},
+            {"mp": sq.yn},
+            {"dp": ring.here + 1 - 2 * (ring.here % 2)},
+            {"dp": 3 - ring.here},
+        ]
+        swaps = [
+            pltpu.make_async_remote_copy(
+                src_ref=sums.at[k],
+                dst_ref=got.at[k],
+                send_sem=nsend.at[k],
+                recv_sem=nrecv.at[k],
+                device_id=other,
+                device_id_type=MESH,
+            )
+            for k, other in enumerate(partners)
+        ]
+
+        @pl.when(step == 0)
+        def _():
+            sums[0] = nt_ref[...]
+            greet(sq.others + [{"dp": ring.left}, {"dp": ring.right}])
+            side.start()
+            swaps[0].start()
+
+        for k in range(5):
+
+            @pl.when(step == k + 1)
+            def _():
+                swaps[k].wait()
+                if k < 4:
+                    sums[k + 1] = sums[k] + got[k]
+                    swaps[k + 1].start()
+                else:
+                    norm_ref[...] = sums[k] + got[k]
+
+        @pl.when(step == last // 2)
+        def _():
+            side.forward()
+
+        for i in range(LEN // BLOCK):
+            rows = slice(i * BLOCK, (i + 1) * BLOCK)
             do = do_ref[rows, :]
             p = p_ref[0, 0, rows, :]
             delta = jnp.sum(do.astype(F32) * o_ref[rows, :].astype(F32), axis=-1, keepdims=True)
             dp = nt_dot(do, v_ref[...])
             ds = (p.astype(F32) * (dp - delta)).astype(BF16)
-            dv_acc[...] += lax.dot_general(p, do, TN, preferred_element_type=F32)
-            dk_acc[...] += lax.dot_general(ds, q_ref[rows, :], TN, preferred_element_type=F32)
+            dv = lax.dot_general(p, do, TN, preferred_element_type=F32)
+            dk = lax.dot_general(ds, q_ref[rows, :], TN, preferred_element_type=F32)
+            if i == 0:
+                dv_acc[...] = dv
+                dk_acc[...] = dk
+            else:
+                dv_acc[...] += dv
+                dk_acc[...] += dk
             dq = jnp.dot(ds, k_ref[...], preferred_element_type=F32)
             turned = dq * cos_ref[rows, :] - pltpu.roll(dq, HEAD_DIM // 2, 1) * sin_ref[rows, :]
             da_ref[0, rows, :] = (turned * scale).astype(BF16)
-            return carry
-
-        lax.fori_loop(0, LEN // BLOCK, step, 0)
         dk = dk_acc[...]
         turned = dk * cos_ref[...] - pltpu.roll(dk, HEAD_DIM // 2, 1) * sin_ref[...]
         da_ref[1] = turned.astype(BF16)
         da_ref[2] = dv_acc[...].astype(BF16)
+
+        @pl.when(step == last)
+        def _():
+            side.finish()
 
     tile = pl.BlockSpec((LEN, HEAD_DIM), lambda p, h: (p, h))
     table = pl.BlockSpec((LEN, HEAD_DIM), lambda p, h: (p, 0))
@@ -750,76 +1070,162 @@
         kernel,
         grid=(proteins, heads),
         in_specs=[tile] * 3
-        + [pl.BlockSpec((1, 1, LEN, LEN), lambda p, h: (p, h, 0, 0)), tile, tile, table, table],
-        out_specs=pl.BlockSpec((3, LEN, HEAD_DIM), lambda p, h: (0, p, h)),
-        out_shape=jax.ShapeDtypeStruct((3, tokens, cols), BF16),
-        scratch_shapes=[pltpu.VMEM((LEN, HEAD_DIM), F32), pltpu.VMEM((LEN, HEAD_DIM), F32)],
-        compiler_params=pltpu.CompilerParams(vmem_limit_bytes=VMEM_BYTES),
-        cost_estimate=pl.CostEstimate(
-            flops=8 * tokens * LEN * cols, bytes_accessed=20 << 20, transcendentals=0
-        ),
+        + [pl.BlockSpec((1, 1, LEN, LEN), lambda p, h: (p, h, 0, 0)), tile, tile, table, table]
+        + [whole(norm_terms.shape), ANY],
+        out_specs=[
+            pl.BlockSpec((3, LEN, HEAD_DIM), lambda p, h: (0, p, h)),
+            whole(norm_terms.shape),
+            whole((2, span[1], depth)),
+        ],
+        out_shape=[
+            jax.ShapeDtypeStruct((3, tokens, cols), BF16),
+            jax.ShapeDtypeStruct(norm_terms.shape, F32),
+            jax.ShapeDtypeStruct((2, span[1], depth), F32),
+        ],
+        scratch_shapes=[
+            pltpu.VMEM((LEN, HEAD_DIM), F32),
+            pltpu.VMEM((LEN, HEAD_DIM), F32),
+            pltpu.VMEM((5,) + norm_terms.shape, F32),
+            pltpu.VMEM((5,) + norm_terms.shape, F32),
+            pltpu.SemaphoreType.DMA((5,)),
+            pltpu.SemaphoreType.DMA((5,)),
+            pltpu.VMEM((10, span[1], depth), BF16),
+        ]
+        + ring_sems(6),
+        compiler_params=params(7),
+        cost_estimate=LIGHT,
         name="attention_back",
-    )(queries, key_rows, value_rows, probs, attended, grad_attended, cos_table, sin_table)
-
-
-def out_call(attended, pieces, rows):
+    )(
+        queries,
+        key_rows,
+        value_rows,
+        probs,
+        attended,
+        grad_attended,
+        cos_table,
+        sin_table,
+        norm_terms,
+        grad_gateup_part,
+    )
+
+
+def out_call(attended, w_out, low_units, rows):
     cols = attended.shape[1]
-    depth = pieces[0].shape[1]
-
-    def kernel(o_ref, *rest):
-        piece_refs, (out, w_buf, pbuf, rcore, rxd, ryd, rx, ry, wsem, send, recv, lsem) = rest[:8], rest[8:]
-        copies = weight_copies(piece_refs, column_place(w_buf, depth), wsem)
-        for copy in copies:
-            copy.start()
-        for copy in copies:
-            copy.wait()
+    count = len(low_units)
+    depth = low_units[0].shape[2]
+
+    def kernel(o_ref, w_ref, *rest):
+        low_refs, (out, *unit_refs), rest = rest[:count], rest[count : 2 * count + 1], rest[2 * count + 1 :]
+        w_buf, pbuf, rcore, rxd, ryd, rx, ry, wsem, send, recv, lsem, zsend, zrecv, zlocal = rest
+        ring = Ring(zsend, zrecv, zlocal)
+        gathers = [
+            RingGather(ring, 6 * k, lambda h, low=low: low.at[h], plane_columns(depth)(unit))
+            for k, (low, unit) in enumerate(zip(low_refs, unit_refs))
+        ]
+        weight = pltpu.make_async_copy(w_ref, w_buf, wsem.at[0])
+        weight.start()
+
+        def start():
+            gathers[0].start()
+            weight.wait()
+
+        def between():
+            gathers[0].forward()
+            for gather in gathers[1:]:
+                gather.start()
+
+        def middle():
+            for gather in gathers[1:]:
+                gather.forward()
+
+        def end():
+            for gather in gathers:
+                gather.finish()
 
         def compute(t, chip, which):
             part = jnp.dot(o_ref[chip, which], w_buf[...], preferred_element_type=F32)
             pbuf[chip, which] = part.astype(BF16)
 
         square_kernel(
-            rows, False, True, compute, None, None, None, pbuf, (rcore, rxd, ryd, rx, ry), out, send, recv, lsem
+            rows,
+            (send, recv, lsem),
+            scatter=(compute, pbuf, (rcore, rxd, ryd, rx, ry), out),
+            ring=ring,
+            start=start,
+            between=nothing,
+            middle=lambda: (between(), middle()),
+            end=end,
         )
 
     return pl.pallas_call(
         kernel,
-        out_shape=jax.ShapeDtypeStruct((rows, D), F32),
-        in_specs=[VM] + [ANY] * 8,
-        out_specs=VM,
+        out_shape=[jax.ShapeDtypeStruct((rows, D), F32)]
+        + [jax.ShapeDtypeStruct(low.shape[:2] + (D,), BF16) for low in low_units],
+        in_specs=[VM, ANY] + [ANY] * count,
+        out_specs=[VM] + [ANY] * count,
         scratch_shapes=[pltpu.VMEM((cols, D), BF16)]
         + scatter_scratch(rows, D)
-        + [pltpu.SemaphoreType.DMA((8,))]
-        + SEMS,
+        + [pltpu.SemaphoreType.DMA((1,))]
+        + SEMS
+        + ring_sems(6 * count),
         compiler_params=params(0),
-        cost_estimate=pl.CostEstimate(flops=40 << 30, bytes_accessed=100 << 20, transcendentals=0),
+        cost_estimate=LIGHT,
         name="out_reduce",
-    )(attended.reshape(4, 2, rows, cols), *pieces)
-
-
-def ffn_call(middle_low, gateup_pieces, down_pieces):
+    )(attended.reshape(4, 2, rows, cols), w_out, *low_units)
+
+
+def ffn_call(middle_low, units, low_unit, low_down):
     rows = middle_low.shape[0]
-    live = gateup_pieces[0].shape[-1]
-    depth = gateup_pieces[0].shape[0]
+    live, depth = low_down.shape
+    count = len(units)
+    rest_rows = low_unit.shape[1]
     curve = math.sqrt(2.0 / math.pi)
 
-    def kernel(share, *rest):
-        g_refs, d_refs = rest[:8], rest[8:16]
-        (out, full, hid_ref, act_ref, pull_ref) = rest[16:21]
-        (w_g, w_d, gbuf, stage, pbuf, rcore, rxd, ryd, rx, ry, gsem, dsem, osem, send, recv, lsem) = rest[21:]
-        copies = weight_copies(g_refs, plane_place(w_g, depth), gsem)
-        copies += weight_copies(d_refs, column_place(w_d, depth), dsem)
+    def kernel(share, lu_ref, ld_ref, *rest):
+        unit_refs, rest = rest[:count], rest[count:]
+        out, full, hid_ref, act_ref, pull_ref, wg_ref, wd_ref = rest[:7]
+        (w_g, w_d, gbuf, hid_buf, stage, pbuf, rcore, rxd, ryd, rx, ry) = rest[7:18]
+        wsem, osem, hsem, send, recv, lsem, zsend, zrecv, zlocal = rest[18:]
+        ring = Ring(zsend, zrecv, zlocal)
+        tail = w_g.at[:, pl.ds(live - rest_rows, rest_rows), :]
+        gather_g = RingGather(ring, 0, lambda h: lu_ref.at[h], plane_columns(depth)(tail))
+        half = live // 2
+        gather_d = RingGather(ring, 6, lambda h: ld_ref.at[pl.ds(h * half, half), :], column_halves(depth)(w_d))
+        copies = []
+        offset = 0
+        for k, ref in enumerate(unit_refs):
+            size = ref.shape[1]
+            copies.append(pltpu.make_async_copy(ref, w_g.at[:, pl.ds(offset, size), :], wsem.at[k]))
+            offset += size
         for copy in copies:
             copy.start()
-        outs = (hid_ref, act_ref, pull_ref)
+        keep_g = pltpu.make_async_copy(w_g, wg_ref, wsem.at[count])
+        keep_d = pltpu.make_async_copy(w_d, wd_ref, wsem.at[count + 1])
+        outs = (act_ref, pull_ref)
+
+        def first():
+            gather_g.forward()
+            gather_d.start()
+            for copy in copies:
+                copy.wait()
+            for copy in gather_g.own:
+                copy.wait()
+            gather_g.near()
+            gather_g.far()
+            keep_g.start()
+
+        def later():
+            gather_d.forward()
+
+        def between():
+            for copy in gather_d.own:
+                copy.wait()
+            gather_d.near()
+            gather_d.far()
+            keep_d.start()
 
         def compute(t, chip, which):
             slot = t % 2
-
-            @pl.when(t == 0)
-            def _():
-                for copy in copies:
-                    copy.wait()
 
             @pl.when(t >= 2)
             def _():
@@ -827,27 +1233,47 @@
                     pltpu.make_async_copy(stage.at[slot, k], ref.at[chip, which], osem.at[slot, k]).wait()
 
             tile = gbuf[chip, which]
-            gate = jnp.dot(tile, w_g[0], preferred_element_type=F32)
-            up = jnp.dot(tile, w_g[1], preferred_element_type=F32)
+            gate = nt_dot(tile, w_g[0])
+            up = nt_dot(tile, w_g[1])
             square = gate * gate
             bent = jnp.tanh(curve * gate * (1.0 + 0.044715 * square))
             half = 0.5 * (1.0 + bent)
             act = gate * half
             slope = half + 0.5 * curve * gate * (1.0 - bent * bent) * (1.0 + 3.0 * 0.044715 * square)
-            hid = (act * up).astype(BF16)
-            stage[slot, 0] = hid
-            stage[slot, 1] = act.astype(BF16)
-            stage[slot, 2] = (slope * up).astype(BF16)
+            hid_buf[chip, which] = (act * up).astype(BF16)
+            stage[slot, 0] = act.astype(BF16)
+            stage[slot, 1] = (slope * up).astype(BF16)
             for k, ref in enumerate(outs):
                 pltpu.make_async_copy(stage.at[slot, k], ref.at[chip, which], osem.at[slot, k]).start()
-            pbuf[chip, which] = jnp.dot(hid, w_d[...], preferred_element_type=F32).astype(BF16)
+            pltpu.make_async_copy(hid_buf.at[chip, which], hid_ref.at[chip, which], hsem.at[t]).start()
+
+        def finish_tile(t, chip, which):
+            part = jnp.dot(hid_buf[chip, which], w_d[...], preferred_element_type=F32)
+            pbuf[chip, which] = part.astype(BF16)
+
+        def end():
+            for slot in range(2):
+                for k, ref in enumerate(outs):
+                    pltpu.make_async_copy(stage.at[slot, k], ref.at[0, 0], osem.at[slot, k]).wait()
+            for t in range(8):
+                pltpu.make_async_copy(hid_buf.at[0, 0], hid_ref.at[0, 0], hsem.at[t]).wait()
+            keep_g.wait()
+            keep_d.wait()
+            gather_g.drain()
+            gather_d.drain()
 
         square_kernel(
-            rows, True, True, compute, share, full, gbuf, pbuf, (rcore, rxd, ryd, rx, ry), out, send, recv, lsem
+            rows,
+            (send, recv, lsem),
+            gather=(compute, share, full, gbuf),
+            scatter=(finish_tile, pbuf, (rcore, rxd, ryd, rx, ry), out),
+            ring=ring,
+            start=gather_g.start,
+            first=first,
+            later=later,
+            between=between,
+            end=end,
         )
-        for slot in range(2):
-            for k, ref in enumerate(outs):
-                pltpu.make_async_copy(stage.at[slot, k], ref.at[0, 0], osem.at[slot, k]).wait()
 
     kept = jax.ShapeDtypeStruct((4, 2, rows, live), BF16)
     return pl.pallas_call(
@@ -858,48 +1284,42 @@
             kept,
             kept,
             kept,
+            jax.ShapeDtypeStruct((2, live, D), BF16),
+            jax.ShapeDtypeStruct((live, D), BF16),
         ],
-        in_specs=[ANY] * 17,
-        out_specs=[VM, ANY, ANY, ANY, ANY],
+        in_specs=[ANY] * (3 + count),
+        out_specs=[VM] + [ANY] * 6,
         scratch_shapes=[
-            pltpu.VMEM((2, D, live), BF16),
+            pltpu.VMEM((2, live, D), BF16),
             pltpu.VMEM((live, D), BF16),
             pltpu.VMEM((4, 2, rows, D), BF16),
-            pltpu.VMEM((2, 3, rows, live), BF16),
+            pltpu.VMEM((4, 2, rows, live), BF16),
+            pltpu.VMEM((2, 2, rows, live), BF16),
         ]
         + scatter_scratch(rows, D)
-        + [pltpu.SemaphoreType.DMA((8,)), pltpu.SemaphoreType.DMA((8,)), pltpu.SemaphoreType.DMA((2, 3))]
-        + SEMS,
+        + [
+            pltpu.SemaphoreType.DMA((count + 2,)),
+            pltpu.SemaphoreType.DMA((2, 2)),
+            pltpu.SemaphoreType.DMA((8,)),
+        ]
+        + SEMS
+        + ring_sems(12),
         compiler_params=params(1),
-        cost_estimate=pl.CostEstimate(flops=100 << 30, bytes_accessed=300 << 20, transcendentals=0),
+        cost_estimate=LIGHT,
         name="ffn",
-    )(middle_low, *gateup_pieces, *down_pieces)
-
-
-def ffn_back_call(ffn_grad, act, pull, gateup_pieces, down_pieces):
+    )(middle_low, low_unit, low_down, *units)
+
+
+def ffn_back_call(ffn_grad, act, pull, w_down):
     rows = ffn_grad.shape[0]
-    live = gateup_pieces[0].shape[-1]
-    depth = gateup_pieces[0].shape[0]
-
-    def kernel(share, act_ref, pull_ref, *rest):
-        g_refs, d_refs = rest[:8], rest[8:16]
-        (out, full, dg_ref) = rest[16:19]
-        (w_g, w_d, gbuf, load, stage, pbuf, rcore, rxd, ryd, rx, ry, gsem, dsem, isem, osem, send, recv, lsem) = rest[
-            19:
-        ]
-        copies = weight_copies(g_refs, plane_place(w_g, depth), gsem)
-        copies += weight_copies(d_refs, column_place(w_d, depth), dsem)
-        for copy in copies:
-            copy.start()
+    live = w_down.shape[0]
+
+    def kernel(share, act_ref, pull_ref, wd_ref, full, dg_ref, w_d, gbuf, load, stage, wsem, isem, osem, send, recv, lsem):
+        weight = pltpu.make_async_copy(wd_ref, w_d, wsem.at[0])
+        weight.start()
 
         def compute(t, chip, which):
             slot = t % 2
-
-            @pl.when(t == 0)
-            def _():
-                for copy in copies:
-                    copy.wait()
-
             loads = [
                 pltpu.make_async_copy(ref.at[chip, which], load.at[k], isem.at[k])
                 for k, ref in enumerate((act_ref, pull_ref))
@@ -919,100 +1339,198 @@
             dh = nt_dot(gbuf[chip, which], w_d[...])
             for copy in loads:
                 copy.wait()
-            d_gate = (dh * load[1].astype(F32)).astype(BF16)
-            d_up = (dh * load[0].astype(F32)).astype(BF16)
-            stage[slot, 0] = d_gate
-            stage[slot, 1] = d_up
+            stage[slot, 0] = (dh * load[1].astype(F32)).astype(BF16)
+            stage[slot, 1] = (dh * load[0].astype(F32)).astype(BF16)
             for copy in stores:
                 copy.start()
-            pbuf[chip, which] = (nt_dot(d_gate, w_g[0]) + nt_dot(d_up, w_g[1])).astype(BF16)
+
+        def end():
+            for slot in range(2):
+                for k in range(2):
+                    pltpu.make_async_copy(stage.at[slot, k], dg_ref.at[k, 0, 0], osem.at[slot, k]).wait()
 
         square_kernel(
-            rows, True, True, compute, share, full, gbuf, pbuf, (rcore, rxd, ryd, rx, ry), out, send, recv, lsem
+            rows, (send, recv, lsem), gather=(compute, share, full, gbuf), first=weight.wait, end=end
         )
-        for slot in range(2):
-            for k in range(2):
-                pltpu.make_async_copy(stage.at[slot, k], dg_ref.at[k, 0, 0], osem.at[slot, k]).wait()
 
     return pl.pallas_call(
         kernel,
         out_shape=[
-            jax.ShapeDtypeStruct((rows, D), F32),
             jax.ShapeDtypeStruct((4, 2, rows, D), BF16),
             jax.ShapeDtypeStruct((2, 4, 2, rows, live), BF16),
         ],
-        in_specs=[ANY] * 19,
-        out_specs=[VM, ANY, ANY],
+        in_specs=[ANY] * 4,
+        out_specs=[ANY, ANY],
         scratch_shapes=[
-            pltpu.VMEM((2, D, live), BF16),
             pltpu.VMEM((live, D), BF16),
             pltpu.VMEM((4, 2, rows, D), BF16),
             pltpu.VMEM((2, rows, live), BF16),
             pltpu.VMEM((2, 2, rows, live), BF16),
-        ]
-        + scatter_scratch(rows, D)
-        + [
-            pltpu.SemaphoreType.DMA((8,)),
-            pltpu.SemaphoreType.DMA((8,)),
+            pltpu.SemaphoreType.DMA((1,)),
             pltpu.SemaphoreType.DMA((2,)),
             pltpu.SemaphoreType.DMA((2, 2)),
         ]
         + SEMS,
         compiler_params=params(2),
-        cost_estimate=pl.CostEstimate(flops=100 << 30, bytes_accessed=300 << 20, transcendentals=0),
+        cost_estimate=LIGHT,
         name="ffn_back",
-    )(ffn_grad, act, pull, *gateup_pieces, *down_pieces)
-
-
-def out_back_call(attn_grad, pieces):
+    )(ffn_grad, act, pull, w_down)
+
+
+def middle_back_call(grad_gateup_rows, w_gateup, grad_down_part, grad_gateup_part, span, rows):
+    live, width = grad_down_part.shape
+    depth = width // 4
+
+    def kernel(
+        dg_ref, wg_ref, gd_ref, gg_ref, out, red_d, red_g,
+        w_g, load, buf_d, buf_g, pbuf, rcore, rxd, ryd, rx, ry, wsem, isem, send, recv, lsem, zsend, zrecv, zlocal,
+    ):
+        ring = Ring(zsend, zrecv, zlocal)
+        half = live // 2
+        sides = (
+            RingScatter(ring, 0, column_halves(depth)(gd_ref), buf_d, lambda h: red_d.at[pl.ds(h * half, half), :]),
+            span_scatter(ring, 6, gg_ref, span, buf_g, red_g),
+        )
+        weight = pltpu.make_async_copy(wg_ref, w_g, wsem.at[0])
+        weight.start()
+        me = lax.axis_index("mp")
+        core, x, y = me % 2, (me // 2) % 2, me // 4
+
+        def loads(t):
+            rel = (t // 2 + 1) % 4
+            chip = ((y + rel % 2) % 2) * 2 + (x + ((rel + 1) // 2) % 2) % 2
+            which = (1 - core + t % 2) % 2
+            return [
+                pltpu.make_async_copy(dg_ref.at[k, chip, which], load.at[t % 2, k], isem.at[t % 2, k])
+                for k in range(2)
+            ]
+
+        for copy in loads(0):
+            copy.start()
+
+        def compute(t, chip, which):
+            @pl.when(t < 7)
+            def _():
+                for copy in loads(t + 1):
+                    copy.start()
+
+            for copy in loads(t):
+                copy.wait()
+            slot = t % 2
+            part = jnp.dot(load[slot, 0], w_g[0], preferred_element_type=F32)
+            part += jnp.dot(load[slot, 1], w_g[1], preferred_element_type=F32)
+            pbuf[chip, which] = part.astype(BF16)
+
+        square_kernel(
+            rows,
+            (send, recv, lsem),
+            scatter=(compute, pbuf, (rcore, rxd, ryd, rx, ry), out),
+            ring=ring,
+            start=lambda: (each(sides, "start"), weight.wait()),
+            middle=lambda: each(sides, "forward"),
+            end=lambda: each(sides, "finish"),
+        )
+
+    return pl.pallas_call(
+        kernel,
+        out_shape=[
+            jax.ShapeDtypeStruct((rows, D), F32),
+            jax.ShapeDtypeStruct((live, depth), F32),
+            jax.ShapeDtypeStruct((2, span[1], depth), F32),
+        ],
+        in_specs=[ANY] * 4,
+        out_specs=[VM] * 3,
+        scratch_shapes=[
+            pltpu.VMEM((2, live, D), BF16),
+            pltpu.VMEM((2, 2, rows, live), BF16),
+            pltpu.VMEM((10, live // 2, depth), BF16),
+            pltpu.VMEM((10, span[1], depth), BF16),
+        ]
+        + scatter_scratch(rows, D)
+        + [pltpu.SemaphoreType.DMA((1,)), pltpu.SemaphoreType.DMA((2, 2))]
+        + SEMS
+        + ring_sems(12),
+        compiler_params=params(8),
+        cost_estimate=LIGHT,
+        name="middle_back",
+    )(grad_gateup_rows, w_gateup, grad_down_part, grad_gateup_part)
+
+
+def out_back_call(attn_grad, w_out, grad_gateup_part, span):
     rows = attn_grad.shape[0]
-    cols = pieces[0].shape[0] * 2
-    depth = pieces[0].shape[1]
-
-    def kernel(share, *rest):
-        piece_refs, (full, dout, w_buf, gbuf, wsem, send, recv, lsem) = rest[:8], rest[8:]
-        copies = weight_copies(piece_refs, column_place(w_buf, depth), wsem)
-        for copy in copies:
-            copy.start()
-        for copy in copies:
-            copy.wait()
+    cols = w_out.shape[0]
+    depth = grad_gateup_part.shape[2] // 4
+
+    def kernel(
+        share, w_ref, gg_ref, full, dout, red, w_buf, gbuf, buf, wsem, send, recv, lsem, zsend, zrecv, zlocal
+    ):
+        ring = Ring(zsend, zrecv, zlocal)
+        side = span_scatter(ring, 0, gg_ref, span, buf, red)
+        weight = pltpu.make_async_copy(w_ref, w_buf, wsem.at[0])
+        weight.start()
 
         def compute(t, chip, which):
             dout[chip, which] = nt_dot(gbuf[chip, which], w_buf[...]).astype(BF16)
 
-        square_kernel(rows, True, False, compute, share, full, gbuf, None, None, None, send, recv, lsem)
+        square_kernel(
+            rows,
+            (send, recv, lsem),
+            gather=(compute, share, full, gbuf),
+            ring=ring,
+            start=side.start,
+            first=weight.wait,
+            early=side.forward,
+            end=side.finish,
+        )
 
     return pl.pallas_call(
         kernel,
         out_shape=[
             jax.ShapeDtypeStruct((4, 2, rows, D), BF16),
             jax.ShapeDtypeStruct((4, 2, rows, cols), BF16),
+            jax.ShapeDtypeStruct((2, span[1], depth), F32),
         ],
-        in_specs=[ANY] * 9,
-        out_specs=[ANY, VM],
+        in_specs=[ANY] * 3,
+        out_specs=[ANY, VM, VM],
         scratch_shapes=[
             pltpu.VMEM((cols, D), BF16),
             pltpu.VMEM((4, 2, rows, D), BF16),
-            pltpu.SemaphoreType.DMA((8,)),
+            pltpu.VMEM((10, span[1], depth), BF16),
+            pltpu.SemaphoreType.DMA((1,)),
         ]
-        + SEMS,
+        + SEMS
+        + ring_sems(6),
         compiler_params=params(3),
-        cost_estimate=pl.CostEstimate(flops=40 << 30, bytes_accessed=100 << 20, transcendentals=0),
+        cost_estimate=LIGHT,
         name="out_back",
-    )(attn_grad, *pieces)
-
-
-def input_back_call(grad_proj, pieces, rows):
-    cols = grad_proj.shape[2]
-    depth = pieces[0].shape[1] * 2
-
-    def kernel(da_ref, *rest):
-        piece_refs, (out, w_buf, pbuf, rcore, rxd, ryd, rx, ry, wsem, send, recv, lsem) = rest[:8], rest[8:]
-        copies = weight_copies(piece_refs, row_place(w_buf, depth), wsem)
-        for copy in copies:
-            copy.start()
-        for copy in copies:
-            copy.wait()
+    )(attn_grad, w_out, grad_gateup_part)
+
+
+def input_back_call(grad_proj, w_qkv, grad_qkv_part, grad_out_part, rows):
+    width, cols = w_qkv.shape[1:]
+    depth = width // 4
+
+    def kernel(
+        da_ref, w_ref, gq_ref, go_ref, out, red_q, red_o,
+        w_buf, buf_q, buf_o, pbuf, rcore, rxd, ryd, rx, ry, wsem, send, recv, lsem, zsend, zrecv, zlocal,
+    ):
+        ring = Ring(zsend, zrecv, zlocal)
+        half = depth // 2
+        part = cols // 2
+        sides = (
+            RingScatter(
+                ring, 0, row_halves(depth)(gq_ref), buf_q, lambda h: red_q.at[:, pl.ds(h * half, half), :]
+            ),
+            RingScatter(
+                ring, 6, column_halves(depth)(go_ref), buf_o, lambda h: red_o.at[pl.ds(h * part, part), :]
+            ),
+        )
+        weight = pltpu.make_async_copy(w_ref, w_buf, wsem.at[0])
+        weight.start()
+
+        def start():
+            each(sides, "start")
+            weight.wait()
 
         def compute(t, chip, which):
             part = nt_dot(da_ref[0, chip, which], w_buf[0])
@@ -1021,22 +1539,40 @@
             pbuf[chip, which] = part.astype(BF16)
 
         square_kernel(
-            rows, False, True, compute, None, None, None, pbuf, (rcore, rxd, ryd, rx, ry), out, send, recv, lsem
+            rows,
+            (send, recv, lsem),
+            scatter=(compute, pbuf, (rcore, rxd, ryd, rx, ry), out),
+            ring=ring,
+            start=start,
+            middle=lambda: each(sides, "forward"),
+            end=lambda: each(sides, "finish"),
         )
 
     return pl.pallas_call(
         kernel,
-        out_shape=jax.ShapeDtypeStruct((rows, D), F32),
-        in_specs=[VM] + [ANY] * 8,
-        out_specs=VM,
-        scratch_shapes=[pltpu.VMEM((3, D, cols), BF16)]
+        out_shape=[
+            jax.ShapeDtypeStruct((rows, D), F32),
+            jax.ShapeDtypeStruct((3, depth, cols), F32),
+            jax.ShapeDtypeStruct((cols, depth), F32),
+        ],
+        in_specs=[VM, ANY, ANY, ANY],
+        out_specs=[VM, VM, VM],
+        scratch_shapes=[
+            pltpu.VMEM((3, D, cols), BF16),
+            pltpu.VMEM((10, 3, depth // 2, cols), BF16),
+            pltpu.VMEM((10, cols // 2, depth), BF16),
+        ]
         + scatter_scratch(rows, D)
-        + [pltpu.SemaphoreType.DMA((8,))]
-        + SEMS,
+        + [pltpu.SemaphoreType.DMA((1,))]
+        + SEMS
+        + ring_sems(12),
         compiler_params=params(4),
-        cost_estimate=pl.CostEstimate(flops=50 << 30, bytes_accessed=100 << 20, transcendentals=0),
+        cost_estimate=LIGHT,
         name="input_back",
-    )(grad_proj.reshape(3, 4, 2, rows, cols), *pieces)
+    )(grad_proj.reshape(3, 4, 2, rows, cols), w_qkv, grad_qkv_part, grad_out_part)
+
+
+SPANS = ((0, 96), (96, 416), (512, 192))
 
 
 def body_ring(
@@ -1067,33 +1603,33 @@
     share_rows = cotangent.shape[0]
     share_start = lax.axis_index("mp") * share_rows
     deep_alpha = math.sqrt(2.0 * DEPTH)
-    depth = master_qkv.shape[1]
-    half = depth // 2
 
     low_qkv = master_qkv.astype(BF16)
-    qkv_pieces = ring_gather(low_qkv[:, :half], low_qkv[:, half:])
     low_out = master_out.astype(BF16)
-    out_half = low_out.shape[0] // 2
-    out_pieces = ring_gather(low_out[:out_half], low_out[out_half:])
-    low_gateup = master_gateup.astype(BF16)
-    gateup_pieces = ring_gather(low_gateup[0], low_gateup[1])
+    low_gateup = jnp.swapaxes(master_gateup, 1, 2).astype(BF16)
+    unit = low_gateup.shape[1] // 4
+    low_units = [low_gateup[:, k * unit : (k + 1) * unit] for k in range(4)]
     low_down = master_down.astype(BF16)
-    down_half = low_down.shape[0] // 2
-    down_pieces = ring_gather(low_down[:down_half], low_down[down_half:])
     w_norm = lax.optimization_barrier(master_norm.astype(BF16)).astype(F32)
 
-    cos_table, sin_table = rope_tables(positions)
-    sign = jnp.where(jnp.arange(HEAD_DIM) < HEAD_DIM // 2, -1.0, 1.0).astype(F32)
-    sin_table = sin_table * sign[None, :]
-    queries, key_rows, value_rows = qkv_call(block_input, qkv_pieces, cos_table, sin_table)
-    attended, probs = attention_call(queries, key_rows, value_rows, prefix_len)
-    attn_share = out_call(attended, out_pieces, share_rows)
+    queries, key_rows, value_rows, cos_table, sin_table, w_qkv = qkv_call(
+        block_input, low_qkv, positions, share_rows
+    )
+    cos_table = cos_table.reshape(token_count, HEAD_DIM)
+    sin_table = sin_table.reshape(token_count, HEAD_DIM)
+    queries, key_rows, value_rows = (
+        part.reshape(token_count, -1) for part in (queries, key_rows, value_rows)
+    )
+    attended, probs, w_out, unit_0 = attention_call(
+        queries, key_rows, value_rows, prefix_len, low_out, low_units[0]
+    )
+    attn_share, unit_1, unit_2 = out_call(attended, w_out, low_units[1:3], share_rows)
     input_share = lax.dynamic_slice_in_dim(block_input, share_start, share_rows, 0).astype(F32)
     middle_share, normed_one, inv_one = norm_forward(
         deep_alpha * input_share + attn_share, w_norm[0], w_norm[1]
     )
-    ffn_share, middle_low, hidden, act, pull = ffn_call(
-        middle_share.astype(BF16), gateup_pieces, down_pieces
+    ffn_share, middle_low, hidden, act, pull, w_gateup, w_down = ffn_call(
+        middle_share.astype(BF16), (unit_0, unit_1, unit_2), low_units[3], low_down
     )
     out_share, normed_two, inv_two = norm_forward(
         deep_alpha * middle_share + ffn_share, w_norm[2], w_norm[3]
@@ -1111,54 +1647,54 @@
     grad_h2, grad_gain_two, grad_bias_two = norm_backward(
         grad_output, normed_two, inv_two, w_norm[2]
     )
-    middle_grad, ffn_grad, grad_gateup_rows = ffn_back_call(
-        grad_h2.astype(BF16), act, pull, gateup_pieces, down_pieces
-    )
+    ffn_grad, grad_gateup_rows = ffn_back_call(grad_h2.astype(BF16), act, pull, w_down)
     hidden = hidden.reshape(token_count, -1)
     middle_low = middle_low.reshape(token_count, D)
     ffn_grad = ffn_grad.reshape(token_count, D)
-    grad_gateup_rows = grad_gateup_rows.reshape(2, token_count, -1)
+    gateup_rows = grad_gateup_rows.reshape(2, token_count, -1)
     grad_down_part = jnp.einsum("tf,td->fd", hidden, ffn_grad, preferred_element_type=F32).astype(BF16)
     grad_gateup_part = jnp.einsum(
-        "td,jtf->jdf", middle_low, grad_gateup_rows, preferred_element_type=F32
+        "jtf,td->jfd", gateup_rows, middle_low, preferred_element_type=F32
     ).astype(BF16)
+    grad_down_part, grad_gateup_part, grad_gateup_rows = lax.optimization_barrier(
+        (grad_down_part, grad_gateup_part, grad_gateup_rows)
+    )
+    middle_grad, red_down, red_gateup_0 = middle_back_call(
+        grad_gateup_rows, w_gateup, grad_down_part, grad_gateup_part, SPANS[0], share_rows
+    )
     middle_grad = middle_grad + deep_alpha * grad_h2
     grad_h1, grad_gain_one, grad_bias_one = norm_backward(
         middle_grad, normed_one, inv_one, w_norm[0]
     )
-    attn_grad, grad_attended = out_back_call(grad_h1.astype(BF16), out_pieces)
+    attn_grad, grad_attended, red_gateup_1 = out_back_call(
+        grad_h1.astype(BF16), w_out, grad_gateup_part, SPANS[1]
+    )
     attn_grad = attn_grad.reshape(token_count, D)
     grad_attended = grad_attended.reshape(token_count, -1)
     grad_out_part = jnp.einsum("tc,td->cd", attended, attn_grad, preferred_element_type=F32).astype(BF16)
-    grad_proj = attention_back_call(
-        queries, key_rows, value_rows, probs, attended, grad_attended, cos_table, sin_table
+    grad_out_part, grad_attended = lax.optimization_barrier((grad_out_part, grad_attended))
+    norm_terms = jnp.stack([grad_gain_one, grad_bias_one, grad_gain_two, grad_bias_two])
+    grad_proj, grad_norm, red_gateup_2 = attention_back_call(
+        queries,
+        key_rows,
+        value_rows,
+        probs,
+        attended,
+        grad_attended,
+        cos_table,
+        sin_table,
+        norm_terms,
+        grad_gateup_part,
+        SPANS[2],
+    )
+    red_gateup = jnp.swapaxes(
+        jnp.concatenate([red_gateup_0, red_gateup_1, red_gateup_2], axis=1), 1, 2
     )
     grad_qkv_part = jnp.einsum("td,jtc->jdc", block_input, grad_proj, preferred_element_type=F32).astype(BF16)
-    input_share_grad = input_back_call(grad_proj, qkv_pieces, share_rows)
+    input_share_grad, red_qkv, red_out = input_back_call(
+        grad_proj, w_qkv, grad_qkv_part, grad_out_part, share_rows
+    )
     grad_input = (input_share_grad + deep_alpha * grad_h1).astype(BF16)
-    norm_terms = jnp.stack([grad_gain_one, grad_bias_one, grad_gain_two, grad_bias_two])
-    grad_norm = lax.psum(norm_terms, ("dp", "mp"))
-
-    def down_shard(owner):
-        part = lax.dynamic_slice_in_dim(grad_down_part, owner * depth, depth, 1)
-        return part[:down_half], part[down_half:]
-
-    def gateup_shard(owner):
-        part = lax.dynamic_slice_in_dim(grad_gateup_part, owner * depth, depth, 1)
-        return part[0], part[1]
-
-    def out_shard(owner):
-        part = lax.dynamic_slice_in_dim(grad_out_part, owner * depth, depth, 1)
-        return part[:out_half], part[out_half:]
-
-    def qkv_shard(owner):
-        part = lax.dynamic_slice_in_dim(grad_qkv_part, owner * depth, depth, 1)
-        return part[:, :half], part[:, half:]
-
-    red_down = jnp.concatenate(ring_scatter(down_shard), axis=0)
-    red_gateup = jnp.stack(ring_scatter(gateup_shard))
-    red_out = jnp.concatenate(ring_scatter(out_shard), axis=0)
-    red_qkv = jnp.concatenate(ring_scatter(qkv_shard), axis=1)
 
     step_value = step_count[0].astype(F32)
     rate_qkv = D ** (-0.5)

time: 990 us -> 743 us (0.75)
  waiting for transfers between devices: 225 us -> 0 us
  Pallas kernels: 466 us -> 618 us
  starting transfers between devices: 70.2 us -> 0 us
  blocking collectives: 49.3 us -> 0 us
  local copies, waits for them, and re-layouts: 51.6 us -> 11.5 us
  other arithmetic: 61.4 us -> 46.9 us
    ppermute x48 -> x0, waiting for transfers between devices: 225 us -> none  [the longest x4 50.1 us: ring_scatter(): lax.ppermute((prv[1].astype(F32) + minus_far.astype(F32)).astype(BF16), '...]
    pallas_call x4 -> x5, Pallas kernels: 239 us -> 330 us  [the longest x1 76 us: input_back_call(): pl.pallas_call(kernel, out_shape=[jax.ShapeDtypeStruct((rows, D), F32), j...]
    ppermute x48 -> x0, starting transfers between devices: 70.2 us -> none  [the longest x4 12.6 us: ring_gather(): lax.ppermute(right[1], 'dp', MINUS)]
    psum x1 -> x0, blocking collectives: 49.3 us -> none  [body_ring(): grad_norm = lax.psum(norm_terms, ('dp', 'mp'))]
    pallas_call x1, Pallas kernels: 106 us -> 138 us  [ffn_call(): pl.pallas_call(kernel, out_shape=[jax.ShapeDtypeStruct((rows, D), F32), j...]
    pallas_call x1, Pallas kernels: 29 us -> 47.2 us  [attention_call(): pl.pallas_call(kernel, grid_spec=pltpu.PrefetchScalarGridSpec(num_scalar_...]
    unnamed x114 -> x60, local copies, waits for them, and re-layouts: 21.8 us -> 7.32 us
    ppermute x6 -> x0, local copies, waits for them, and re-layouts: 13.7 us -> none  [the longest x2 4.56 us: ring_gather(): left = (lax.ppermute(first, 'dp', PLUS), lax.ppermute(second, 'dp', PLUS))]
  transfers between devices with their start and end apart: 48 -> 0, of which waited for: 18 -> 0; matrix products, arithmetic and copies ran while one was open for 12% -> 0% of each run, Pallas kernels for 26% -> 0%
where the time goes in v2:
time: 743 us; the launch traced here: 733 us
  Pallas kernels  618 us (83%)
  matrix products  54.6 us (7%)
  other arithmetic  46.9 us (6%)
  local copies, waits for them, and re-layouts  11.5 us (2%)
    pallas_call x1, Pallas kernels, ffn_call(): pl.pallas_call(kernel, out_shape=[jax.ShapeDtypeStruct((rows, D), F32), j...  138 us
    pallas_call x1, Pallas kernels, input_back_call(): pl.pallas_call(kernel, out_shape=[jax.ShapeDtypeStruct((rows, D), F32), j...  76 us
    pallas_call x1, Pallas kernels, middle_back_call(): pl.pallas_call(kernel, out_shape=[jax.ShapeDtypeStruct((rows, D), F32), j...  65.7 us
    pallas_call x1, Pallas kernels, ffn_back_call(): pl.pallas_call(kernel, out_shape=[jax.ShapeDtypeStruct((4, 2, rows, D), B...  64.8 us
    pallas_call x1, Pallas kernels, qkv_call(): pl.pallas_call(kernel, out_shape=[tile] * 3 + [jax.ShapeDtypeStruct((tile...  64.7 us
    pallas_call x1, Pallas kernels, out_back_call(): pl.pallas_call(kernel, out_shape=[jax.ShapeDtypeStruct((4, 2, rows, D), B...  61.7 us
    pallas_call x1, Pallas kernels, out_call(): pl.pallas_call(kernel, out_shape=[jax.ShapeDtypeStruct((rows, D), F32)] +...  58.5 us
    pallas_call x1, Pallas kernels, attention_call(): pl.pallas_call(kernel, grid_spec=pltpu.PrefetchScalarGridSpec(num_scalar_...  47.2 us

profile of v2, /device:TPU:0, one launch (start us, length us, event | category | flops | bytes accessed | tf_op | source)
XLA Modules:
  0.0 733.3 jit_solution(15102708709518315447)
XLA Ops:
  0.7 3.0 reshape.161.pos_ref
  3.7 2.4 convert_element_type.65.low_ref
  6.1 64.7 %qkv.1 = (bf16[8,336,256]{2,1,0:T(8,128)(2,1)}, bf16[8,336,256]{2,1,0:T(8,128)(2,1)}, bf16[8,336,256]{2,1,0:T(8,128)(2,1)}, f32[8,336,128]{2,1,0:T(8,128)}, f32[...) custom-call(bf16[8,336,2048]{2,1,0:T(8,128)(2,1)} %bitcast.61, bf16[3,512,256]{2,1,0:T(8,128)(2,1)} %convert_element_type.65.low_ref, ...), custom_call_target="tpu_custom_call" | custom-call | flops 1048576 | bytes 65536 | tf_op jit(solution)/shard_map/qkv/pallas_call | solution.py:878
  72.8 47.2 %attention.1 = (bf16[2688,256]{1,0:T(8,128)(2,1)}, bf16[3,2,896,896]{3,2,1,0:T(8,128)(2,1)}, bf16[256,2048]{1,0:T(8,128)(2,1)}, bf16[2,176,2048]{2,1,0:T(8,128)(2,1)}) custom-call(s32[3]{0:T(128)} %pre_ref.1, bf16[2688,256]{1,0:T(8,128)(2,1)} %bitcast.62, bf16[2688,256]{1,0:T(8,128)(2,1)} %bitcast.64, bf16[2688,256]{1,0:T(8,128)(2,1)} %bitcast.66, ...), custom_call_target="tpu_custom_call" | custom-call | flops 1048576 | bytes 65536 | tf_op jit(solution)/shard_map/attention/pallas_call | solution.py:955
  120.1 58.5 %out_reduce.1 = (f32[336,2048]{1,0:T(8,128)}, bf16[2,176,2048]{2,1,0:T(8,128)(2,1)}, bf16[2,176,2048]{2,1,0:T(8,128)(2,1)}) custom-call(bf16[4,2,336,256]{3,2,1,0:T(8,128)(2,1)} %bitcast.60, bf16[256,2048]{1,0:T(8,128)(2,1)} %get-tuple-element.65.w_ref, bf16[2,176,512]{2,1,0:T(8,128)(2,1)} %get-tuple-element.134.rest_0_, ...), custom_call_target="tpu_custom_call" | custom-call | flops 1048576 | bytes 65536 | tf_op jit(solution)/shard_map/out_reduce/pallas_call | solution.py:1160
  178.6 2.6 fusion.30
  184.6 138.3 %ffn.1 = (f32[336,2048]{1,0:T(8,128)}, bf16[4,2,336,2048]{3,2,1,0:T(8,128)(2,1)}, bf16[4,2,336,704]{3,2,1,0:T(8,128)(2,1)}, bf16[4,2,336,704]{3,2,1,0:T(8,128)(2...) custom-call(bf16[336,2048]{1,0:T(8,128)(2,1)} %fusion.16.share, ...), custom_call_target="tpu_custom_call" | custom-call | flops 1048576 | bytes 65536 | tf_op jit(solution)/shard_map/ffn/pallas_call | solution.py:1279
  322.9 2.6 fusion.29
  327.8 3.7 multiply_reduce_fusion
  331.6 2.1 fusion.22.share
  333.7 64.8 %ffn_back.1 = (bf16[4,2,336,2048]{3,2,1,0:T(8,128)(2,1)}, bf16[2,4,2,336,704]{4,3,2,1,0:T(8,128)(2,1)}) custom-call(bf16[336,2048]{1,0:T(8,128)(2,1)} %fusion.22.share, bf16[4,2,336,704]{3,2,1,0:T(8,128)(2,1)} %get-tuple-element.73.act_ref, bf16[4,2,336,704]{3,2,1,0:T(8,128)(2,1)} %get-tuple-element.74.pull_ref, bf16[704,2048]{1,0:T(8,128)(2,1)} %get-tuple-element.75.wd_ref), custom_call_target="tpu_custom_call" | custom-call | flops 1048576 | bytes 65536 | tf_op jit(solution)/shard_map/ffn_back/pallas_call | solution.py:1356
  398.5 22.7 %bitcast_convert_fusion.gg_ref = bf16[2,704,2048]{2,1,0:T(8,128)(2,1)} fusion(bf16[2,4,2,336,704]{4,3,2,1,0:T(8,128)(2,1)} %get-tuple-element.79.dg_ref, bf16[4,2,336,2048]{3,2,1,0:T(8,128)(2,1)} %get-tuple-element.78), kind=kOutput, calls=%fused_computation | convolution fusion | flops 15505031168 | bytes 24346624 | tf_op jit(solution)/shard_map/jtf,td->jfd/dot_general | solution.py:1656
  421.3 10.0 %bitcast_convert_fusion.1.gd_ref = bf16[704,2048]{1,0:T(8,128)(2,1)} fusion(bf16[4,2,336,704]{3,2,1,0:T(8,128)(2,1)S(1)} %copy-done.26, bf16[4,2,336,2048]{3,2,1,0:T(8,128)(2,1)S(1)} %copy-done.25), kind=kOutput, calls=%fused_computation.5 | convolution fusion | flops 7752515584 | bytes 17678336 | tf_op jit(solution)/shard_map/tf,td->fd/dot_general | solution.py:1655
  431.3 65.7 %middle_back.1 = (f32[336,2048]{1,0:T(8,128)}, f32[704,512]{1,0:T(8,128)}, f32[2,96,512]{2,1,0:T(8,128)}) custom-call(bf16[2,4,2,336,704]{4,3,2,1,0:T(8,128)(2,1)} %get-tuple-element.79.dg_ref, bf16[2,704,2048]{2,1,0:T(8,128)(2,1)} %get-tuple-element.80.wg_ref, bf16[704,2048]{1,0:T(8,128)(2,1)} %bitcast_convert_fusion.1.gd_ref, ...), custom_call_target="tpu_custom_call" | custom-call | flops 1048576 | bytes 65536 | tf_op jit(solution)/shard_map/middle_back/pallas_call | solution.py:1434
  496.9 5.7 multiply_reduce_fusion.1
  503.3 2.9 fusion.28
  506.2 61.7 %out_back.1 = (bf16[4,2,336,2048]{3,2,1,0:T(8,128)(2,1)}, bf16[4,2,336,256]{3,2,1,0:T(8,128)(2,1)}, f32[2,416,512]{2,1,0:T(8,128)}) custom-call(bf16[336,2048]{1,0:T(8,128)(2,1)} %get-tuple-element.124.share, bf16[256,2048]{1,0:T(8,128)(2,1)} %get-tuple-element.65.w_ref, bf16[2,704,2048]{2,1,0:T(8,128)(2,1)} %bitcast_convert_fusion.gg_ref), custom_call_target="tpu_custom_call" | custom-call | flops 1048576 | bytes 65536 | tf_op jit(solution)/shard_map/out_back/pallas_call | solution.py:1486
  567.9 8.3 %convolution_convert_fusion.go_ref = bf16[256,2048]{1,0:T(8,128)(2,1)} fusion(bf16[2688,256]{1,0:T(8,128)(2,1)S(1)} %copy-done.2, bf16[2688,2048]{1,0:T(8,128)(2,1)} %bitcast.59), kind=kOutput, calls=%fused_computation.31 | convolution fusion | flops 2819096576 | bytes 13434880 | tf_op jit(solution)/shard_map/tc,td->cd/dot_general | solution.py:1674
  576.1 41.5 %attention_back.1 = (bf16[3,2688,256]{2,1,0:T(8,128)(2,1)}, f32[4,2048]{1,0:T(4,128)}, f32[2,192,512]{2,1,0:T(8,128)}) custom-call(bf16[2688,256]{1,0:T(8,128)(2,1)} %bitcast.63, bf16[2688,256]{1,0:T(8,128)(2,1)} %bitcast.65, bf16[2688,256]{1,0:T(8,128)(2,1)} %bitcast.67, bf16[3,2,896,896]{3,2,1,0:T(8,128)(2,1)} %get-tuple-element.71.p_ref, ...), custom_call_target="tpu_custom_call" | custom-call | flops 1048576 | bytes 65536 | tf_op jit(solution)/shard_map/attention_back/pallas_call | solution.py:1069
  618.4 7.5 %multiply_subtract_fusion = (f32[2,512,704]{1,2,0:T(8,128)}, f32[2,512,704]{1,2,0:T(8,128)}, f32[2,512,704]{1,2,0:T(8,128)}, f32[2,512,704]{1,2,0:T(8,128)}) fusion(f32[2,512,704]{1,2,0:T(8,128)S(1)} %copy-done.5, f32[]{:T(128)} %bitcast.28, f32[]{:T(128)} %bitcast.27, f32[2,512,704]{1,2,0:T(8,128)} %param.35, f32[2,512,704]{1,2,0:T(8,128)} %param.34, ...), kind=kLoop, calls=%fused_computation.11 | loop fusion | flops 12255232 | bytes 23068680 | tf_op jit(solution)/shard_map/sub | solution.py:84
  625.9 13.6 %fusion.9.gq_ref = bf16[3,2048,256]{2,1,0:T(8,128)(2,1)} fusion(bf16[3,2688,256]{2,1,0:T(8,128)(2,1)S(1)} %copy-done.12, bf16[2688,2048]{1,0:T(8,128)(2,1)} %param.21), kind=kOutput, calls=%fused_computation.8 | convolution fusion | flops 8457289728 | bytes 18284544 | tf_op jit(solution)/shard_map/td,jtc->jdc/dot_general | solution.py:1693
  639.5 76.0 %input_back.1 = (f32[336,2048]{1,0:T(8,128)}, f32[3,512,256]{2,1,0:T(8,128)}, f32[256,512]{1,0:T(8,128)}) custom-call(bf16[3,4,2,336,256]{4,3,2,1,0:T(8,128)(2,1)} %bitcast.68, bf16[3,2048,256]{2,1,0:T(8,128)(2,1)} %get-tuple-element.90.w_ref, bf16[3,2048,256]{2,1,0:T(8,128)(2,1)} %fusion.9.gq_ref, bf16[256,2048]{1,0:T(8,128)(2,1)} %convolution_convert_fusion.go_ref), custom_call_target="tpu_custom_call" | custom-call | flops 1048576 | bytes 65536 | tf_op jit(solution)/shard_map/input_back/pallas_call | solution.py:1551
  715.6 5.4 multiply_subtract_fusion.1
  726.6 2.8 multiply_subtract_fusion.2
  (84 shorter events, 17.6 us)
Async XLA Ops:
  6.1 64.7 %copy-start.4 = (f32[2,512,704]{1,2,0:T(8,128)S(1)}, f32[2,512,704]{1,2,0:T(8,128)}, u32[]{:S(2)}) copy-start(f32[2,512,704]{1,2,0:T(8,128)} %param.33) | copy-start | bytes 8650756
  181.7 2.0 copy-start.9
  325.5 2.0 copy-start.27
  327.4 4.1 copy-start.1
  327.5 4.1 copy-start.3
  398.5 22.7 %copy-start.25 = (bf16[4,2,336,2048]{3,2,1,0:T(8,128)(2,1)S(1)}, bf16[4,2,336,2048]{3,2,1,0:T(8,128)(2,1)}, u32[]{:S(2)}) copy-start(bf16[4,2,336,2048]{3,2,1,0:T(8,128)(2,1)} %get-tuple-element.76) | copy-start | bytes 33030148
  398.5 22.7 %copy-start.26 = (bf16[4,2,336,704]{3,2,1,0:T(8,128)(2,1)S(1)}, bf16[4,2,336,704]{3,2,1,0:T(8,128)(2,1)}, u32[]{:S(2)}) copy-start(bf16[4,2,336,704]{3,2,1,0:T(8,128)(2,1)} %get-tuple-element.72) | copy-start | bytes 11354116
  506.2 61.7 %copy-start.2 = (bf16[2688,256]{1,0:T(8,128)(2,1)S(1)}, bf16[2688,256]{1,0:T(8,128)(2,1)}, u32[]{:S(2)}) copy-start(bf16[2688,256]{1,0:T(8,128)(2,1)} %get-tuple-element.64.o_ref) | copy-start | bytes 4128772
  576.1 42.2 %copy-start.5 = (f32[2,512,704]{1,2,0:T(8,128)S(1)}, f32[2,512,704]{1,2,0:T(8,128)}, u32[]{:S(2)}) copy-start(f32[2,512,704]{1,2,0:T(8,128)} %param.33) | copy-start | bytes 8650756
  618.3 7.6 %copy-start.12 = (bf16[3,2688,256]{2,1,0:T(8,128)(2,1)S(1)}, bf16[3,2688,256]{2,1,0:T(8,128)(2,1)}, u32[]{:S(2)}) copy-start(bf16[3,2688,256]{2,1,0:T(8,128)(2,1)} %get-tuple-element.89) | copy-start | bytes 12386308
  639.5 76.0 %copy-start.7 = (f32[3,512,256]{2,1,0:T(8,128)S(1)}, f32[3,512,256]{2,1,0:T(8,128)}, u32[]{:S(2)}) copy-start(f32[3,512,256]{2,1,0:T(8,128)} %param.27) | copy-start | bytes 4718596
  715.5 5.5 copy-start.15
  715.5 5.5 copy-start.16
  715.5 5.5 copy-start.19
  715.5 5.5 copy-start.20
  715.6 6.9 copy-start.13
  721.0 2.3 copy-start.6
  723.3 1.7 copy-start.23
  723.3 1.7 copy-start.24
  723.3 2.4 copy-start.10
  723.3 2.4 copy-start.11
  723.3 2.8 copy-start.17
  723.4 3.2 copy-start.18
  726.6 2.8 copy-start.8
  (4 other events, 5.3 us)

commit v3 on v2

--- a/solution.py
+++ b/solution.py
@@ -542,11 +542,6 @@
     return RingScatter(ring, first, at, buf, lambda h: out.at[h])
 
 
-def each(items, name):
-    for item in items:
-        getattr(item, name)()
-
-
 def greet(others):
     sem = pltpu.get_barrier_semaphore()
     for other in others:
@@ -613,6 +608,7 @@
     between=nothing,
     middle=nothing,
     end=nothing,
+    near_first=False,
 ):
     send, recv, lsem = sems
     sq = Square(send, recv, rows)
@@ -639,49 +635,71 @@
         local = pltpu.make_async_copy(share, gbuf.at[sq.own, core], lsem.at[8])
         x_a.start()
         y_b.start()
+        if near_first:
+            x_b.start()
+            y_a.start()
         c_own.start()
         local.start()
     start()
     if gather is not None:
 
+        def take_own():
+            c_own.wait_recv()
+            local.wait()
+            first()
+
+        def forward():
+            x_a.wait_recv()
+            y_b.wait_recv()
+            f_x.start()
+            f_y.start()
+            if not near_first:
+                x_b.start()
+                y_a.start()
+            early()
+
+        def take_far():
+            f_x.wait_recv()
+            f_y.wait_recv()
+            c_d.start()
+            c_d.wait_recv()
+
+        def take_near():
+            x_b.wait_recv()
+            y_a.wait_recv()
+            c_x.start()
+            c_y.start()
+            later()
+            c_x.wait_recv()
+            c_y.wait_recv()
+
         def gather_step(t, carry):
-            chip, which = place(t // 2, t % 2)
-
-            @pl.when(t == 0)
-            def _():
-                c_own.wait_recv()
-                local.wait()
-                first()
+            unit = t // 2
+            if near_first:
+                chip_y = (sq.y + unit // 2) % 2
+                chip_x = (sq.x + unit % 2) % 2
+                chip, which = chip_y * 2 + chip_x, (1 - core + t % 2) % 2
+            else:
+                chip, which = place(unit, t % 2)
+
+            pl.when(t == 0)(take_own)
 
             @pl.when(t == 2)
             def _():
-                x_a.wait_recv()
-                y_b.wait_recv()
-                f_x.start()
-                f_y.start()
-                x_b.start()
-                y_a.start()
-                early()
-                f_x.wait_recv()
-                f_y.wait_recv()
-                c_d.start()
-                c_d.wait_recv()
-
-            @pl.when(t == 4)
-            def _():
-                x_b.wait_recv()
-                y_a.wait_recv()
-                c_x.start()
-                c_y.start()
-                later()
-                c_x.wait_recv()
-                c_y.wait_recv()
-
-            pltpu.make_async_copy(gbuf.at[chip, which], full.at[chip, which], lsem.at[t]).start()
+                forward()
+                if near_first:
+                    take_near()
+                else:
+                    take_far()
+
+            pl.when(t == (6 if near_first else 4))(take_far if near_first else take_near)
+
+            if full is not None:
+                pltpu.make_async_copy(gbuf.at[chip, which], full.at[chip, which], lsem.at[t]).start()
             compute(t, chip, which)
             return carry
 
-        lax.fori_loop(0, 8, gather_step, 0)
+        lax.fori_loop(0, 8 if scatter is None else 6, gather_step, 0)
     between()
     if scatter is not None:
         finish_tile, pbuf, (rcore, rxd, ryd, rx, ry), out = scatter
@@ -723,7 +741,12 @@
 
             return carry
 
-        lax.fori_loop(0, 8, scatter_step, 0)
+        if gather is None:
+            lax.fori_loop(0, 8, scatter_step, 0)
+        else:
+            lax.fori_loop(0, 2, scatter_step, 0)
+            lax.fori_loop(6, 8, gather_step, 0)
+            lax.fori_loop(2, 8, scatter_step, 0)
         x_d.wait_recv()
         add_rows(pbuf.at[sq.yc, core, sq.a], rxd, sq.na)
         y_ra.start()
@@ -754,8 +777,9 @@
     if gather is not None:
         for copy in (c_own, x_a, y_b, f_x, f_y, x_b, y_a, c_d, c_x, c_y):
             copy.wait_send()
-        for t in range(8):
-            pltpu.make_async_copy(gbuf.at[0, 0], full.at[0, 0], lsem.at[t]).wait()
+        if full is not None:
+            for t in range(8):
+                pltpu.make_async_copy(gbuf.at[0, 0], full.at[0, 0], lsem.at[t]).wait()
 
 
 def scatter_scratch(rows, width):
@@ -787,7 +811,7 @@
     return pl.BlockSpec(shape, lambda *_: (0,) * len(shape))
 
 
-def qkv_call(block_input, low_qkv, positions, rows):
+def qkv_call(block_input, low_qkv, low_out, positions, rows):
     tokens, width = block_input.shape
     depth, cols = low_qkv.shape[1:]
     tiles = tokens // rows
@@ -796,12 +820,17 @@
     half = depth // 2
 
     def kernel(
-        x_ref, low_ref, pos_ref, q_ref, k_ref, v_ref, cos_ref, sin_ref, w_ref,
+        x_ref, low_ref, lo_ref, pos_ref, q_ref, k_ref, v_ref, cos_ref, sin_ref, w_ref, wo_ref,
         x_buf, w_buf, acc, xsem, osem, send, recv, local,
     ):
         ring = Ring(send, recv, local)
         gather = RingGather(
             ring, 0, lambda h: low_ref.at[:, pl.ds(h * half, half), :], row_halves(depth)(w_buf)
+        )
+
+        out_half = lo_ref.shape[0] // 2
+        gather_out = RingGather(
+            ring, 6, lambda h: lo_ref.at[pl.ds(h * out_half, out_half), :], column_halves(depth)(wo_ref)
         )
 
         def x_copy(t, k):
@@ -845,6 +874,7 @@
 
         lax.fori_loop(0, tiles // 2, table_tile, 0)
         gather.forward()
+        gather_out.start()
         lax.fori_loop(tiles // 2, tiles, table_tile, 0)
         gather.near()
 
@@ -871,17 +901,19 @@
             return carry
 
         lax.fori_loop(0, tiles, far_tile, 0)
+        gather_out.forward()
         keep.wait()
         gather.drain()
+        gather_out.finish()
 
     tile = jax.ShapeDtypeStruct((tiles, rows, cols), BF16)
     return pl.pallas_call(
         kernel,
         out_shape=[tile] * 3
         + [jax.ShapeDtypeStruct((tiles, rows, HEAD_DIM), F32)] * 2
-        + [jax.ShapeDtypeStruct((3, width, cols), BF16)],
-        in_specs=[ANY, ANY, VM],
-        out_specs=[VM] * 5 + [ANY],
+        + [jax.ShapeDtypeStruct((3, width, cols), BF16), jax.ShapeDtypeStruct((cols, 4 * depth), BF16)],
+        in_specs=[ANY, ANY, ANY, VM],
+        out_specs=[VM] * 5 + [ANY, ANY],
         scratch_shapes=[
             pltpu.VMEM((tiles, 4, rows, depth), BF16),
             pltpu.VMEM((3, width, cols), BF16),
@@ -889,13 +921,14 @@
             pltpu.SemaphoreType.DMA((tiles, 4)),
             pltpu.SemaphoreType.DMA((1,)),
         ]
-        + ring_sems(6),
+        + ring_sems(12),
         compiler_params=params(5),
         cost_estimate=LIGHT,
         name="qkv",
     )(
         block_input.reshape(tiles, rows, width),
         low_qkv,
+        low_out,
         positions.reshape(tiles, rows, 1),
     )
 
@@ -903,28 +936,23 @@
 BLOCK = 128
 
 
-def attention_call(queries, key_rows, value_rows, prefix_len, low_out, low_unit):
+def attention_call(queries, key_rows, value_rows, prefix_len, low_unit):
     tokens, cols = queries.shape
     proteins = tokens // LEN
     heads = cols // HEAD_DIM
-    depth = low_out.shape[1]
+    depth = low_unit.shape[2]
     last = proteins * heads - 1
 
-    def kernel(pre_ref, q_ref, k_ref, v_ref, lo_ref, lu_ref, o_ref, p_ref, wo_ref, wu_ref, send, recv, local):
+    def kernel(pre_ref, q_ref, k_ref, v_ref, lu_ref, o_ref, p_ref, wu_ref, send, recv, local):
         prefix = pre_ref[pl.program_id(0)]
         step = pl.program_id(0) * heads + pl.program_id(1)
         ring = Ring(send, recv, local)
-        half = lo_ref.shape[0] // 2
-        gathers = [
-            RingGather(ring, 0, lambda h: lo_ref.at[pl.ds(h * half, half), :], column_halves(depth)(wo_ref)),
-            RingGather(ring, 6, lambda h: lu_ref.at[h], plane_columns(depth)(wu_ref)),
-        ]
+        gather = RingGather(ring, 0, lambda h: lu_ref.at[h], plane_columns(depth)(wu_ref))
 
         @pl.when(step == 0)
         def _():
             greet([{"dp": ring.left}, {"dp": ring.right}])
-            for gather in gathers:
-                gather.start()
+            gather.start()
 
         for i in range(LEN // BLOCK):
             rows = slice(i * BLOCK, (i + 1) * BLOCK)
@@ -937,19 +965,13 @@
             p_ref[0, 0, rows, :] = p
             o_ref[rows, :] = jnp.dot(p, v_ref[...], preferred_element_type=F32).astype(BF16)
 
-        @pl.when(step == last // 2)
+        @pl.when(step == last - 1)
         def _():
-            for gather in gathers:
-                gather.forward()
+            gather.forward()
 
         @pl.when(step == last)
         def _():
-            for gather in gathers:
-                for copy in gather.own:
-                    copy.wait()
-                gather.near()
-                gather.far()
-                gather.drain()
+            gather.finish()
 
     tile = pl.BlockSpec((LEN, HEAD_DIM), lambda p, h, *_: (p, h))
     return pl.pallas_call(
@@ -957,20 +979,19 @@
         grid_spec=pltpu.PrefetchScalarGridSpec(
             num_scalar_prefetch=1,
             grid=(proteins, heads),
-            in_specs=[tile] * 3 + [ANY, ANY],
-            out_specs=[tile, pl.BlockSpec((1, 1, LEN, LEN), lambda p, h, *_: (p, h, 0, 0)), ANY, ANY],
-            scratch_shapes=ring_sems(12),
+            in_specs=[tile] * 3 + [ANY],
+            out_specs=[tile, pl.BlockSpec((1, 1, LEN, LEN), lambda p, h, *_: (p, h, 0, 0)), ANY],
+            scratch_shapes=ring_sems(6),
         ),
         out_shape=[
             jax.ShapeDtypeStruct((tokens, cols), BF16),
             jax.ShapeDtypeStruct((proteins, heads, LEN, LEN), BF16),
-            jax.ShapeDtypeStruct((low_out.shape[0], 4 * depth), BF16),
             jax.ShapeDtypeStruct(low_unit.shape[:2] + (4 * depth,), BF16),
         ],
         compiler_params=params(6),
         cost_estimate=LIGHT,
         name="attention",
-    )(prefix_len, queries, key_rows, value_rows, low_out, low_unit)
+    )(prefix_len, queries, key_rows, value_rows, low_unit)
 
 
 TN = (((0,), (0,)), ((), ()))
@@ -978,7 +999,7 @@
 
 def attention_back_call(
     queries, key_rows, value_rows, probs, attended, grad_attended, cos_table, sin_table, norm_terms,
-    grad_gateup_part, span,
+    grad_out_part, grad_gateup_part, span,
 ):
     tokens, cols = queries.shape
     proteins = tokens // LEN
@@ -988,13 +1009,19 @@
     depth = grad_gateup_part.shape[2] // 4
 
     def kernel(
-        q_ref, k_ref, v_ref, p_ref, o_ref, do_ref, cos_ref, sin_ref, nt_ref, gg_ref,
-        da_ref, norm_ref, red_ref,
-        dk_acc, dv_acc, sums, got, nsend, nrecv, buf, send, recv, local,
+        q_ref, k_ref, v_ref, p_ref, o_ref, do_ref, cos_ref, sin_ref, nt_ref, go_ref, gg_ref,
+        da_ref, norm_ref, red_o, red_g,
+        dk_acc, dv_acc, sums, got, nsend, nrecv, buf_o, buf_g, send, recv, local,
     ):
         step = pl.program_id(0) * heads + pl.program_id(1)
         ring = Ring(send, recv, local)
-        side = span_scatter(ring, 0, gg_ref, span, buf, red_ref)
+        part = cols // 2
+        sides = (
+            span_scatter(ring, 0, gg_ref, span, buf_g, red_g),
+            RingScatter(
+                ring, 6, column_halves(depth)(go_ref), buf_o, lambda h: red_o.at[pl.ds(h * part, part), :]
+            ),
+        )
         sq = Square(nsend, nrecv, 32)
         partners = [
             {"mp": sq.peer},
@@ -1019,7 +1046,8 @@
         def _():
             sums[0] = nt_ref[...]
             greet(sq.others + [{"dp": ring.left}, {"dp": ring.right}])
-            side.start()
+            for side in sides:
+                side.start()
             swaps[0].start()
 
         for k in range(5):
@@ -1033,9 +1061,10 @@
                 else:
                     norm_ref[...] = sums[k] + got[k]
 
-        @pl.when(step == last // 2)
+        @pl.when(step == last - 1)
         def _():
-            side.forward()
+            for side in sides:
+                side.forward()
 
         for i in range(LEN // BLOCK):
             rows = slice(i * BLOCK, (i + 1) * BLOCK)
@@ -1062,7 +1091,8 @@
 
         @pl.when(step == last)
         def _():
-            side.finish()
+            for side in sides:
+                side.finish()
 
     tile = pl.BlockSpec((LEN, HEAD_DIM), lambda p, h: (p, h))
     table = pl.BlockSpec((LEN, HEAD_DIM), lambda p, h: (p, 0))
@@ -1071,15 +1101,17 @@
         grid=(proteins, heads),
         in_specs=[tile] * 3
         + [pl.BlockSpec((1, 1, LEN, LEN), lambda p, h: (p, h, 0, 0)), tile, tile, table, table]
-        + [whole(norm_terms.shape), ANY],
+        + [whole(norm_terms.shape), ANY, ANY],
         out_specs=[
             pl.BlockSpec((3, LEN, HEAD_DIM), lambda p, h: (0, p, h)),
             whole(norm_terms.shape),
+            whole((cols, depth)),
             whole((2, span[1], depth)),
         ],
         out_shape=[
             jax.ShapeDtypeStruct((3, tokens, cols), BF16),
             jax.ShapeDtypeStruct(norm_terms.shape, F32),
+            jax.ShapeDtypeStruct((cols, depth), F32),
             jax.ShapeDtypeStruct((2, span[1], depth), F32),
         ],
         scratch_shapes=[
@@ -1089,9 +1121,10 @@
             pltpu.VMEM((5,) + norm_terms.shape, F32),
             pltpu.SemaphoreType.DMA((5,)),
             pltpu.SemaphoreType.DMA((5,)),
+            pltpu.VMEM((10, cols // 2, depth), BF16),
             pltpu.VMEM((10, span[1], depth), BF16),
         ]
-        + ring_sems(6),
+        + ring_sems(12),
         compiler_params=params(7),
         cost_estimate=LIGHT,
         name="attention_back",
@@ -1105,6 +1138,7 @@
         cos_table,
         sin_table,
         norm_terms,
+        grad_out_part,
         grad_gateup_part,
     )
 
@@ -1174,23 +1208,20 @@
     )(attended.reshape(4, 2, rows, cols), w_out, *low_units)
 
 
-def ffn_call(middle_low, units, low_unit, low_down):
+def ffn_call(middle_low, units, low_down):
     rows = middle_low.shape[0]
     live, depth = low_down.shape
     count = len(units)
-    rest_rows = low_unit.shape[1]
     curve = math.sqrt(2.0 / math.pi)
 
-    def kernel(share, lu_ref, ld_ref, *rest):
+    def kernel(share, ld_ref, *rest):
         unit_refs, rest = rest[:count], rest[count:]
         out, full, hid_ref, act_ref, pull_ref, wg_ref, wd_ref = rest[:7]
         (w_g, w_d, gbuf, hid_buf, stage, pbuf, rcore, rxd, ryd, rx, ry) = rest[7:18]
         wsem, osem, hsem, send, recv, lsem, zsend, zrecv, zlocal = rest[18:]
         ring = Ring(zsend, zrecv, zlocal)
-        tail = w_g.at[:, pl.ds(live - rest_rows, rest_rows), :]
-        gather_g = RingGather(ring, 0, lambda h: lu_ref.at[h], plane_columns(depth)(tail))
         half = live // 2
-        gather_d = RingGather(ring, 6, lambda h: ld_ref.at[pl.ds(h * half, half), :], column_halves(depth)(w_d))
+        gather_d = RingGather(ring, 0, lambda h: ld_ref.at[pl.ds(h * half, half), :], column_halves(depth)(w_d))
         copies = []
         offset = 0
         for k, ref in enumerate(unit_refs):
@@ -1204,18 +1235,9 @@
         outs = (act_ref, pull_ref)
 
         def first():
-            gather_g.forward()
-            gather_d.start()
             for copy in copies:
                 copy.wait()
-            for copy in gather_g.own:
-                copy.wait()
-            gather_g.near()
-            gather_g.far()
             keep_g.start()
-
-        def later():
-            gather_d.forward()
 
         def between():
             for copy in gather_d.own:
@@ -1259,7 +1281,6 @@
                 pltpu.make_async_copy(hid_buf.at[0, 0], hid_ref.at[0, 0], hsem.at[t]).wait()
             keep_g.wait()
             keep_d.wait()
-            gather_g.drain()
             gather_d.drain()
 
         square_kernel(
@@ -1268,9 +1289,9 @@
             gather=(compute, share, full, gbuf),
             scatter=(finish_tile, pbuf, (rcore, rxd, ryd, rx, ry), out),
             ring=ring,
-            start=gather_g.start,
+            start=gather_d.start,
             first=first,
-            later=later,
+            early=gather_d.forward,
             between=between,
             end=end,
         )
@@ -1287,7 +1308,7 @@
             jax.ShapeDtypeStruct((2, live, D), BF16),
             jax.ShapeDtypeStruct((live, D), BF16),
         ],
-        in_specs=[ANY] * (3 + count),
+        in_specs=[ANY] * (2 + count),
         out_specs=[VM] + [ANY] * 6,
         scratch_shapes=[
             pltpu.VMEM((2, live, D), BF16),
@@ -1303,11 +1324,11 @@
             pltpu.SemaphoreType.DMA((8,)),
         ]
         + SEMS
-        + ring_sems(12),
+        + ring_sems(6),
         compiler_params=params(1),
         cost_estimate=LIGHT,
         name="ffn",
-    )(middle_low, low_unit, low_down, *units)
+    )(middle_low, low_down, *units)
 
 
 def ffn_back_call(ffn_grad, act, pull, w_down):
@@ -1350,7 +1371,12 @@
                     pltpu.make_async_copy(stage.at[slot, k], dg_ref.at[k, 0, 0], osem.at[slot, k]).wait()
 
         square_kernel(
-            rows, (send, recv, lsem), gather=(compute, share, full, gbuf), first=weight.wait, end=end
+            rows,
+            (send, recv, lsem),
+            gather=(compute, share, full, gbuf),
+            first=weight.wait,
+            end=end,
+            near_first=True,
         )
 
     return pl.pallas_call(
@@ -1377,20 +1403,16 @@
     )(ffn_grad, act, pull, w_down)
 
 
-def middle_back_call(grad_gateup_rows, w_gateup, grad_down_part, grad_gateup_part, span, rows):
-    live, width = grad_down_part.shape
+def middle_back_call(grad_gateup_rows, w_gateup, grad_gateup_part, span, rows):
+    live, width = grad_gateup_part.shape[1:]
     depth = width // 4
 
     def kernel(
-        dg_ref, wg_ref, gd_ref, gg_ref, out, red_d, red_g,
-        w_g, load, buf_d, buf_g, pbuf, rcore, rxd, ryd, rx, ry, wsem, isem, send, recv, lsem, zsend, zrecv, zlocal,
+        dg_ref, wg_ref, gg_ref, out, red_g,
+        w_g, load, buf_g, pbuf, rcore, rxd, ryd, rx, ry, wsem, isem, send, recv, lsem, zsend, zrecv, zlocal,
     ):
         ring = Ring(zsend, zrecv, zlocal)
-        half = live // 2
-        sides = (
-            RingScatter(ring, 0, column_halves(depth)(gd_ref), buf_d, lambda h: red_d.at[pl.ds(h * half, half), :]),
-            span_scatter(ring, 6, gg_ref, span, buf_g, red_g),
-        )
+        side = span_scatter(ring, 0, gg_ref, span, buf_g, red_g)
         weight = pltpu.make_async_copy(wg_ref, w_g, wsem.at[0])
         weight.start()
         me = lax.axis_index("mp")
@@ -1426,43 +1448,42 @@
             (send, recv, lsem),
             scatter=(compute, pbuf, (rcore, rxd, ryd, rx, ry), out),
             ring=ring,
-            start=lambda: (each(sides, "start"), weight.wait()),
-            middle=lambda: each(sides, "forward"),
-            end=lambda: each(sides, "finish"),
+            start=lambda: (side.start(), weight.wait()),
+            middle=side.forward,
+            end=side.finish,
         )
 
     return pl.pallas_call(
         kernel,
         out_shape=[
             jax.ShapeDtypeStruct((rows, D), F32),
-            jax.ShapeDtypeStruct((live, depth), F32),
             jax.ShapeDtypeStruct((2, span[1], depth), F32),
         ],
-        in_specs=[ANY] * 4,
-        out_specs=[VM] * 3,
+        in_specs=[ANY] * 3,
+        out_specs=[VM] * 2,
         scratch_shapes=[
             pltpu.VMEM((2, live, D), BF16),
             pltpu.VMEM((2, 2, rows, live), BF16),
-            pltpu.VMEM((10, live // 2, depth), BF16),
             pltpu.VMEM((10, span[1], depth), BF16),
         ]
         + scatter_scratch(rows, D)
         + [pltpu.SemaphoreType.DMA((1,)), pltpu.SemaphoreType.DMA((2, 2))]
         + SEMS
-        + ring_sems(12),
+        + ring_sems(6),
         compiler_params=params(8),
         cost_estimate=LIGHT,
         name="middle_back",
-    )(grad_gateup_rows, w_gateup, grad_down_part, grad_gateup_part)
-
-
-def out_back_call(attn_grad, w_out, grad_gateup_part, span):
+    )(grad_gateup_rows, w_gateup, grad_gateup_part)
+
+
+def out_back_call(attn_grad, w_out, attended, grad_gateup_part, span):
     rows = attn_grad.shape[0]
     cols = w_out.shape[0]
     depth = grad_gateup_part.shape[2] // 4
 
     def kernel(
-        share, w_ref, gg_ref, full, dout, red, w_buf, gbuf, buf, wsem, send, recv, lsem, zsend, zrecv, zlocal
+        share, w_ref, o_ref, gg_ref, dout, go_ref, red,
+        w_buf, gbuf, buf, acc, wsem, send, recv, lsem, zsend, zrecv, zlocal,
     ):
         ring = Ring(zsend, zrecv, zlocal)
         side = span_scatter(ring, 0, gg_ref, span, buf, red)
@@ -1470,32 +1491,48 @@
         weight.start()
 
         def compute(t, chip, which):
-            dout[chip, which] = nt_dot(gbuf[chip, which], w_buf[...]).astype(BF16)
+            tile = gbuf[chip, which]
+            dout[chip, which] = nt_dot(tile, w_buf[...]).astype(BF16)
+            part = lax.dot_general(o_ref[chip, which], tile, TN, preferred_element_type=F32)
+
+            @pl.when(t == 0)
+            def _():
+                acc[...] = part
+
+            @pl.when(t > 0)
+            def _():
+                acc[...] += part
+
+        def end():
+            go_ref[...] = acc[...].astype(BF16)
+            side.finish()
 
         square_kernel(
             rows,
             (send, recv, lsem),
-            gather=(compute, share, full, gbuf),
+            gather=(compute, share, None, gbuf),
             ring=ring,
             start=side.start,
             first=weight.wait,
             early=side.forward,
-            end=side.finish,
+            end=end,
+            near_first=True,
         )
 
     return pl.pallas_call(
         kernel,
         out_shape=[
-            jax.ShapeDtypeStruct((4, 2, rows, D), BF16),
             jax.ShapeDtypeStruct((4, 2, rows, cols), BF16),
+            jax.ShapeDtypeStruct((cols, D), BF16),
             jax.ShapeDtypeStruct((2, span[1], depth), F32),
         ],
-        in_specs=[ANY] * 3,
-        out_specs=[ANY, VM, VM],
+        in_specs=[ANY, ANY, VM, ANY],
+        out_specs=[VM, VM, VM],
         scratch_shapes=[
             pltpu.VMEM((cols, D), BF16),
             pltpu.VMEM((4, 2, rows, D), BF16),
             pltpu.VMEM((10, span[1], depth), BF16),
+            pltpu.VMEM((cols, D), F32),
             pltpu.SemaphoreType.DMA((1,)),
         ]
         + SEMS
@@ -1503,33 +1540,27 @@
         compiler_params=params(3),
         cost_estimate=LIGHT,
         name="out_back",
-    )(attn_grad, w_out, grad_gateup_part)
-
-
-def input_back_call(grad_proj, w_qkv, grad_qkv_part, grad_out_part, rows):
+    )(attn_grad, w_out, attended.reshape(4, 2, rows, cols), grad_gateup_part)
+
+
+def input_back_call(grad_proj, w_qkv, grad_qkv_part, rows):
     width, cols = w_qkv.shape[1:]
     depth = width // 4
 
     def kernel(
-        da_ref, w_ref, gq_ref, go_ref, out, red_q, red_o,
-        w_buf, buf_q, buf_o, pbuf, rcore, rxd, ryd, rx, ry, wsem, send, recv, lsem, zsend, zrecv, zlocal,
+        da_ref, w_ref, gq_ref, out, red_q,
+        w_buf, buf_q, pbuf, rcore, rxd, ryd, rx, ry, wsem, send, recv, lsem, zsend, zrecv, zlocal,
     ):
         ring = Ring(zsend, zrecv, zlocal)
         half = depth // 2
-        part = cols // 2
-        sides = (
-            RingScatter(
-                ring, 0, row_halves(depth)(gq_ref), buf_q, lambda h: red_q.at[:, pl.ds(h * half, half), :]
-            ),
-            RingScatter(
-                ring, 6, column_halves(depth)(go_ref), buf_o, lambda h: red_o.at[pl.ds(h * part, part), :]
-            ),
+        side = RingScatter(
+            ring, 0, row_halves(depth)(gq_ref), buf_q, lambda h: red_q.at[:, pl.ds(h * half, half), :]
         )
         weight = pltpu.make_async_copy(w_ref, w_buf, wsem.at[0])
         weight.start()
 
         def start():
-            each(sides, "start")
+            side.start()
             weight.wait()
 
         def compute(t, chip, which):
@@ -1544,8 +1575,8 @@
             scatter=(compute, pbuf, (rcore, rxd, ryd, rx, ry), out),
             ring=ring,
             start=start,
-            middle=lambda: each(sides, "forward"),
-            end=lambda: each(sides, "finish"),
+            middle=side.forward,
+            end=side.finish,
         )
 
     return pl.pallas_call(
@@ -1553,26 +1584,25 @@
         out_shape=[
             jax.ShapeDtypeStruct((rows, D), F32),
             jax.ShapeDtypeStruct((3, depth, cols), F32),
-            jax.ShapeDtypeStruct((cols, depth), F32),
         ],
-        in_specs=[VM, ANY, ANY, ANY],
-        out_specs=[VM, VM, VM],
+        in_specs=[VM, ANY, ANY],
+        out_specs=[VM, VM],
         scratch_shapes=[
             pltpu.VMEM((3, D, cols), BF16),
             pltpu.VMEM((10, 3, depth // 2, cols), BF16),
-            pltpu.VMEM((10, cols // 2, depth), BF16),
         ]
         + scatter_scratch(rows, D)
         + [pltpu.SemaphoreType.DMA((1,))]
         + SEMS
-        + ring_sems(12),
+        + ring_sems(6),
         compiler_params=params(4),
         cost_estimate=LIGHT,
         name="input_back",
-    )(grad_proj.reshape(3, 4, 2, rows, cols), w_qkv, grad_qkv_part, grad_out_part)
-
-
-SPANS = ((0, 96), (96, 416), (512, 192))
+    )(grad_proj.reshape(3, 4, 2, rows, cols), w_qkv, grad_qkv_part)
+
+
+PARTS = ((0, 240), (240, 464))
+SPANS = ((0, 176), (176, 416), (592, 112))
 
 
 def body_ring(
@@ -1607,29 +1637,26 @@
     low_qkv = master_qkv.astype(BF16)
     low_out = master_out.astype(BF16)
     low_gateup = jnp.swapaxes(master_gateup, 1, 2).astype(BF16)
-    unit = low_gateup.shape[1] // 4
-    low_units = [low_gateup[:, k * unit : (k + 1) * unit] for k in range(4)]
+    low_units = [low_gateup[:, first : first + size] for first, size in PARTS]
     low_down = master_down.astype(BF16)
     w_norm = lax.optimization_barrier(master_norm.astype(BF16)).astype(F32)
 
-    queries, key_rows, value_rows, cos_table, sin_table, w_qkv = qkv_call(
-        block_input, low_qkv, positions, share_rows
+    queries, key_rows, value_rows, cos_table, sin_table, w_qkv, w_out = qkv_call(
+        block_input, low_qkv, low_out, positions, share_rows
     )
     cos_table = cos_table.reshape(token_count, HEAD_DIM)
     sin_table = sin_table.reshape(token_count, HEAD_DIM)
     queries, key_rows, value_rows = (
         part.reshape(token_count, -1) for part in (queries, key_rows, value_rows)
     )
-    attended, probs, w_out, unit_0 = attention_call(
-        queries, key_rows, value_rows, prefix_len, low_out, low_units[0]
-    )
-    attn_share, unit_1, unit_2 = out_call(attended, w_out, low_units[1:3], share_rows)
+    attended, probs, unit_0 = attention_call(queries, key_rows, value_rows, prefix_len, low_units[0])
+    attn_share, unit_1 = out_call(attended, w_out, low_units[1:2], share_rows)
     input_share = lax.dynamic_slice_in_dim(block_input, share_start, share_rows, 0).astype(F32)
     middle_share, normed_one, inv_one = norm_forward(
         deep_alpha * input_share + attn_share, w_norm[0], w_norm[1]
     )
     ffn_share, middle_low, hidden, act, pull, w_gateup, w_down = ffn_call(
-        middle_share.astype(BF16), (unit_0, unit_1, unit_2), low_units[3], low_down
+        middle_share.astype(BF16), (unit_0, unit_1), low_down
     )
     out_share, normed_two, inv_two = norm_forward(
         deep_alpha * middle_share + ffn_share, w_norm[2], w_norm[3]
@@ -1653,28 +1680,26 @@
     ffn_grad = ffn_grad.reshape(token_count, D)
     gateup_rows = grad_gateup_rows.reshape(2, token_count, -1)
     grad_down_part = jnp.einsum("tf,td->fd", hidden, ffn_grad, preferred_element_type=F32).astype(BF16)
+    red_down = lax.psum_scatter(grad_down_part, "dp", scatter_dimension=1, tiled=True).astype(F32)
+    gateup_rows, grad_gateup_rows, grad_down_part = lax.optimization_barrier(
+        (gateup_rows, grad_gateup_rows, grad_down_part)
+    )
     grad_gateup_part = jnp.einsum(
         "jtf,td->jfd", gateup_rows, middle_low, preferred_element_type=F32
     ).astype(BF16)
-    grad_down_part, grad_gateup_part, grad_gateup_rows = lax.optimization_barrier(
-        (grad_down_part, grad_gateup_part, grad_gateup_rows)
-    )
-    middle_grad, red_down, red_gateup_0 = middle_back_call(
-        grad_gateup_rows, w_gateup, grad_down_part, grad_gateup_part, SPANS[0], share_rows
+    middle_grad, red_gateup_0 = middle_back_call(
+        grad_gateup_rows, w_gateup, grad_gateup_part, SPANS[0], share_rows
     )
     middle_grad = middle_grad + deep_alpha * grad_h2
     grad_h1, grad_gain_one, grad_bias_one = norm_backward(
         middle_grad, normed_one, inv_one, w_norm[0]
     )
-    attn_grad, grad_attended, red_gateup_1 = out_back_call(
-        grad_h1.astype(BF16), w_out, grad_gateup_part, SPANS[1]
-    )
-    attn_grad = attn_grad.reshape(token_count, D)
+    grad_attended, grad_out_part, red_gateup_1 = out_back_call(
+        grad_h1.astype(BF16), w_out, attended, grad_gateup_part, SPANS[1]
+    )
     grad_attended = grad_attended.reshape(token_count, -1)
-    grad_out_part = jnp.einsum("tc,td->cd", attended, attn_grad, preferred_element_type=F32).astype(BF16)
-    grad_out_part, grad_attended = lax.optimization_barrier((grad_out_part, grad_attended))
     norm_terms = jnp.stack([grad_gain_one, grad_bias_one, grad_gain_two, grad_bias_two])
-    grad_proj, grad_norm, red_gateup_2 = attention_back_call(
+    grad_proj, grad_norm, red_out, red_gateup_2 = attention_back_call(
         queries,
         key_rows,
         value_rows,
@@ -1684,6 +1709,7 @@
         cos_table,
         sin_table,
         norm_terms,
+        grad_out_part,
         grad_gateup_part,
         SPANS[2],
     )
@@ -1691,9 +1717,7 @@
         jnp.concatenate([red_gateup_0, red_gateup_1, red_gateup_2], axis=1), 1, 2
     )
     grad_qkv_part = jnp.einsum("td,jtc->jdc", block_input, grad_proj, preferred_element_type=F32).astype(BF16)
-    input_share_grad, red_qkv, red_out = input_back_call(
-        grad_proj, w_qkv, grad_qkv_part, grad_out_part, share_rows
-    )
+    input_share_grad, red_qkv = input_back_call(grad_proj, w_qkv, grad_qkv_part, share_rows)
     grad_input = (input_share_grad + deep_alpha * grad_h1).astype(BF16)
 
     step_value = step_count[0].astype(F32)

time: 743 us -> 712 us (0.958)
  Pallas kernels: 618 us -> 577 us
  between operations: 2 us -> 15.4 us
    pallas_call x1, Pallas kernels: 138 us -> 112 us  [ffn_call(): pl.pallas_call(kernel, out_shape=[jax.ShapeDtypeStruct((rows, D), F32), j...]
    pallas_call x1, Pallas kernels: 76 us -> 59.7 us  [input_back_call(): pl.pallas_call(kernel, out_shape=[jax.ShapeDtypeStruct((rows, D), F32), j...]
    pallas_call x1, Pallas kernels: 64.7 us -> 77.7 us  [qkv_call(): pl.pallas_call(kernel, out_shape=[tile] * 3 + [jax.ShapeDtypeStruct((tile...]
    pallas_call x1, Pallas kernels: 58.5 us -> 68.2 us  [out_call(): pl.pallas_call(kernel, out_shape=[jax.ShapeDtypeStruct((rows, D), F32)] +...]
    pallas_call x1, Pallas kernels: 64.8 us -> 55.3 us  [ffn_back_call(): pl.pallas_call(kernel, out_shape=[jax.ShapeDtypeStruct((4, 2, rows, D), B...]
    pallas_call x1, Pallas kernels: 47.2 us -> 38.6 us  [attention_call(): pl.pallas_call(kernel, grid_spec=pltpu.PrefetchScalarGridSpec(num_scalar_...]
    dot_general x1 -> x0, matrix products: 8.25 us -> none  [body_ring(): jnp.einsum('tc,td->cd', attended, attn_grad, preferred_element_type=F32)]
  transfers between devices with their start and end apart: 0 -> 1, of which waited for: 0 -> 0; matrix products, arithmetic and copies ran while one was open for 0% -> 9% of each run, Pallas kernels for 0% -> 32%
where the time goes in v3:
time: 712 us; the launch traced here: 703 us
  Pallas kernels  577 us (81%)
  matrix products  51.1 us (7%)
  other arithmetic  46.2 us (6%)
  between operations  15.4 us (2%)
  local copies, waits for them, and re-layouts  12.7 us (2%)
    pallas_call x1, Pallas kernels, ffn_call(): pl.pallas_call(kernel, out_shape=[jax.ShapeDtypeStruct((rows, D), F32), j...  112 us
    pallas_call x1, Pallas kernels, qkv_call(): pl.pallas_call(kernel, out_shape=[tile] * 3 + [jax.ShapeDtypeStruct((tile...  77.7 us
    pallas_call x1, Pallas kernels, out_call(): pl.pallas_call(kernel, out_shape=[jax.ShapeDtypeStruct((rows, D), F32)] +...  68.2 us
    pallas_call x1, Pallas kernels, out_back_call(): pl.pallas_call(kernel, out_shape=[jax.ShapeDtypeStruct((4, 2, rows, cols)...  62.7 us
    pallas_call x1, Pallas kernels, middle_back_call(): pl.pallas_call(kernel, out_shape=[jax.ShapeDtypeStruct((rows, D), F32), j...  60.7 us
    pallas_call x1, Pallas kernels, input_back_call(): pl.pallas_call(kernel, out_shape=[jax.ShapeDtypeStruct((rows, D), F32), j...  59.7 us
    pallas_call x1, Pallas kernels, ffn_back_call(): pl.pallas_call(kernel, out_shape=[jax.ShapeDtypeStruct((4, 2, rows, D), B...  55.3 us
    pallas_call x1, Pallas kernels, attention_back_call(): pl.pallas_call(kernel, grid=(proteins, heads), in_specs=[tile] * 3 + [pl....  42.4 us
  transfers between devices with their start and end apart: 1, of which 0 were waited for; matrix products, arithmetic and copies ran while one was open for 9% of the time, Pallas kernels for 32%

profile of v3, /device:TPU:0, one launch (start us, length us, event | category | flops | bytes accessed | tf_op | source)
XLA Modules:
  0.0 702.8 jit_solution(1484010068748470977)
XLA Ops:
  7.2 2.0 convert_bitcast_fusion
  11.1 2.3 reshape.163.pos_ref
  15.1 77.7 %qkv.1 = (bf16[8,336,256]{2,1,0:T(8,128)(2,1)}, bf16[8,336,256]{2,1,0:T(8,128)(2,1)}, bf16[8,336,256]{2,1,0:T(8,128)(2,1)}, f32[8,336,128]{2,1,0:T(8,128)}, f32[...) custom-call(bf16[8,336,2048]{2,1,0:T(8,128)(2,1)} %bitcast.46, ...), custom_call_target="tpu_custom_call" | custom-call | flops 1048576 | bytes 65536 | tf_op jit(solution)/shard_map/qkv/pallas_call | solution.py:910
  92.8 38.6 %attention.1 = (bf16[2688,256]{1,0:T(8,128)(2,1)}, bf16[3,2,896,896]{3,2,1,0:T(8,128)(2,1)}, bf16[2,240,2048]{2,1,0:T(8,128)(2,1)}) custom-call(s32[3]{0:T(128)} %pre_ref.1, bf16[2688,256]{1,0:T(8,128)(2,1)} %bitcast.50, bf16[2688,256]{1,0:T(8,128)(2,1)} %bitcast.52, bf16[2688,256]{1,0:T(8,128)(2,1)} %bitcast.54, bf16[2,240,512]{2,1,0:T(8,128)(2,1)} %slice.26.lu_ref), custom_call_target="tpu_custom_call" | custom-call | flops 1048576 | bytes 65536 | tf_op jit(solution)/shard_map/attention/pallas_call | solution.py:977
  131.4 68.2 %out_reduce.1 = (f32[336,2048]{1,0:T(8,128)}, bf16[2,464,2048]{2,1,0:T(8,128)(2,1)}) custom-call(bf16[4,2,336,256]{3,2,1,0:T(8,128)(2,1)} %bitcast.47, bf16[256,2048]{1,0:T(8,128)(2,1)} %get-tuple-element.60.w_ref, bf16[2,464,512]{2,1,0:T(8,128)(2,1)} %slice.27.rest_0_), custom_call_target="tpu_custom_call" | custom-call | flops 1048576 | bytes 65536 | tf_op jit(solution)/shard_map/out_reduce/pallas_call | solution.py:1194
  199.7 2.6 fusion.26
  206.2 112.1 %ffn.1 = (f32[336,2048]{1,0:T(8,128)}, bf16[4,2,336,2048]{3,2,1,0:T(8,128)(2,1)}, bf16[4,2,336,704]{3,2,1,0:T(8,128)(2,1)}, bf16[4,2,336,704]{3,2,1,0:T(8,128)(2...) custom-call(bf16[336,2048]{1,0:T(8,128)(2,1)} %fusion.12.share, ...), custom_call_target="tpu_custom_call" | custom-call | flops 1048576 | bytes 65536 | tf_op jit(solution)/shard_map/ffn/pallas_call | solution.py:1300
  318.3 2.6 fusion.25
  323.3 3.7 multiply_reduce_fusion
  327.0 2.1 fusion.18.share
  329.1 55.3 %ffn_back.1 = (bf16[4,2,336,2048]{3,2,1,0:T(8,128)(2,1)}, bf16[2,4,2,336,704]{4,3,2,1,0:T(8,128)(2,1)}) custom-call(bf16[336,2048]{1,0:T(8,128)(2,1)} %fusion.18.share, bf16[4,2,336,704]{3,2,1,0:T(8,128)(2,1)} %get-tuple-element.66.act_ref, bf16[4,2,336,704]{3,2,1,0:T(8,128)(2,1)} %get-tuple-element.67.pull_ref, bf16[704,2048]{1,0:T(8,128)(2,1)} %get-tuple-element.68.wd_ref), custom_call_target="tpu_custom_call" | custom-call | flops 1048576 | bytes 65536 | tf_op jit(solution)/shard_map/ffn_back/pallas_call | solution.py:1382
  384.4 13.6 %bitcast_convert_fusion = bf16[704,2048]{1,0:T(8,128)(2,1)} fusion(bf16[4,2,336,704]{3,2,1,0:T(8,128)(2,1)} %get-tuple-element.70, bf16[4,2,336,2048]{3,2,1,0:T(8,128)(2,1)} %get-tuple-element.71), kind=kOutput, calls=%fused_computation.2 | convolution fusion | flops 7752515584 | bytes 17678336 | tf_op jit(solution)/shard_map/tf,td->fd/dot_general | solution.py:1682
  398.0 23.1 %convolution_convert_fusion.gg_ref = bf16[2,704,2048]{2,1,0:T(8,128)(2,1)} fusion(bf16[2,2688,704]{2,1,0:T(8,128)(2,1)} %bitcast.49, bf16[2688,2048,1]{1,0,2:T(8,128)(2,1)} %bitcast.74), kind=kOutput, calls=%fused_computation.3 | convolution fusion | flops 15505031168 | bytes 24346624 | tf_op jit(solution)/shard_map/jtf,td->jfd/dot_general | solution.py:1687
  421.1 60.7 %middle_back.1 = (f32[336,2048]{1,0:T(8,128)}, f32[2,176,512]{2,1,0:T(8,128)}) custom-call(bf16[2,4,2,336,704]{4,3,2,1,0:T(8,128)(2,1)} %get-tuple-element.72.dg_ref, bf16[2,704,2048]{2,1,0:T(8,128)(2,1)} %get-tuple-element.73.wg_ref, bf16[2,704,2048]{2,1,0:T(8,128)(2,1)} %convolution_convert_fusion.gg_ref), custom_call_target="tpu_custom_call" | custom-call | flops 1048576 | bytes 65536 | tf_op jit(solution)/shard_map/middle_back/pallas_call | solution.py:1456
  481.8 5.7 multiply_reduce_fusion.1
  487.5 2.9 fusion.24
  491.2 62.7 %out_back.1 = (bf16[4,2,336,256]{3,2,1,0:T(8,128)(2,1)}, bf16[256,2048]{1,0:T(8,128)(2,1)}, f32[2,416,512]{2,1,0:T(8,128)}) custom-call(bf16[336,2048]{1,0:T(8,128)(2,1)} %get-tuple-element.115.share, bf16[256,2048]{1,0:T(8,128)(2,1)} %get-tuple-element.60.w_ref, bf16[4,2,336,256]{3,2,1,0:T(8,128)(2,1)} %bitcast.48, ...), custom_call_target="tpu_custom_call" | custom-call | flops 1048576 | bytes 65536 | tf_op jit(solution)/shard_map/out_back/pallas_call | solution.py:1522
  554.5 42.4 %attention_back.1 = (bf16[3,2688,256]{2,1,0:T(8,128)(2,1)}, f32[4,2048]{1,0:T(4,128)}, f32[256,512]{1,0:T(8,128)}, f32[2,112,512]{2,1,0:T(8,128)}) custom-call(bf16[2688,256]{1,0:T(8,128)(2,1)} %bitcast.51, bf16[2688,256]{1,0:T(8,128)(2,1)} %bitcast.53, bf16[2688,256]{1,0:T(8,128)(2,1)} %bitcast.55, bf16[3,2,896,896]{3,2,1,0:T(8,128)(2,1)} %get-tuple-element.65.p_ref, ...), custom_call_target="tpu_custom_call" | custom-call | flops 1048576 | bytes 65536 | tf_op jit(solution)/shard_map/attention_back/pallas_call | solution.py:1099
  596.9 14.4 %fusion.5.gq_ref = bf16[3,2048,256]{2,1,0:T(8,128)(2,1)} fusion(bf16[3,2688,256]{2,1,0:T(8,128)(2,1)} %get-tuple-element.81, bf16[2688,2048]{1,0:T(8,128)(2,1)} %param.21), kind=kOutput, calls=%fused_computation.6 | convolution fusion | flops 8457289728 | bytes 18284544 | tf_op jit(solution)/shard_map/td,jtc->jdc/dot_general | solution.py:1719
  611.3 59.7 %input_back.1 = (f32[336,2048]{1,0:T(8,128)}, f32[3,512,256]{2,1,0:T(8,128)}) custom-call(bf16[3,4,2,336,256]{4,3,2,1,0:T(8,128)(2,1)} %bitcast.56, bf16[3,2048,256]{2,1,0:T(8,128)(2,1)} %get-tuple-element.82.w_ref, bf16[3,2048,256]{2,1,0:T(8,128)(2,1)} %fusion.5.gq_ref), custom_call_target="tpu_custom_call" | custom-call | flops 1048576 | bytes 65536 | tf_op jit(solution)/shard_map/input_back/pallas_call | solution.py:1582
  673.5 3.6 add_convert_fusion
  677.6 2.9 multiply_subtract_fusion.1
  683.3 4.8 multiply_subtract_fusion
  688.2 5.0 multiply_subtract_fusion.2
  (90 shorter events, 18.7 us)
Async XLA Ops:
  7.2 3.9 copy-start.28
  7.2 681.0 %reduce-scatter.2.cloned.1.call-start = ((), (), s32[]{:S(2)}) async-start(), calls=%async_computation.1 | async-start | bytes 3604480 | tf_op jit(solution)/shard_map/reduce_scatter | solution.py:1683
  9.3 4.2 copy-start.5
  10.1 4.3 copy-start.12
  320.9 2.0 copy-start.29
  323.1 3.9 copy-start.1
  323.1 3.9 copy-start.2
  611.3 59.8 %copy-start.13 = (f32[256,512]{1,0:T(8,128)S(1)}, f32[256,512]{1,0:T(8,128)}, u32[]{:S(2)}) copy-start(f32[256,512]{1,0:T(8,128)} %param.30) | copy-start | bytes 1572868
  611.3 59.8 %copy-start.14 = (f32[256,512]{1,0:T(8,128)S(1)}, f32[256,512]{1,0:T(8,128)}, u32[]{:S(2)}) copy-start(f32[256,512]{1,0:T(8,128)} %get-tuple-element.157) | copy-start | bytes 1572868
  611.3 59.8 %copy-start.19 = (f32[256,512]{1,0:T(8,128)S(1)}, f32[256,512]{1,0:T(8,128)}, u32[]{:S(2)}) copy-start(f32[256,512]{1,0:T(8,128)} %param.32) | copy-start | bytes 1572868
  611.3 59.8 %copy-start.20 = (f32[256,512]{1,0:T(8,128)S(1)}, f32[256,512]{1,0:T(8,128)}, u32[]{:S(2)}) copy-start(f32[256,512]{1,0:T(8,128)} %param.31) | copy-start | bytes 1572868
  671.1 2.4 copy-start.4
  673.4 3.6 copy-start.6
  673.5 3.6 copy-start.7
  673.5 3.6 copy-start.16
  673.5 4.1 copy-start.17
  673.5 7.1 %copy-start.18 = (f32[2,176,512]{2,1,0:T(8,128)S(1)}, f32[2,176,512]{2,1,0:T(8,128)}, u32[]{:S(2)}) copy-start(f32[2,176,512]{2,1,0:T(8,128)} %get-tuple-element.86) | copy-start | bytes 2162692
  677.6 3.0 copy-start.3
  677.6 4.4 copy-start.10
  677.6 5.3 copy-start.11
  677.6 5.7 copy-start.15
  677.6 5.8 copy-start.21
  683.3 4.9 copy-start.9
  693.2 1.9 copy-start.25
  (7 other events, 9.7 us)
Sparse Core Ops, SparseCore 0:
  398.1 81.2 reduce-scatter.1

commit v4 on v3

--- a/solution.py
+++ b/solution.py
@@ -350,6 +350,7 @@
 VMEM_BYTES = 61 * 1024 * 1024
 BF16 = jnp.bfloat16
 F32 = jnp.float32
+EMIT = 48
 NT = (((1,), (1,)), ((), ()))
 ANY = pl.BlockSpec(memory_space=pl.ANY)
 VM = pl.BlockSpec(memory_space=pltpu.VMEM)
@@ -606,14 +607,17 @@
     early=nothing,
     later=nothing,
     between=nothing,
+    halfway=nothing,
     middle=nothing,
     end=nothing,
     near_first=False,
+    greeting=True,
 ):
     send, recv, lsem = sems
     sq = Square(send, recv, rows)
     core = sq.core
-    greet(sq.others + ([{"dp": ring.left}, {"dp": ring.right}] if ring is not None else []))
+    if greeting:
+        greet(sq.others + ([{"dp": ring.left}, {"dp": ring.right}] if ring is not None else []))
 
     def place(rel, turn):
         chip_y = (sq.y + rel % 2) % 2
@@ -702,7 +706,7 @@
         lax.fori_loop(0, 8 if scatter is None else 6, gather_step, 0)
     between()
     if scatter is not None:
-        finish_tile, pbuf, (rcore, rxd, ryd, rx, ry), out = scatter
+        finish_tile, pbuf, (rcore, rxd, ryd, rx, ry), emit = scatter
         x_d = sq.copy(14, pbuf.at[sq.dc, core, sq.a], rxd, sq.xn)
         y_d = sq.copy(15, pbuf.at[sq.dc, core, sq.b], ryd, sq.yn)
         x_ra = sq.copy(16, pbuf.at[sq.xc, core, sq.a], rx.at[sq.a], sq.xn)
@@ -714,6 +718,11 @@
             turn = t % 2
             rel = (t // 2 + 1) % 4
             chip, which = place(rel, turn)
+
+            @pl.when(t == 4)
+            def _():
+                halfway()
+
             finish_tile(t, chip, which)
             to_peer = sq.copy(10 + rel, pbuf.at[chip, which], rcore.at[chip], sq.peer)
 
@@ -760,15 +769,16 @@
         x_rb.wait_recv()
 
         def last(i, carry):
-            part = pl.ds(pl.multiple_of(i * 16, 16), 16)
-            out[part, :] = (
+            part = pl.ds(pl.multiple_of(i * EMIT, 16), EMIT)
+            emit(
+                part,
                 pbuf[sq.own, core, part, :].astype(F32)
                 + rx[part, :].astype(F32)
-                + ry[part, :].astype(F32)
+                + ry[part, :].astype(F32),
             )
             return carry
 
-        lax.fori_loop(0, rows // 16, last, 0)
+        lax.fori_loop(0, rows // EMIT, last, 0)
         for k in range(4):
             sq.copy(10 + k, pbuf.at[0, 0], rcore.at[0], sq.peer).wait_send()
         for copy in (x_d, y_d, x_ra, y_rb, x_rb, y_ra):
@@ -782,10 +792,28 @@
                 pltpu.make_async_copy(gbuf.at[0, 0], full.at[0, 0], lsem.at[t]).wait()
 
 
-def scatter_scratch(rows, width):
+def row_mean(values):
+    return jnp.mean(values, axis=-1, keepdims=True)
+
+
+def norm_rows(values):
+    centre = values - row_mean(values)
+    inv_std = lax.rsqrt(row_mean(centre * centre) + norm_epsilon)
+    return centre * inv_std, inv_std
+
+
+def norm_rows_back(grads, normed, inv_std, gain):
+    grad_normed = grads * gain
+    return inv_std * (grad_normed - row_mean(grad_normed) - normed * row_mean(grad_normed * normed))
+
+
+def fold(values):
+    return sum(values[i : i + 8] for i in range(0, EMIT, 8))
+
+
+def scatter_scratch(rows, width, with_sums=True):
     cut = rows // 2 // 16 * 16
-    return [
-        pltpu.VMEM((4, 2, rows, width), BF16),
+    return ([pltpu.VMEM((4, 2, rows, width), BF16)] if with_sums else []) + [
         pltpu.VMEM((4, rows, width), BF16),
         pltpu.VMEM((cut, width), BF16),
         pltpu.VMEM((rows - cut, width), BF16),
@@ -811,51 +839,76 @@
     return pl.BlockSpec(shape, lambda *_: (0,) * len(shape))
 
 
-def qkv_call(block_input, low_qkv, low_out, positions, rows):
+def front_call(block_input, low_qkv, low_out, low_gateup, positions, prefix_len, w_norm, rows, spans):
     tokens, width = block_input.shape
     depth, cols = low_qkv.shape[1:]
     tiles = tokens // rows
     heads = cols // HEAD_DIM
+    proteins = tokens // LEN
     scale = 1.0 / math.sqrt(HEAD_DIM)
+    alpha = math.sqrt(2.0 * DEPTH)
     half = depth // 2
+    out_half = cols // 2
+    span = spans[-1][0] + spans[-1][1]
 
     def kernel(
-        x_ref, low_ref, lo_ref, pos_ref, q_ref, k_ref, v_ref, cos_ref, sin_ref, w_ref, wo_ref,
-        x_buf, w_buf, acc, xsem, osem, send, recv, local,
+        pre_ref, x_ref, low_ref, lo_ref, lg_ref, pos_ref, norm_ref,
+        q_ref, k_ref, v_ref, o_ref, p_ref, cos_ref, sin_ref, w_ref, wo_ref, wg_ref,
+        x1_ref, x1b_ref, n1_ref, inv_ref,
+        x_buf, w_buf, acc, q_buf, k_buf, v_buf, o_buf, cos_buf, sin_buf, p_buf, wo_buf, xs_buf,
+        rcore, rxd, ryd, rx, ry, xsem, psem, ksem, send, recv, lsem, zsend, zrecv, zlocal,
     ):
-        ring = Ring(send, recv, local)
+        ring = Ring(zsend, zrecv, zlocal)
+        sems = Square(send, recv, rows)
         gather = RingGather(
             ring, 0, lambda h: low_ref.at[:, pl.ds(h * half, half), :], row_halves(depth)(w_buf)
         )
-
-        out_half = lo_ref.shape[0] // 2
         gather_out = RingGather(
-            ring, 6, lambda h: lo_ref.at[pl.ds(h * out_half, out_half), :], column_halves(depth)(wo_ref)
-        )
-
-        def x_copy(t, k):
-            return pltpu.make_async_copy(
-                x_ref.at[t, :, pl.ds(k * depth, depth)], x_buf.at[t, k], xsem.at[t, k]
+            ring, 6, lambda h: lo_ref.at[pl.ds(h * out_half, out_half), :], column_halves(depth)(wo_buf)
+        )
+        gathers = []
+        for n, (low, size) in enumerate(spans):
+            at = pl.ds(low, size)
+            gathers.append(
+                RingGather(
+                    ring,
+                    12 + 6 * n,
+                    lambda h, at=at: lg_ref.at[h, at, :],
+                    plane_columns(depth)(wg_ref.at[:, at, :]),
+                )
             )
+        own_rows = pltpu.make_async_copy(x_ref.at[sems.own, sems.core], xs_buf, xsem.at[8])
+        kept = ((q_buf, q_ref), (k_buf, k_ref), (v_buf, v_ref), (cos_buf, cos_ref), (sin_buf, sin_ref))
+        keeps = [pltpu.make_async_copy(src, dst, ksem.at[n]) for n, (src, dst) in enumerate(kept)]
+        keep_w = pltpu.make_async_copy(w_buf, w_ref, ksem.at[5])
+        keep_wo = pltpu.make_async_copy(wo_buf, wo_ref, ksem.at[6])
+        keep_o = pltpu.make_async_copy(o_buf, o_ref, ksem.at[7])
+
+        def x_copy(t):
+            return pltpu.make_async_copy(x_ref.at[t // 2, t % 2], x_buf.at[t // 2, t % 2], xsem.at[t])
 
         def start_tile(t, carry):
-            for k in range(4):
-                x_copy(t, k).start()
+            x_copy(t).start()
             return carry
 
         lax.fori_loop(0, tiles, start_tile, 0)
-        greet([{"dp": ring.left}, {"dp": ring.right}])
+        own_rows.start()
+        greet(sems.others + [{"dp": ring.left}, {"dp": ring.right}])
         gather.start()
         for copy in gather.own:
             copy.wait()
 
         def part(t, j, owner):
             depths = pl.ds(pl.multiple_of(owner * depth, depth), depth)
-            return jnp.dot(x_buf[t, owner], w_buf[j, depths, :], preferred_element_type=F32)
+            return jnp.dot(
+                x_buf[t // 2, t % 2, :, depths], w_buf[j, depths, :], preferred_element_type=F32
+            )
+
+        def tile_rows(t):
+            return pl.ds(pl.multiple_of(t * rows, 16), rows)
 
         def own_tile(t, carry):
-            for k in range(4):
-                x_copy(t, k).wait()
+            x_copy(t).wait()
             for j in range(3):
                 acc[t, j] = part(t, j, ring.here)
             return carry
@@ -868,8 +921,8 @@
 
         def table_tile(t, carry):
             angles = pos_ref[t].astype(F32) * inverse
-            cos_ref[t] = jnp.cos(angles)
-            sin_ref[t] = jnp.sin(angles) * sign
+            cos_buf[tile_rows(t), :] = jnp.cos(angles)
+            sin_buf[tile_rows(t), :] = jnp.sin(angles) * sign
             return carry
 
         lax.fori_loop(0, tiles // 2, table_tile, 0)
@@ -885,142 +938,172 @@
 
         lax.fori_loop(0, tiles, near_tile, 0)
         gather.far()
-        keep = pltpu.make_async_copy(w_buf, w_ref, osem.at[0])
-        keep.start()
+        gathers[0].start()
+        keep_w.start()
 
         def far_tile(t, carry):
-            for j, ref in enumerate((q_ref, k_ref)):
+            here = tile_rows(t)
+            for j, buf in enumerate((q_buf, k_buf)):
                 a = acc[t, j] + part(t, j, ring.far)
                 for h in range(heads):
                     cut = slice(h * HEAD_DIM, (h + 1) * HEAD_DIM)
-                    turned = a[:, cut] * cos_ref[t] + pltpu.roll(a[:, cut], HEAD_DIM // 2, 1) * sin_ref[t]
+                    turned = a[:, cut] * cos_buf[here, :]
+                    turned += pltpu.roll(a[:, cut], HEAD_DIM // 2, 1) * sin_buf[here, :]
                     if j == 0:
                         turned = turned * scale
-                    ref[t, :, cut] = turned.astype(BF16)
-            v_ref[t] = (acc[t, 2] + part(t, 2, ring.far)).astype(BF16)
+                    buf[here, cut] = turned.astype(BF16)
+            v_buf[here, :] = (acc[t, 2] + part(t, 2, ring.far)).astype(BF16)
             return carry
 
         lax.fori_loop(0, tiles, far_tile, 0)
         gather_out.forward()
-        keep.wait()
+        for keep in keeps:
+            keep.start()
+
+        def protein(p, carry):
+            prefix = pre_ref[p]
+            keys = pl.ds(pl.multiple_of(p * LEN, LEN), LEN)
+
+            @pl.when(p == proteins - 1)
+            def _():
+                gathers[0].forward()
+                gathers[1].start()
+
+            for h in range(heads):
+                cut = slice(h * HEAD_DIM, (h + 1) * HEAD_DIM)
+                store = pltpu.make_async_copy(p_buf.at[h], p_ref.at[p, h], psem.at[h])
+
+                @pl.when(p > 0)
+                def _():
+                    store.wait()
+
+                for i in range(LEN // BLOCK):
+                    here = pl.ds(pl.multiple_of(p * LEN + i * BLOCK, BLOCK), BLOCK)
+                    s = nt_dot(q_buf[here, cut], k_buf[keys, cut])
+                    col = lax.broadcasted_iota(jnp.int32, s.shape, 1)
+                    row = lax.broadcasted_iota(jnp.int32, (BLOCK, 1), 0) + i * BLOCK
+                    s = jnp.where(col < jnp.maximum(prefix, row + 1), s, -1e30)
+                    e = jnp.exp(s - jnp.max(s, axis=-1, keepdims=True))
+                    prob = (e * (1.0 / jnp.sum(e, axis=-1, keepdims=True))).astype(BF16)
+                    p_buf[h, i * BLOCK : (i + 1) * BLOCK, :] = prob
+                    mixed = jnp.dot(prob, v_buf[keys, cut], preferred_element_type=F32)
+                    o_buf[here, cut] = mixed.astype(BF16)
+                store.start()
+            return carry
+
+        lax.fori_loop(0, proteins, protein, 0)
+        for copy in gather_out.own:
+            copy.wait()
+        gather_out.near()
+        gather_out.far()
+        keep_wo.start()
+        keep_o.start()
+        own_rows.wait()
+
+        def compute(t, chip, which):
+            tile = o_buf[tile_rows(chip * 2 + which), :]
+            x_buf[chip, which] = jnp.dot(tile, wo_buf[...], preferred_element_type=F32).astype(BF16)
+
+        def emit(at, value):
+            normed, inv_std = norm_rows(alpha * xs_buf[at, :].astype(F32) + value)
+            x1 = normed * norm_ref[0:1, :] + norm_ref[1:2, :]
+            x1_ref[at, :] = x1
+            x1b_ref[at, :] = x1.astype(BF16)
+            n1_ref[at, :] = normed
+            inv_ref[at, :] = jnp.broadcast_to(inv_std, (EMIT, HEAD_DIM))
+
+        square_kernel(
+            rows,
+            (send, recv, lsem),
+            scatter=(compute, x_buf, (rcore, rxd, ryd, rx, ry), emit),
+            middle=gathers[1].forward,
+            greeting=False,
+        )
+        for other in gathers:
+            other.finish()
         gather.drain()
-        gather_out.finish()
-
-    tile = jax.ShapeDtypeStruct((tiles, rows, cols), BF16)
+        gather_out.drain()
+        for keep in keeps + [keep_w, keep_wo, keep_o]:
+            keep.wait()
+        for h in range(heads):
+            pltpu.make_async_copy(p_buf.at[h], p_ref.at[0, h], psem.at[h]).wait()
+
+    wide = jax.ShapeDtypeStruct((rows, width), F32)
     return pl.pallas_call(
         kernel,
-        out_shape=[tile] * 3
-        + [jax.ShapeDtypeStruct((tiles, rows, HEAD_DIM), F32)] * 2
-        + [jax.ShapeDtypeStruct((3, width, cols), BF16), jax.ShapeDtypeStruct((cols, 4 * depth), BF16)],
-        in_specs=[ANY, ANY, ANY, VM],
-        out_specs=[VM] * 5 + [ANY, ANY],
+        out_shape=[jax.ShapeDtypeStruct((tokens, cols), BF16)] * 4
+        + [jax.ShapeDtypeStruct((proteins, heads, LEN, LEN), BF16)]
+        + [jax.ShapeDtypeStruct((tokens, HEAD_DIM), F32)] * 2
+        + [
+            jax.ShapeDtypeStruct((3, width, cols), BF16),
+            jax.ShapeDtypeStruct((cols, width), BF16),
+            jax.ShapeDtypeStruct((2, span, width), BF16),
+            wide,
+            jax.ShapeDtypeStruct((rows, width), BF16),
+            wide,
+            jax.ShapeDtypeStruct((rows, HEAD_DIM), F32),
+        ],
+        in_specs=[pl.BlockSpec(memory_space=pltpu.SMEM)] + [ANY] * 4 + [VM, VM],
+        out_specs=[ANY] * 10 + [VM] * 4,
         scratch_shapes=[
-            pltpu.VMEM((tiles, 4, rows, depth), BF16),
+            pltpu.VMEM((4, 2, rows, width), BF16),
             pltpu.VMEM((3, width, cols), BF16),
             pltpu.VMEM((tiles, 3, rows, cols), F32),
-            pltpu.SemaphoreType.DMA((tiles, 4)),
-            pltpu.SemaphoreType.DMA((1,)),
         ]
-        + ring_sems(12),
-        compiler_params=params(5),
+        + [pltpu.VMEM((tokens, cols), BF16)] * 4
+        + [pltpu.VMEM((tokens, HEAD_DIM), F32)] * 2
+        + [
+            pltpu.VMEM((heads, LEN, LEN), BF16),
+            pltpu.VMEM((cols, width), BF16),
+            pltpu.VMEM((rows, width), BF16),
+        ]
+        + scatter_scratch(rows, width, False)
+        + [
+            pltpu.SemaphoreType.DMA((9,)),
+            pltpu.SemaphoreType.DMA((heads,)),
+            pltpu.SemaphoreType.DMA((8,)),
+        ]
+        + SEMS
+        + ring_sems(12 + 6 * len(spans)),
+        compiler_params=params(0),
         cost_estimate=LIGHT,
-        name="qkv",
+        name="front",
     )(
-        block_input.reshape(tiles, rows, width),
+        prefix_len,
+        block_input.reshape(4, 2, rows, width),
         low_qkv,
         low_out,
+        low_gateup,
         positions.reshape(tiles, rows, 1),
+        w_norm,
     )
 
 
 BLOCK = 128
-
-
-def attention_call(queries, key_rows, value_rows, prefix_len, low_unit):
-    tokens, cols = queries.shape
-    proteins = tokens // LEN
-    heads = cols // HEAD_DIM
-    depth = low_unit.shape[2]
-    last = proteins * heads - 1
-
-    def kernel(pre_ref, q_ref, k_ref, v_ref, lu_ref, o_ref, p_ref, wu_ref, send, recv, local):
-        prefix = pre_ref[pl.program_id(0)]
-        step = pl.program_id(0) * heads + pl.program_id(1)
-        ring = Ring(send, recv, local)
-        gather = RingGather(ring, 0, lambda h: lu_ref.at[h], plane_columns(depth)(wu_ref))
-
-        @pl.when(step == 0)
-        def _():
-            greet([{"dp": ring.left}, {"dp": ring.right}])
-            gather.start()
-
-        for i in range(LEN // BLOCK):
-            rows = slice(i * BLOCK, (i + 1) * BLOCK)
-            s = nt_dot(q_ref[rows, :], k_ref[...])
-            col = lax.broadcasted_iota(jnp.int32, s.shape, 1)
-            row = lax.broadcasted_iota(jnp.int32, (BLOCK, 1), 0) + i * BLOCK
-            s = jnp.where(col < jnp.maximum(prefix, row + 1), s, -1e30)
-            e = jnp.exp(s - jnp.max(s, axis=-1, keepdims=True))
-            p = (e * (1.0 / jnp.sum(e, axis=-1, keepdims=True))).astype(BF16)
-            p_ref[0, 0, rows, :] = p
-            o_ref[rows, :] = jnp.dot(p, v_ref[...], preferred_element_type=F32).astype(BF16)
-
-        @pl.when(step == last - 1)
-        def _():
-            gather.forward()
-
-        @pl.when(step == last)
-        def _():
-            gather.finish()
-
-    tile = pl.BlockSpec((LEN, HEAD_DIM), lambda p, h, *_: (p, h))
-    return pl.pallas_call(
-        kernel,
-        grid_spec=pltpu.PrefetchScalarGridSpec(
-            num_scalar_prefetch=1,
-            grid=(proteins, heads),
-            in_specs=[tile] * 3 + [ANY],
-            out_specs=[tile, pl.BlockSpec((1, 1, LEN, LEN), lambda p, h, *_: (p, h, 0, 0)), ANY],
-            scratch_shapes=ring_sems(6),
-        ),
-        out_shape=[
-            jax.ShapeDtypeStruct((tokens, cols), BF16),
-            jax.ShapeDtypeStruct((proteins, heads, LEN, LEN), BF16),
-            jax.ShapeDtypeStruct(low_unit.shape[:2] + (4 * depth,), BF16),
-        ],
-        compiler_params=params(6),
-        cost_estimate=LIGHT,
-        name="attention",
-    )(prefix_len, queries, key_rows, value_rows, low_unit)
-
-
 TN = (((0,), (0,)), ((), ()))
 
 
 def attention_back_call(
     queries, key_rows, value_rows, probs, attended, grad_attended, cos_table, sin_table, norm_terms,
-    grad_out_part, grad_gateup_part, span,
+    grad_out_part,
 ):
     tokens, cols = queries.shape
     proteins = tokens // LEN
     heads = cols // HEAD_DIM
     scale = 1.0 / math.sqrt(HEAD_DIM)
     last = proteins * heads - 1
-    depth = grad_gateup_part.shape[2] // 4
+    depth = grad_out_part.shape[1] // 4
 
     def kernel(
-        q_ref, k_ref, v_ref, p_ref, o_ref, do_ref, cos_ref, sin_ref, nt_ref, go_ref, gg_ref,
-        da_ref, norm_ref, red_o, red_g,
-        dk_acc, dv_acc, sums, got, nsend, nrecv, buf_o, buf_g, send, recv, local,
+        q_ref, k_ref, v_ref, p_ref, o_ref, do_ref, cos_ref, sin_ref, nt_ref, go_ref,
+        da_ref, norm_ref, red_o,
+        dk_acc, dv_acc, sums, got, nsend, nrecv, buf_o, send, recv, local,
     ):
         step = pl.program_id(0) * heads + pl.program_id(1)
         ring = Ring(send, recv, local)
         part = cols // 2
-        sides = (
-            span_scatter(ring, 0, gg_ref, span, buf_g, red_g),
-            RingScatter(
-                ring, 6, column_halves(depth)(go_ref), buf_o, lambda h: red_o.at[pl.ds(h * part, part), :]
-            ),
+        side = RingScatter(
+            ring, 0, column_halves(depth)(go_ref), buf_o, lambda h: red_o.at[pl.ds(h * part, part), :]
         )
         sq = Square(nsend, nrecv, 32)
         partners = [
@@ -1046,8 +1129,7 @@
         def _():
             sums[0] = nt_ref[...]
             greet(sq.others + [{"dp": ring.left}, {"dp": ring.right}])
-            for side in sides:
-                side.start()
+            side.start()
             swaps[0].start()
 
         for k in range(5):
@@ -1061,10 +1143,9 @@
                 else:
                     norm_ref[...] = sums[k] + got[k]
 
-        @pl.when(step == last - 1)
+        @pl.when(step == last // 2)
         def _():
-            for side in sides:
-                side.forward()
+            side.forward()
 
         for i in range(LEN // BLOCK):
             rows = slice(i * BLOCK, (i + 1) * BLOCK)
@@ -1091,8 +1172,7 @@
 
         @pl.when(step == last)
         def _():
-            for side in sides:
-                side.finish()
+            side.finish()
 
     tile = pl.BlockSpec((LEN, HEAD_DIM), lambda p, h: (p, h))
     table = pl.BlockSpec((LEN, HEAD_DIM), lambda p, h: (p, 0))
@@ -1101,18 +1181,16 @@
         grid=(proteins, heads),
         in_specs=[tile] * 3
         + [pl.BlockSpec((1, 1, LEN, LEN), lambda p, h: (p, h, 0, 0)), tile, tile, table, table]
-        + [whole(norm_terms.shape), ANY, ANY],
+        + [whole(norm_terms.shape), ANY],
         out_specs=[
             pl.BlockSpec((3, LEN, HEAD_DIM), lambda p, h: (0, p, h)),
             whole(norm_terms.shape),
             whole((cols, depth)),
-            whole((2, span[1], depth)),
         ],
         out_shape=[
             jax.ShapeDtypeStruct((3, tokens, cols), BF16),
             jax.ShapeDtypeStruct(norm_terms.shape, F32),
             jax.ShapeDtypeStruct((cols, depth), F32),
-            jax.ShapeDtypeStruct((2, span[1], depth), F32),
         ],
         scratch_shapes=[
             pltpu.VMEM((LEN, HEAD_DIM), F32),
@@ -1122,9 +1200,8 @@
             pltpu.SemaphoreType.DMA((5,)),
             pltpu.SemaphoreType.DMA((5,)),
             pltpu.VMEM((10, cols // 2, depth), BF16),
-            pltpu.VMEM((10, span[1], depth), BF16),
         ]
-        + ring_sems(12),
+        + ring_sems(6),
         compiler_params=params(7),
         cost_estimate=LIGHT,
         name="attention_back",
@@ -1139,105 +1216,28 @@
         sin_table,
         norm_terms,
         grad_out_part,
-        grad_gateup_part,
-    )
-
-
-def out_call(attended, w_out, low_units, rows):
-    cols = attended.shape[1]
-    count = len(low_units)
-    depth = low_units[0].shape[2]
-
-    def kernel(o_ref, w_ref, *rest):
-        low_refs, (out, *unit_refs), rest = rest[:count], rest[count : 2 * count + 1], rest[2 * count + 1 :]
-        w_buf, pbuf, rcore, rxd, ryd, rx, ry, wsem, send, recv, lsem, zsend, zrecv, zlocal = rest
-        ring = Ring(zsend, zrecv, zlocal)
-        gathers = [
-            RingGather(ring, 6 * k, lambda h, low=low: low.at[h], plane_columns(depth)(unit))
-            for k, (low, unit) in enumerate(zip(low_refs, unit_refs))
-        ]
-        weight = pltpu.make_async_copy(w_ref, w_buf, wsem.at[0])
-        weight.start()
-
-        def start():
-            gathers[0].start()
-            weight.wait()
-
-        def between():
-            gathers[0].forward()
-            for gather in gathers[1:]:
-                gather.start()
-
-        def middle():
-            for gather in gathers[1:]:
-                gather.forward()
-
-        def end():
-            for gather in gathers:
-                gather.finish()
-
-        def compute(t, chip, which):
-            part = jnp.dot(o_ref[chip, which], w_buf[...], preferred_element_type=F32)
-            pbuf[chip, which] = part.astype(BF16)
-
-        square_kernel(
-            rows,
-            (send, recv, lsem),
-            scatter=(compute, pbuf, (rcore, rxd, ryd, rx, ry), out),
-            ring=ring,
-            start=start,
-            between=nothing,
-            middle=lambda: (between(), middle()),
-            end=end,
-        )
-
-    return pl.pallas_call(
-        kernel,
-        out_shape=[jax.ShapeDtypeStruct((rows, D), F32)]
-        + [jax.ShapeDtypeStruct(low.shape[:2] + (D,), BF16) for low in low_units],
-        in_specs=[VM, ANY] + [ANY] * count,
-        out_specs=[VM] + [ANY] * count,
-        scratch_shapes=[pltpu.VMEM((cols, D), BF16)]
-        + scatter_scratch(rows, D)
-        + [pltpu.SemaphoreType.DMA((1,))]
-        + SEMS
-        + ring_sems(6 * count),
-        compiler_params=params(0),
-        cost_estimate=LIGHT,
-        name="out_reduce",
-    )(attended.reshape(4, 2, rows, cols), w_out, *low_units)
-
-
-def ffn_call(middle_low, units, low_down):
+    )
+
+
+def ffn_call(middle_low, middle_share, w_gateup, low_down, cotangent, row_weight, w_norm):
     rows = middle_low.shape[0]
     live, depth = low_down.shape
-    count = len(units)
     curve = math.sqrt(2.0 / math.pi)
-
-    def kernel(share, ld_ref, *rest):
-        unit_refs, rest = rest[:count], rest[count:]
-        out, full, hid_ref, act_ref, pull_ref, wg_ref, wd_ref = rest[:7]
-        (w_g, w_d, gbuf, hid_buf, stage, pbuf, rcore, rxd, ryd, rx, ry) = rest[7:18]
-        wsem, osem, hsem, send, recv, lsem, zsend, zrecv, zlocal = rest[18:]
+    alpha = math.sqrt(2.0 * DEPTH)
+
+    def kernel(
+        share, x1_ref, wg_ref, ld_ref, cot_ref, rw_ref, norm_ref,
+        y_ref, dh_ref, dhb_ref, terms_ref, full, hid_ref, act_ref, pull_ref, wd_ref,
+        w_g, w_d, gbuf, hid_buf, stage, pbuf, rcore, rxd, ryd, rx, ry, sums,
+        wsem, osem, hsem, send, recv, lsem, zsend, zrecv, zlocal,
+    ):
         ring = Ring(zsend, zrecv, zlocal)
         half = live // 2
         gather_d = RingGather(ring, 0, lambda h: ld_ref.at[pl.ds(h * half, half), :], column_halves(depth)(w_d))
-        copies = []
-        offset = 0
-        for k, ref in enumerate(unit_refs):
-            size = ref.shape[1]
-            copies.append(pltpu.make_async_copy(ref, w_g.at[:, pl.ds(offset, size), :], wsem.at[k]))
-            offset += size
-        for copy in copies:
-            copy.start()
-        keep_g = pltpu.make_async_copy(w_g, wg_ref, wsem.at[count])
-        keep_d = pltpu.make_async_copy(w_d, wd_ref, wsem.at[count + 1])
+        load_g = pltpu.make_async_copy(wg_ref, w_g, wsem.at[0])
+        load_g.start()
+        keep_d = pltpu.make_async_copy(w_d, wd_ref, wsem.at[1])
         outs = (act_ref, pull_ref)
-
-        def first():
-            for copy in copies:
-                copy.wait()
-            keep_g.start()
 
         def between():
             for copy in gather_d.own:
@@ -1273,13 +1273,26 @@
             part = jnp.dot(hid_buf[chip, which], w_d[...], preferred_element_type=F32)
             pbuf[chip, which] = part.astype(BF16)
 
+        def emit(at, value):
+            normed, inv_std = norm_rows(alpha * x1_ref[at, :] + value)
+            gain = norm_ref[2:3, :]
+            y_ref[at, :] = (normed * gain + norm_ref[3:4, :]).astype(BF16)
+            dy = cot_ref[at, :].astype(F32) * rw_ref[at, :]
+            sums[0] += fold(dy * normed)
+            sums[1] += fold(dy)
+            dh = norm_rows_back(dy, normed, inv_std, gain)
+            dh_ref[at, :] = dh
+            dhb_ref[at, :] = dh.astype(BF16)
+
+        sums[...] = jnp.zeros_like(sums)
+
         def end():
+            terms_ref[...] = jnp.sum(sums[...], axis=1)
             for slot in range(2):
                 for k, ref in enumerate(outs):
                     pltpu.make_async_copy(stage.at[slot, k], ref.at[0, 0], osem.at[slot, k]).wait()
             for t in range(8):
                 pltpu.make_async_copy(hid_buf.at[0, 0], hid_ref.at[0, 0], hsem.at[t]).wait()
-            keep_g.wait()
             keep_d.wait()
             gather_d.drain()
 
@@ -1287,11 +1300,11 @@
             rows,
             (send, recv, lsem),
             gather=(compute, share, full, gbuf),
-            scatter=(finish_tile, pbuf, (rcore, rxd, ryd, rx, ry), out),
+            scatter=(finish_tile, pbuf, (rcore, rxd, ryd, rx, ry), emit),
             ring=ring,
             start=gather_d.start,
-            first=first,
-            early=gather_d.forward,
+            first=load_g.wait,
+            later=gather_d.forward,
             between=between,
             end=end,
         )
@@ -1300,16 +1313,18 @@
     return pl.pallas_call(
         kernel,
         out_shape=[
+            jax.ShapeDtypeStruct((rows, D), BF16),
             jax.ShapeDtypeStruct((rows, D), F32),
+            jax.ShapeDtypeStruct((rows, D), BF16),
+            jax.ShapeDtypeStruct((2, D), F32),
             jax.ShapeDtypeStruct((4, 2, rows, D), BF16),
             kept,
             kept,
             kept,
-            jax.ShapeDtypeStruct((2, live, D), BF16),
             jax.ShapeDtypeStruct((live, D), BF16),
         ],
-        in_specs=[ANY] * (2 + count),
-        out_specs=[VM] + [ANY] * 6,
+        in_specs=[ANY, VM, ANY, ANY, VM, VM, VM],
+        out_specs=[VM] * 4 + [ANY] * 5,
         scratch_shapes=[
             pltpu.VMEM((2, live, D), BF16),
             pltpu.VMEM((live, D), BF16),
@@ -1319,7 +1334,8 @@
         ]
         + scatter_scratch(rows, D)
         + [
-            pltpu.SemaphoreType.DMA((count + 2,)),
+            pltpu.VMEM((2, 8, D), F32),
+            pltpu.SemaphoreType.DMA((2,)),
             pltpu.SemaphoreType.DMA((2, 2)),
             pltpu.SemaphoreType.DMA((8,)),
         ]
@@ -1328,7 +1344,7 @@
         compiler_params=params(1),
         cost_estimate=LIGHT,
         name="ffn",
-    )(middle_low, low_down, *units)
+    )(middle_low, middle_share, w_gateup, low_down, cotangent, row_weight, w_norm)
 
 
 def ffn_back_call(ffn_grad, act, pull, w_down):
@@ -1403,16 +1419,19 @@
     )(ffn_grad, act, pull, w_down)
 
 
-def middle_back_call(grad_gateup_rows, w_gateup, grad_gateup_part, span, rows):
+def middle_back_call(grad_gateup_rows, w_gateup, grad_gateup_part, spans, grad_h2, normed, inv_std, w_norm):
+    rows = grad_h2.shape[0]
+    alpha = math.sqrt(2.0 * DEPTH)
     live, width = grad_gateup_part.shape[1:]
     depth = width // 4
 
     def kernel(
-        dg_ref, wg_ref, gg_ref, out, red_g,
-        w_g, load, buf_g, pbuf, rcore, rxd, ryd, rx, ry, wsem, isem, send, recv, lsem, zsend, zrecv, zlocal,
+        dg_ref, wg_ref, gg_ref, dh2_ref, n1_ref, inv_ref, norm_ref, dh_ref, dhb_ref, terms_ref, red_0, red_1,
+        w_g, load, buf_0, buf_1, pbuf, rcore, rxd, ryd, rx, ry, sums, wsem, isem, send, recv, lsem, zsend, zrecv, zlocal,
     ):
         ring = Ring(zsend, zrecv, zlocal)
-        side = span_scatter(ring, 0, gg_ref, span, buf_g, red_g)
+        early = span_scatter(ring, 0, gg_ref, spans[0], buf_0, red_0)
+        late = span_scatter(ring, 6, gg_ref, spans[1], buf_1, red_1)
         weight = pltpu.make_async_copy(wg_ref, w_g, wsem.at[0])
         weight.start()
         me = lax.axis_index("mp")
@@ -1443,37 +1462,59 @@
             part += jnp.dot(load[slot, 1], w_g[1], preferred_element_type=F32)
             pbuf[chip, which] = part.astype(BF16)
 
+        sums[...] = jnp.zeros_like(sums)
+
+        def emit(at, value):
+            grads = value + alpha * dh2_ref[at, :]
+            normed = n1_ref[at, :]
+            sums[0] += fold(grads * normed)
+            sums[1] += fold(grads)
+            dh = norm_rows_back(grads, normed, inv_ref[at, 0:1], norm_ref[0:1, :])
+            dh_ref[at, :] = dh
+            dhb_ref[at, :] = dh.astype(BF16)
+
+        def end():
+            terms_ref[...] = jnp.sum(sums[...], axis=1)
+            early.finish()
+            late.finish()
+
         square_kernel(
             rows,
             (send, recv, lsem),
-            scatter=(compute, pbuf, (rcore, rxd, ryd, rx, ry), out),
+            scatter=(compute, pbuf, (rcore, rxd, ryd, rx, ry), emit),
             ring=ring,
-            start=lambda: (side.start(), weight.wait()),
-            middle=side.forward,
-            end=side.finish,
+            start=lambda: (early.start(), weight.wait()),
+            halfway=lambda: (early.forward(), late.start()),
+            middle=late.forward,
+            end=end,
         )
 
     return pl.pallas_call(
         kernel,
         out_shape=[
             jax.ShapeDtypeStruct((rows, D), F32),
-            jax.ShapeDtypeStruct((2, span[1], depth), F32),
+            jax.ShapeDtypeStruct((rows, D), BF16),
+            jax.ShapeDtypeStruct((2, D), F32),
+            jax.ShapeDtypeStruct((2, spans[0][1], depth), F32),
+            jax.ShapeDtypeStruct((2, spans[1][1], depth), F32),
         ],
-        in_specs=[ANY] * 3,
-        out_specs=[VM] * 2,
+        in_specs=[ANY] * 3 + [VM] * 4,
+        out_specs=[VM] * 5,
         scratch_shapes=[
             pltpu.VMEM((2, live, D), BF16),
             pltpu.VMEM((2, 2, rows, live), BF16),
-            pltpu.VMEM((10, span[1], depth), BF16),
+            pltpu.VMEM((10, spans[0][1], depth), BF16),
+            pltpu.VMEM((10, spans[1][1], depth), BF16),
         ]
         + scatter_scratch(rows, D)
+        + [pltpu.VMEM((2, 8, D), F32)]
         + [pltpu.SemaphoreType.DMA((1,)), pltpu.SemaphoreType.DMA((2, 2))]
         + SEMS
-        + ring_sems(6),
+        + ring_sems(12),
         compiler_params=params(8),
         cost_estimate=LIGHT,
         name="middle_back",
-    )(grad_gateup_rows, w_gateup, grad_gateup_part)
+    )(grad_gateup_rows, w_gateup, grad_gateup_part, grad_h2, normed, inv_std, w_norm)
 
 
 def out_back_call(attn_grad, w_out, attended, grad_gateup_part, span):
@@ -1543,12 +1584,14 @@
     )(attn_grad, w_out, attended.reshape(4, 2, rows, cols), grad_gateup_part)
 
 
-def input_back_call(grad_proj, w_qkv, grad_qkv_part, rows):
+def input_back_call(grad_proj, w_qkv, grad_qkv_part, grad_h1):
+    rows = grad_h1.shape[0]
+    alpha = math.sqrt(2.0 * DEPTH)
     width, cols = w_qkv.shape[1:]
     depth = width // 4
 
     def kernel(
-        da_ref, w_ref, gq_ref, out, red_q,
+        da_ref, w_ref, gq_ref, dh_ref, out, red_q,
         w_buf, buf_q, pbuf, rcore, rxd, ryd, rx, ry, wsem, send, recv, lsem, zsend, zrecv, zlocal,
     ):
         ring = Ring(zsend, zrecv, zlocal)
@@ -1569,10 +1612,13 @@
             part += nt_dot(da_ref[2, chip, which], w_buf[2])
             pbuf[chip, which] = part.astype(BF16)
 
+        def emit(at, value):
+            out[at, :] = (value + alpha * dh_ref[at, :]).astype(BF16)
+
         square_kernel(
             rows,
             (send, recv, lsem),
-            scatter=(compute, pbuf, (rcore, rxd, ryd, rx, ry), out),
+            scatter=(compute, pbuf, (rcore, rxd, ryd, rx, ry), emit),
             ring=ring,
             start=start,
             middle=side.forward,
@@ -1582,10 +1628,10 @@
     return pl.pallas_call(
         kernel,
         out_shape=[
-            jax.ShapeDtypeStruct((rows, D), F32),
+            jax.ShapeDtypeStruct((rows, D), BF16),
             jax.ShapeDtypeStruct((3, depth, cols), F32),
         ],
-        in_specs=[VM, ANY, ANY],
+        in_specs=[VM, ANY, ANY, VM],
         out_specs=[VM, VM],
         scratch_shapes=[
             pltpu.VMEM((3, D, cols), BF16),
@@ -1598,11 +1644,11 @@
         compiler_params=params(4),
         cost_estimate=LIGHT,
         name="input_back",
-    )(grad_proj.reshape(3, 4, 2, rows, cols), w_qkv, grad_qkv_part)
-
-
-PARTS = ((0, 240), (240, 464))
-SPANS = ((0, 176), (176, 416), (592, 112))
+    )(grad_proj.reshape(3, 4, 2, rows, cols), w_qkv, grad_qkv_part, grad_h1)
+
+
+FRONT_SPANS = ((0, 240), (240, 464))
+SPANS = ((0, 144), (144, 144), (288, 416))
 
 
 def body_ring(
@@ -1632,36 +1678,19 @@
     protein_count = token_count // LEN
     share_rows = cotangent.shape[0]
     share_start = lax.axis_index("mp") * share_rows
-    deep_alpha = math.sqrt(2.0 * DEPTH)
 
     low_qkv = master_qkv.astype(BF16)
     low_out = master_out.astype(BF16)
     low_gateup = jnp.swapaxes(master_gateup, 1, 2).astype(BF16)
-    low_units = [low_gateup[:, first : first + size] for first, size in PARTS]
     low_down = master_down.astype(BF16)
     w_norm = lax.optimization_barrier(master_norm.astype(BF16)).astype(F32)
 
-    queries, key_rows, value_rows, cos_table, sin_table, w_qkv, w_out = qkv_call(
-        block_input, low_qkv, low_out, positions, share_rows
-    )
-    cos_table = cos_table.reshape(token_count, HEAD_DIM)
-    sin_table = sin_table.reshape(token_count, HEAD_DIM)
-    queries, key_rows, value_rows = (
-        part.reshape(token_count, -1) for part in (queries, key_rows, value_rows)
-    )
-    attended, probs, unit_0 = attention_call(queries, key_rows, value_rows, prefix_len, low_units[0])
-    attn_share, unit_1 = out_call(attended, w_out, low_units[1:2], share_rows)
-    input_share = lax.dynamic_slice_in_dim(block_input, share_start, share_rows, 0).astype(F32)
-    middle_share, normed_one, inv_one = norm_forward(
-        deep_alpha * input_share + attn_share, w_norm[0], w_norm[1]
-    )
-    ffn_share, middle_low, hidden, act, pull, w_gateup, w_down = ffn_call(
-        middle_share.astype(BF16), (unit_0, unit_1), low_down
-    )
-    out_share, normed_two, inv_two = norm_forward(
-        deep_alpha * middle_share + ffn_share, w_norm[2], w_norm[3]
-    )
-    block_output = out_share.astype(BF16)
+    (
+        queries, key_rows, value_rows, attended, probs, cos_table, sin_table, w_qkv, w_out, w_gateup,
+        middle_share, middle_low, normed_one, inv_one,
+    ) = front_call(
+        block_input, low_qkv, low_out, low_gateup, positions, prefix_len, w_norm, share_rows, FRONT_SPANS
+    )
     matches = (cluster_id[:, None] == cluster_id[None, :]).astype(F32)
     counts = jnp.sum(matches, axis=1)
     group_counts = lax.dynamic_slice_in_dim(
@@ -1670,11 +1699,10 @@
     row_protein = (share_start + jnp.arange(share_rows)) // LEN
     one_hot = (row_protein[:, None] == jnp.arange(protein_count)[None, :]).astype(F32)
     row_weight = jnp.sum(one_hot * (1.0 / group_counts)[None, :], axis=1)
-    grad_output = cotangent.astype(F32) * row_weight[:, None]
-    grad_h2, grad_gain_two, grad_bias_two = norm_backward(
-        grad_output, normed_two, inv_two, w_norm[2]
-    )
-    ffn_grad, grad_gateup_rows = ffn_back_call(grad_h2.astype(BF16), act, pull, w_down)
+    block_output, grad_h2, grad_h2_low, terms_two, middle_low, hidden, act, pull, w_down = ffn_call(
+        middle_low, middle_share, w_gateup, low_down, cotangent, row_weight[:, None], w_norm
+    )
+    ffn_grad, grad_gateup_rows = ffn_back_call(grad_h2_low, act, pull, w_down)
     hidden = hidden.reshape(token_count, -1)
     middle_low = middle_low.reshape(token_count, D)
     ffn_grad = ffn_grad.reshape(token_count, D)
@@ -1687,19 +1715,15 @@
     grad_gateup_part = jnp.einsum(
         "jtf,td->jfd", gateup_rows, middle_low, preferred_element_type=F32
     ).astype(BF16)
-    middle_grad, red_gateup_0 = middle_back_call(
-        grad_gateup_rows, w_gateup, grad_gateup_part, SPANS[0], share_rows
-    )
-    middle_grad = middle_grad + deep_alpha * grad_h2
-    grad_h1, grad_gain_one, grad_bias_one = norm_backward(
-        middle_grad, normed_one, inv_one, w_norm[0]
-    )
-    grad_attended, grad_out_part, red_gateup_1 = out_back_call(
-        grad_h1.astype(BF16), w_out, attended, grad_gateup_part, SPANS[1]
+    grad_h1, grad_h1_low, terms_one, red_gateup_0, red_gateup_1 = middle_back_call(
+        grad_gateup_rows, w_gateup, grad_gateup_part, SPANS[:2], grad_h2, normed_one, inv_one, w_norm
+    )
+    grad_attended, grad_out_part, red_gateup_2 = out_back_call(
+        grad_h1_low, w_out, attended, grad_gateup_part, SPANS[2]
     )
     grad_attended = grad_attended.reshape(token_count, -1)
-    norm_terms = jnp.stack([grad_gain_one, grad_bias_one, grad_gain_two, grad_bias_two])
-    grad_proj, grad_norm, red_out, red_gateup_2 = attention_back_call(
+    norm_terms = jnp.concatenate([terms_one, terms_two])
+    grad_proj, grad_norm, red_out = attention_back_call(
         queries,
         key_rows,
         value_rows,
@@ -1710,15 +1734,12 @@
         sin_table,
         norm_terms,
         grad_out_part,
-        grad_gateup_part,
-        SPANS[2],
     )
     red_gateup = jnp.swapaxes(
         jnp.concatenate([red_gateup_0, red_gateup_1, red_gateup_2], axis=1), 1, 2
     )
     grad_qkv_part = jnp.einsum("td,jtc->jdc", block_input, grad_proj, preferred_element_type=F32).astype(BF16)
-    input_share_grad, red_qkv = input_back_call(grad_proj, w_qkv, grad_qkv_part, share_rows)
-    grad_input = (input_share_grad + deep_alpha * grad_h1).astype(BF16)
+    grad_input, red_qkv = input_back_call(grad_proj, w_qkv, grad_qkv_part, grad_h1)
 
     step_value = step_count[0].astype(F32)
     rate_qkv = D ** (-0.5)

time: 712 us -> 696 us (0.978)
  other arithmetic: 46.2 us -> 26.7 us
    reduce_sum x6 -> x0, other arithmetic: 15.4 us -> none  [the longest x2 9.36 us: norm_backward(): jnp.sum(grad_rows * normed, axis=0)]
    pallas_call x1, Pallas kernels: 60.7 us -> 75 us  [middle_back_call(): pl.pallas_call(kernel, out_shape=[jax.ShapeDtypeStruct((rows, D), F32), j...]
    pallas_call x1, Pallas kernels: 42.4 us -> 31.3 us  [attention_back_call(): pl.pallas_call(kernel, grid=(proteins, heads), in_specs=[tile] * 3 + [pl....]
    convert_element_type x4 -> x0, other arithmetic: 10.2 us -> none  [the longest x1 3.56 us: body_ring(): grad_input = (input_share_grad + deep_alpha * grad_h1).astype(BF16)]
    pallas_call x5 -> x3, Pallas kernels: 356 us -> 355 us  [the longest x1 171 us: front_call(): pl.pallas_call(kernel, out_shape=[jax.ShapeDtypeStruct((tokens, cols), BF...]
  transfers between devices with their start and end apart: 1 -> 1, of which waited for: 0 -> 0; matrix products, arithmetic and copies ran while one was open for 9% -> 8% of each run, Pallas kernels for 32% -> 33%
where the time goes in v4:
time: 696 us; the launch traced here: 685 us
  Pallas kernels  581 us (83%)
  matrix products  50.6 us (7%)
  other arithmetic  26.7 us (4%)
  between operations  15.2 us (2%)
  local copies, waits for them, and re-layouts  11.7 us (2%)
    pallas_call x1, Pallas kernels, front_call(): pl.pallas_call(kernel, out_shape=[jax.ShapeDtypeStruct((tokens, cols), BF...  171 us
    pallas_call x1, Pallas kernels, ffn_call(): pl.pallas_call(kernel, out_shape=[jax.ShapeDtypeStruct((rows, D), BF16),...  124 us
    pallas_call x1, Pallas kernels, middle_back_call(): pl.pallas_call(kernel, out_shape=[jax.ShapeDtypeStruct((rows, D), F32), j...  75 us
    pallas_call x1, Pallas kernels, out_back_call(): pl.pallas_call(kernel, out_shape=[jax.ShapeDtypeStruct((4, 2, rows, cols)...  63.5 us
    pallas_call x1, Pallas kernels, input_back_call(): pl.pallas_call(kernel, out_shape=[jax.ShapeDtypeStruct((rows, D), BF16),...  59.2 us
    pallas_call x1, Pallas kernels, ffn_back_call(): pl.pallas_call(kernel, out_shape=[jax.ShapeDtypeStruct((4, 2, rows, D), B...  56.2 us
    pallas_call x1, Pallas kernels, attention_back_call(): pl.pallas_call(kernel, grid=(proteins, heads), in_specs=[tile] * 3 + [pl....  31.3 us
    dot_general x1, matrix products, body_ring(): jnp.einsum('jtf,td->jfd', gateup_rows, middle_low, preferred_element_type...  22.7 us
  transfers between devices with their start and end apart: 1, of which 0 were waited for; matrix products, arithmetic and copies ran while one was open for 8% of the time, Pallas kernels for 33%

profile of v4, /device:TPU:0, one launch (start us, length us, event | category | flops | bytes accessed | tf_op | source)
XLA Modules:
  0.0 685.0 jit_solution(10082715420402860419)
XLA Ops:
  8.6 3.2 convert_bitcast_fusion.lg_ref
  11.9 2.3 reshape.101.pos_ref
  14.2 1.0 convert_element_type.42.low_ref
  17.3 0.9 convert_element_type.48.ld_ref
  18.2 171.4 %front.1 = (bf16[2688,256]{1,0:T(8,128)(2,1)}, bf16[2688,256]{1,0:T(8,128)(2,1)}, bf16[2688,256]{1,0:T(8,128)(2,1)}, bf16[2688,256]{1,0:T(8,128)(2,1)}, bf16[3,2...) custom-call(s32[3]{0:T(128)} %pre_ref.1, ...), custom_call_target="tpu_custom_call" | custom-call | flops 1048576 | bytes 65536 | tf_op jit(solution)/shard_map/front/pallas_call | solution.py:1032
  189.6 124.1 %ffn.1 = (bf16[336,2048]{1,0:T(8,128)(2,1)}, f32[336,2048]{1,0:T(8,128)}, bf16[336,2048]{1,0:T(8,128)(2,1)}, f32[2,2048]{1,0:T(2,128)}, bf16[4,2,336,2048]{3,2,1...) custom-call(bf16[336,2048]{1,0:T(8,128)(2,1)} %get-tuple-element.62., ...), custom_call_target="tpu_custom_call" | custom-call | flops 1048576 | bytes 65536 | tf_op jit(solution)/shard_map/ffn/pallas_call | solution.py:1313
  313.7 56.2 %ffn_back.1 = (bf16[4,2,336,2048]{3,2,1,0:T(8,128)(2,1)}, bf16[2,4,2,336,704]{4,3,2,1,0:T(8,128)(2,1)}) custom-call(bf16[336,2048]{1,0:T(8,128)(2,1)} %get-tuple-element.71.share, bf16[4,2,336,704]{3,2,1,0:T(8,128)(2,1)} %get-tuple-element.72.act_ref, bf16[4,2,336,704]{3,2,1,0:T(8,128)(2,1)} %get-tuple-element.73.pull_ref, ...), custom_call_target="tpu_custom_call" | custom-call | flops 1048576 | bytes 65536 | tf_op jit(solution)/shard_map/ffn_back/pallas_call | solution.py:1398
  369.9 13.6 %bitcast_convert_fusion = bf16[704,2048]{1,0:T(8,128)(2,1)} fusion(bf16[4,2,336,704]{3,2,1,0:T(8,128)(2,1)} %get-tuple-element.76, bf16[4,2,336,2048]{3,2,1,0:T(8,128)(2,1)} %get-tuple-element.77), kind=kOutput, calls=%fused_computation.2 | convolution fusion | flops 7752515584 | bytes 17678336 | tf_op jit(solution)/shard_map/tf,td->fd/dot_general | solution.py:1710
  383.5 22.7 %convolution_convert_fusion.gg_ref = bf16[2,704,2048]{2,1,0:T(8,128)(2,1)} fusion(bf16[2,2688,704]{2,1,0:T(8,128)(2,1)} %bitcast.34, bf16[2688,2048,1]{1,0,2:T(8,128)(2,1)} %bitcast.38), kind=kOutput, calls=%fused_computation.3 | convolution fusion | flops 15505031168 | bytes 24346624 | tf_op jit(solution)/shard_map/jtf,td->jfd/dot_general | solution.py:1715
  406.9 75.0 %middle_back.1 = (f32[336,2048]{1,0:T(8,128)}, bf16[336,2048]{1,0:T(8,128)(2,1)}, f32[2,2048]{1,0:T(2,128)}, f32[2,144,512]{2,1,0:T(8,128)}, f32[2,144,512]{2,1,0:T(8,128)}) custom-call(bf16[2,4,2,336,704]{4,3,2,1,0:T(8,128)(2,1)} %get-tuple-element.78.dg_ref, bf16[2,704,2048]{2,1,0:T(8,128)(2,1)} %get-tuple-element.64.wg_ref, ...), custom_call_target="tpu_custom_call" | custom-call | flops 1048576 | bytes 65536 | tf_op jit(solution)/shard_map/middle_back/pallas_call | solution.py:1492
  482.0 63.5 %out_back.1 = (bf16[4,2,336,256]{3,2,1,0:T(8,128)(2,1)}, bf16[256,2048]{1,0:T(8,128)(2,1)}, f32[2,416,512]{2,1,0:T(8,128)}) custom-call(bf16[336,2048]{1,0:T(8,128)(2,1)} %get-tuple-element.84.share, bf16[256,2048]{1,0:T(8,128)(2,1)} %get-tuple-element.85.w_ref, bf16[4,2,336,256]{3,2,1,0:T(8,128)(2,1)} %bitcast.35, ...), custom_call_target="tpu_custom_call" | custom-call | flops 1048576 | bytes 65536 | tf_op jit(solution)/shard_map/out_back/pallas_call | solution.py:1563
  546.1 31.3 %attention_back.1 = (bf16[3,2688,256]{2,1,0:T(8,128)(2,1)}, f32[4,2048]{1,0:T(4,128)}, f32[256,512]{1,0:T(8,128)}) custom-call(bf16[2688,256]{1,0:T(8,128)(2,1)} %get-tuple-element.66.q_ref, bf16[2688,256]{1,0:T(8,128)(2,1)} %get-tuple-element.67.k_ref, bf16[2688,256]{1,0:T(8,128)(2,1)} %get-tuple-element.68.v_ref, ...), custom_call_target="tpu_custom_call" | custom-call | flops 1048576 | bytes 65536 | tf_op jit(solution)/shard_map/attention_back/pallas_call | solution.py:1179
  577.4 14.4 %fusion.5.gq_ref = bf16[3,2048,256]{2,1,0:T(8,128)(2,1)} fusion(bf16[3,2688,256]{2,1,0:T(8,128)(2,1)} %get-tuple-element.92, bf16[2688,2048]{1,0:T(8,128)(2,1)} %param.21), kind=kOutput, calls=%fused_computation.6 | convolution fusion | flops 8457289728 | bytes 18284544 | tf_op jit(solution)/shard_map/td,jtc->jdc/dot_general | solution.py:1741
  591.9 59.2 %input_back.1 = (bf16[336,2048]{1,0:T(8,128)(2,1)}, f32[3,512,256]{2,1,0:T(8,128)}) custom-call(bf16[3,4,2,336,256]{4,3,2,1,0:T(8,128)(2,1)} %bitcast.36, bf16[3,2048,256]{2,1,0:T(8,128)(2,1)} %get-tuple-element.93.w_ref, bf16[3,2048,256]{2,1,0:T(8,128)(2,1)} %fusion.5.gq_ref, f32[336,2048]{1,0:T(8,128)} %get-tuple-element.94.dh_ref), custom_call_target="tpu_custom_call" | custom-call | flops 1048576 | bytes 65536 | tf_op jit(solution)/shard_map/input_back/pallas_call | solution.py:1628
  651.1 3.1 multiply_subtract_fusion.3
  654.2 1.5 add_subtract_fusion
  655.7 4.5 multiply_subtract_fusion.1
  660.2 1.2 copy-done.6
  661.9 4.8 multiply_subtract_fusion
  666.7 4.7 multiply_subtract_fusion.2
  671.4 1.1 copy.66
  673.3 1.1 copy.67
  674.3 0.8 copy-done.3
  675.2 1.1 copy.68
  (56 shorter events, 7.2 us)
Async XLA Ops:
  7.2 659.5 %reduce-scatter.2.cloned.1.call-start = ((), (), s32[]{:S(2)}) async-start(), calls=%async_computation.1 | async-start | bytes 3604480 | tf_op jit(solution)/shard_map/reduce_scatter | solution.py:1711
  8.6 3.2 copy-start.20
  8.6 5.5 copy-start.1
  14.2 1.2 copy-start.7
  14.2 1.9 copy-start.21
  14.2 3.1 copy-start.4
  481.9 63.5 %copy-start.18 = (f32[2,2048]{1,0:T(2,128)S(1)}, f32[2,2048]{1,0:T(2,128)}, u32[]{:S(2)}) copy-start(f32[2,2048]{1,0:T(2,128)} %get-tuple-element.90) | copy-start | bytes 49156
  481.9 63.5 %copy-start.19 = (f32[2,2048]{1,0:T(2,128)S(1)}, f32[2,2048]{1,0:T(2,128)}, u32[]{:S(2)}) copy-start(f32[2,2048]{1,0:T(2,128)} %get-tuple-element.89) | copy-start | bytes 49156
  591.9 62.3 %copy-start.16 = (f32[4,2048]{1,0:T(4,128)S(1)}, f32[4,2048]{1,0:T(4,128)}, u32[]{:S(2)}) copy-start(f32[4,2048]{1,0:T(4,128)} %param.39) | copy-start | bytes 98308
  591.9 62.3 %copy-start.17 = (f32[4,2048]{1,0:T(4,128)S(1)}, f32[4,2048]{1,0:T(4,128)}, u32[]{:S(2)}) copy-start(f32[4,2048]{1,0:T(4,128)} %get-tuple-element.159) | copy-start | bytes 98308
  651.1 4.6 copy-start.2
  651.1 4.6 copy-start.10
  651.1 9.1 %copy-start.15 = (f32[2,144,512]{2,1,0:T(8,128)S(1)}, f32[2,144,512]{2,1,0:T(8,128)}, u32[]{:S(2)}) copy-start(f32[2,144,512]{2,1,0:T(8,128)} %get-tuple-element.99) | copy-start | bytes 1769476
  655.6 4.5 copy-start
  655.6 4.5 copy-start.5
  655.7 5.7 copy-start.6
  655.7 6.1 copy-start.9
  655.7 6.2 copy-start.14
  661.9 4.8 copy-start.11
  666.7 4.7 copy-start.12
  671.4 1.8 copy-start.13
  673.3 1.9 copy-start.3
  675.2 1.4 copy-start.8
Sparse Core Ops, SparseCore 0:
  383.6 82.6 reduce-scatter.1

commit v5 on v4

--- a/solution.py
+++ b/solution.py
@@ -839,7 +839,7 @@
     return pl.BlockSpec(shape, lambda *_: (0,) * len(shape))
 
 
-def front_call(block_input, low_qkv, low_out, low_gateup, positions, prefix_len, w_norm, rows, spans):
+def front_call(block_input, low_qkv, low_out, gateup, positions, prefix_len, w_norm, rows, spans):
     tokens, width = block_input.shape
     depth, cols = low_qkv.shape[1:]
     tiles = tokens // rows
@@ -850,12 +850,13 @@
     half = depth // 2
     out_half = cols // 2
     span = spans[-1][0] + spans[-1][1]
+    live = gateup.shape[1]
 
     def kernel(
         pre_ref, x_ref, low_ref, lo_ref, lg_ref, pos_ref, norm_ref,
         q_ref, k_ref, v_ref, o_ref, p_ref, cos_ref, sin_ref, w_ref, wo_ref, wg_ref,
         x1_ref, x1b_ref, n1_ref, inv_ref,
-        x_buf, w_buf, acc, q_buf, k_buf, v_buf, o_buf, cos_buf, sin_buf, p_buf, wo_buf, xs_buf,
+        x_buf, w_buf, acc, q_buf, k_buf, v_buf, o_buf, cos_buf, sin_buf, p_buf, wo_buf, xs_buf, wide_g, low_g,
         rcore, rxd, ryd, rx, ry, xsem, psem, ksem, send, recv, lsem, zsend, zrecv, zlocal,
     ):
         ring = Ring(zsend, zrecv, zlocal)
@@ -873,11 +874,12 @@
                 RingGather(
                     ring,
                     12 + 6 * n,
-                    lambda h, at=at: lg_ref.at[h, at, :],
+                    lambda h, at=at: low_g.at[h, at, :],
                     plane_columns(depth)(wg_ref.at[:, at, :]),
                 )
             )
         own_rows = pltpu.make_async_copy(x_ref.at[sems.own, sems.core], xs_buf, xsem.at[8])
+        load_g = pltpu.make_async_copy(lg_ref, wide_g, xsem.at[9])
         kept = ((q_buf, q_ref), (k_buf, k_ref), (v_buf, v_ref), (cos_buf, cos_ref), (sin_buf, sin_ref))
         keeps = [pltpu.make_async_copy(src, dst, ksem.at[n]) for n, (src, dst) in enumerate(kept)]
         keep_w = pltpu.make_async_copy(w_buf, w_ref, ksem.at[5])
@@ -893,6 +895,7 @@
 
         lax.fori_loop(0, tiles, start_tile, 0)
         own_rows.start()
+        load_g.start()
         greet(sems.others + [{"dp": ring.left}, {"dp": ring.right}])
         gather.start()
         for copy in gather.own:
@@ -914,21 +917,32 @@
             return carry
 
         lax.fori_loop(0, tiles, own_tile, 0)
-        lane = lax.broadcasted_iota(jnp.int32, (1, HEAD_DIM), 1)
-        ladder = (lane % (HEAD_DIM // 2)).astype(F32)
+        rung = lax.broadcasted_iota(jnp.int32, (HEAD_DIM, 1), 0)
+        ladder = (rung % (HEAD_DIM // 2)).astype(F32)
         inverse = jnp.exp(ladder * (-2.0 * math.log(10000.0) / HEAD_DIM))
-        sign = jnp.where(lane < HEAD_DIM // 2, -1.0, 1.0)
-
-        def table_tile(t, carry):
-            angles = pos_ref[t].astype(F32) * inverse
-            cos_buf[tile_rows(t), :] = jnp.cos(angles)
-            sin_buf[tile_rows(t), :] = jnp.sin(angles) * sign
+        sign = jnp.where(rung < HEAD_DIM // 2, -1.0, 1.0)
+
+        def table_tile(b, carry):
+            angles = inverse * pos_ref[pl.ds(b, 1), :].astype(F32)
+            here = pl.ds(pl.multiple_of(b * HEAD_DIM, HEAD_DIM), HEAD_DIM)
+            cos_buf[here, :] = jnp.cos(angles).T
+            sin_buf[here, :] = (jnp.sin(angles) * sign).T
             return carry
 
-        lax.fori_loop(0, tiles // 2, table_tile, 0)
+        blocks = tokens // HEAD_DIM
+        lax.fori_loop(0, blocks // 2, table_tile, 0)
         gather.forward()
         gather_out.start()
-        lax.fori_loop(tiles // 2, tiles, table_tile, 0)
+        lax.fori_loop(blocks // 2, blocks, table_tile, 0)
+        load_g.wait()
+
+        def round_rows(i, carry):
+            here = pl.ds(pl.multiple_of(i * 16, 16), 16)
+            for h in range(2):
+                low_g[h, here, :] = wide_g[h, here, :].astype(BF16)
+            return carry
+
+        lax.fori_loop(0, live // 16, round_rows, 0)
         gather.near()
 
         def near_tile(t, carry):
@@ -1056,10 +1070,12 @@
             pltpu.VMEM((heads, LEN, LEN), BF16),
             pltpu.VMEM((cols, width), BF16),
             pltpu.VMEM((rows, width), BF16),
+            pltpu.VMEM(gateup.shape, F32),
+            pltpu.VMEM(gateup.shape, BF16),
         ]
         + scatter_scratch(rows, width, False)
         + [
-            pltpu.SemaphoreType.DMA((9,)),
+            pltpu.SemaphoreType.DMA((10,)),
             pltpu.SemaphoreType.DMA((heads,)),
             pltpu.SemaphoreType.DMA((8,)),
         ]
@@ -1073,8 +1089,8 @@
         block_input.reshape(4, 2, rows, width),
         low_qkv,
         low_out,
-        low_gateup,
-        positions.reshape(tiles, rows, 1),
+        gateup,
+        positions.reshape(tokens // HEAD_DIM, HEAD_DIM),
         w_norm,
     )
 
@@ -1304,7 +1320,7 @@
             ring=ring,
             start=gather_d.start,
             first=load_g.wait,
-            later=gather_d.forward,
+            early=gather_d.forward,
             between=between,
             end=end,
         )
@@ -1584,26 +1600,43 @@
     )(attn_grad, w_out, attended.reshape(4, 2, rows, cols), grad_gateup_part)
 
 
-def input_back_call(grad_proj, w_qkv, grad_qkv_part, grad_h1):
+def input_back_call(grad_proj, w_qkv, block_input, grad_gateup_part, span, grad_h1):
     rows = grad_h1.shape[0]
     alpha = math.sqrt(2.0 * DEPTH)
     width, cols = w_qkv.shape[1:]
     depth = width // 4
+    tokens = block_input.shape[0]
 
     def kernel(
-        da_ref, w_ref, gq_ref, dh_ref, out, red_q,
-        w_buf, buf_q, pbuf, rcore, rxd, ryd, rx, ry, wsem, send, recv, lsem, zsend, zrecv, zlocal,
+        da_ref, w_ref, x_ref, gg_ref, dh_ref, out, red_q, red_g,
+        w_buf, x_buf, gq_buf, buf_q, buf_g, pbuf, rcore, rxd, ryd, rx, ry,
+        wsem, send, recv, lsem, zsend, zrecv, zlocal,
     ):
         ring = Ring(zsend, zrecv, zlocal)
         half = depth // 2
-        side = RingScatter(
-            ring, 0, row_halves(depth)(gq_ref), buf_q, lambda h: red_q.at[:, pl.ds(h * half, half), :]
+        side_g = span_scatter(ring, 0, gg_ref, span, buf_g, red_g)
+        side_q = RingScatter(
+            ring, 6, row_halves(depth)(gq_buf), buf_q, lambda h: red_q.at[:, pl.ds(h * half, half), :]
         )
         weight = pltpu.make_async_copy(w_ref, w_buf, wsem.at[0])
+        load = pltpu.make_async_copy(x_ref, x_buf, wsem.at[1])
+        load.start()
         weight.start()
 
+        def product(n, carry):
+            depths = pl.ds(pl.multiple_of(n * depth, depth), depth)
+            left = x_buf[:, :, :, depths].reshape(tokens, depth)
+            for j in range(3):
+                right = da_ref[j].reshape(tokens, cols)
+                gq_buf[j, depths, :] = lax.dot_general(left, right, TN, preferred_element_type=F32).astype(BF16)
+            return carry
+
         def start():
-            side.start()
+            side_g.start()
+            load.wait()
+            lax.fori_loop(0, 4, product, 0)
+            side_g.forward()
+            side_q.start()
             weight.wait()
 
         def compute(t, chip, which):
@@ -1614,6 +1647,10 @@
 
         def emit(at, value):
             out[at, :] = (value + alpha * dh_ref[at, :]).astype(BF16)
+
+        def end():
+            side_g.finish()
+            side_q.finish()
 
         square_kernel(
             rows,
@@ -1621,8 +1658,8 @@
             scatter=(compute, pbuf, (rcore, rxd, ryd, rx, ry), emit),
             ring=ring,
             start=start,
-            middle=side.forward,
-            end=side.finish,
+            middle=side_q.forward,
+            end=end,
         )
 
     return pl.pallas_call(
@@ -1630,25 +1667,35 @@
         out_shape=[
             jax.ShapeDtypeStruct((rows, D), BF16),
             jax.ShapeDtypeStruct((3, depth, cols), F32),
+            jax.ShapeDtypeStruct((2, span[1], depth), F32),
         ],
-        in_specs=[VM, ANY, ANY, VM],
-        out_specs=[VM, VM],
+        in_specs=[VM, ANY, ANY, ANY, VM],
+        out_specs=[VM, VM, VM],
         scratch_shapes=[
             pltpu.VMEM((3, D, cols), BF16),
+            pltpu.VMEM((4, 2, rows, width), BF16),
+            pltpu.VMEM((3, width, cols), BF16),
             pltpu.VMEM((10, 3, depth // 2, cols), BF16),
+            pltpu.VMEM((10, span[1], depth), BF16),
         ]
         + scatter_scratch(rows, D)
-        + [pltpu.SemaphoreType.DMA((1,))]
+        + [pltpu.SemaphoreType.DMA((2,))]
         + SEMS
-        + ring_sems(6),
+        + ring_sems(12),
         compiler_params=params(4),
         cost_estimate=LIGHT,
         name="input_back",
-    )(grad_proj.reshape(3, 4, 2, rows, cols), w_qkv, grad_qkv_part, grad_h1)
+    )(
+        grad_proj.reshape(3, 4, 2, rows, cols),
+        w_qkv,
+        block_input.reshape(4, 2, rows, width),
+        grad_gateup_part,
+        grad_h1,
+    )
 
 
 FRONT_SPANS = ((0, 240), (240, 464))
-SPANS = ((0, 144), (144, 144), (288, 416))
+SPANS = ((0, 96), (96, 112), (208, 384), (592, 112))
 
 
 def body_ring(
@@ -1681,7 +1728,6 @@
 
     low_qkv = master_qkv.astype(BF16)
     low_out = master_out.astype(BF16)
-    low_gateup = jnp.swapaxes(master_gateup, 1, 2).astype(BF16)
     low_down = master_down.astype(BF16)
     w_norm = lax.optimization_barrier(master_norm.astype(BF16)).astype(F32)
 
@@ -1689,7 +1735,7 @@
         queries, key_rows, value_rows, attended, probs, cos_table, sin_table, w_qkv, w_out, w_gateup,
         middle_share, middle_low, normed_one, inv_one,
     ) = front_call(
-        block_input, low_qkv, low_out, low_gateup, positions, prefix_len, w_norm, share_rows, FRONT_SPANS
+        block_input, low_qkv, low_out, jnp.swapaxes(master_gateup, 1, 2), positions, prefix_len, w_norm, share_rows, FRONT_SPANS
     )
     matches = (cluster_id[:, None] == cluster_id[None, :]).astype(F32)
     counts = jnp.sum(matches, axis=1)
@@ -1735,11 +1781,12 @@
         norm_terms,
         grad_out_part,
     )
+    grad_input, red_qkv, red_gateup_3 = input_back_call(
+        grad_proj, w_qkv, block_input, grad_gateup_part, SPANS[3], grad_h1
+    )
     red_gateup = jnp.swapaxes(
-        jnp.concatenate([red_gateup_0, red_gateup_1, red_gateup_2], axis=1), 1, 2
-    )
-    grad_qkv_part = jnp.einsum("td,jtc->jdc", block_input, grad_proj, preferred_element_type=F32).astype(BF16)
-    grad_input, red_qkv = input_back_call(grad_proj, w_qkv, grad_qkv_part, grad_h1)
+        jnp.concatenate([red_gateup_0, red_gateup_1, red_gateup_2, red_gateup_3], axis=1), 1, 2
+    )
 
     step_value = step_count[0].astype(F32)
     rate_qkv = D ** (-0.5)

time: 696 us -> 673 us (0.967)
  matrix products: 50.6 us -> 36.2 us
    pallas_call x1, Pallas kernels: 59.2 us -> 76.6 us  [input_back_call(): pl.pallas_call(kernel, out_shape=[jax.ShapeDtypeStruct((rows, D), BF16),...]
    dot_general x1 -> x0, matrix products: 14.4 us -> none  [body_ring(): jnp.einsum('td,jtc->jdc', block_input, grad_proj, preferred_element_type=...]
    pallas_call x1, Pallas kernels: 75 us -> 65.1 us  [middle_back_call(): pl.pallas_call(kernel, out_shape=[jax.ShapeDtypeStruct((rows, D), F32), j...]
  transfers between devices with their start and end apart: 1 -> 1, of which waited for: 0 -> 0; matrix products, arithmetic and copies ran while one was open for 8% -> 6% of each run, Pallas kernels for 33% -> 35%
where the time goes in v5:
time: 673 us; the launch traced here: 664 us
  Pallas kernels  579 us (86%)
  matrix products  36.2 us (5%)
  other arithmetic  25.1 us (4%)
  between operations  15.5 us (2%)
  local copies, waits for them, and re-layouts  8.23 us (1%)
    pallas_call x1, Pallas kernels, front_call(): pl.pallas_call(kernel, out_shape=[jax.ShapeDtypeStruct((tokens, cols), BF...  171 us
    pallas_call x1, Pallas kernels, ffn_call(): pl.pallas_call(kernel, out_shape=[jax.ShapeDtypeStruct((rows, D), BF16),...  121 us
    pallas_call x1, Pallas kernels, input_back_call(): pl.pallas_call(kernel, out_shape=[jax.ShapeDtypeStruct((rows, D), BF16),...  76.6 us
    pallas_call x1, Pallas kernels, middle_back_call(): pl.pallas_call(kernel, out_shape=[jax.ShapeDtypeStruct((rows, D), F32), j...  65.1 us
    pallas_call x1, Pallas kernels, out_back_call(): pl.pallas_call(kernel, out_shape=[jax.ShapeDtypeStruct((4, 2, rows, cols)...  57.6 us
    pallas_call x1, Pallas kernels, ffn_back_call(): pl.pallas_call(kernel, out_shape=[jax.ShapeDtypeStruct((4, 2, rows, D), B...  55.1 us
    pallas_call x1, Pallas kernels, attention_back_call(): pl.pallas_call(kernel, grid=(proteins, heads), in_specs=[tile] * 3 + [pl....  32.8 us
    dot_general x1, matrix products, body_ring(): jnp.einsum('jtf,td->jfd', gateup_rows, middle_low, preferred_element_type...  22.7 us
  transfers between devices with their start and end apart: 1, of which 0 were waited for; matrix products, arithmetic and copies ran while one was open for 6% of the time, Pallas kernels for 35%

profile of v5, /device:TPU:0, one launch (start us, length us, event | category | flops | bytes accessed | tf_op | source)
XLA Modules:
  0.0 664.3 jit_solution(3024011920601665012)
XLA Ops:
  7.3 0.8 convert_element_type.34
  8.7 2.5 convert_element_type.32.low_ref
  11.2 0.7 convert_element_type.33.lo_ref
  12.3 0.8 broadcast_in_dim.3.rw_ref
  13.1 0.9 convert_element_type.36.ld_ref
  14.0 170.9 %front.1 = (bf16[2688,256]{1,0:T(8,128)(2,1)}, bf16[2688,256]{1,0:T(8,128)(2,1)}, bf16[2688,256]{1,0:T(8,128)(2,1)}, bf16[2688,256]{1,0:T(8,128)(2,1)}, bf16[3,2...) custom-call(s32[3]{0:T(128)} %pre_ref.1, ...), custom_call_target="tpu_custom_call" | custom-call | flops 1048576 | bytes 65536 | tf_op jit(solution)/shard_map/front/pallas_call | solution.py:1046
  184.9 121.1 %ffn.1 = (bf16[336,2048]{1,0:T(8,128)(2,1)}, f32[336,2048]{1,0:T(8,128)}, bf16[336,2048]{1,0:T(8,128)(2,1)}, f32[2,2048]{1,0:T(2,128)}, bf16[4,2,336,2048]{3,2,1...) custom-call(bf16[336,2048]{1,0:T(8,128)(2,1)} %get-tuple-element.63., ...), custom_call_target="tpu_custom_call" | custom-call | flops 1048576 | bytes 65536 | tf_op jit(solution)/shard_map/ffn/pallas_call | solution.py:1329
  306.0 55.1 %ffn_back.1 = (bf16[4,2,336,2048]{3,2,1,0:T(8,128)(2,1)}, bf16[2,4,2,336,704]{4,3,2,1,0:T(8,128)(2,1)}) custom-call(bf16[336,2048]{1,0:T(8,128)(2,1)} %get-tuple-element.72.share, bf16[4,2,336,704]{3,2,1,0:T(8,128)(2,1)} %get-tuple-element.73.act_ref, bf16[4,2,336,704]{3,2,1,0:T(8,128)(2,1)} %get-tuple-element.74.pull_ref, ...), custom_call_target="tpu_custom_call" | custom-call | flops 1048576 | bytes 65536 | tf_op jit(solution)/shard_map/ffn_back/pallas_call | solution.py:1414
  361.0 13.6 %bitcast_convert_fusion = bf16[704,2048]{1,0:T(8,128)(2,1)} fusion(bf16[4,2,336,704]{3,2,1,0:T(8,128)(2,1)} %get-tuple-element.77, bf16[4,2,336,2048]{3,2,1,0:T(8,128)(2,1)} %get-tuple-element.78), kind=kOutput, calls=%fused_computation | convolution fusion | flops 7752515584 | bytes 17678336 | tf_op jit(solution)/shard_map/tf,td->fd/dot_general | solution.py:1756
  375.4 22.7 %convolution_convert_fusion.gg_ref = bf16[2,704,2048]{2,1,0:T(8,128)(2,1)} fusion(bf16[2,2688,704]{2,1,0:T(8,128)(2,1)} %bitcast.26, bf16[2688,2048,1]{1,0,2:T(8,128)(2,1)} %bitcast.31), kind=kOutput, calls=%fused_computation.1 | convolution fusion | flops 15505031168 | bytes 24346624 | tf_op jit(solution)/shard_map/jtf,td->jfd/dot_general | solution.py:1761
  398.0 65.1 %middle_back.1 = (f32[336,2048]{1,0:T(8,128)}, bf16[336,2048]{1,0:T(8,128)(2,1)}, f32[2,2048]{1,0:T(2,128)}, f32[2,96,512]{2,1,0:T(8,128)}, f32[2,112,512]{2,1,0:T(8,128)}) custom-call(bf16[2,4,2,336,704]{4,3,2,1,0:T(8,128)(2,1)} %get-tuple-element.79.dg_ref, bf16[2,704,2048]{2,1,0:T(8,128)(2,1)} %get-tuple-element.65.wg_ref, ...), custom_call_target="tpu_custom_call" | custom-call | flops 1048576 | bytes 65536 | tf_op jit(solution)/shard_map/middle_back/pallas_call | solution.py:1508
  463.2 57.6 %out_back.1 = (bf16[4,2,336,256]{3,2,1,0:T(8,128)(2,1)}, bf16[256,2048]{1,0:T(8,128)(2,1)}, f32[2,384,512]{2,1,0:T(8,128)}) custom-call(bf16[336,2048]{1,0:T(8,128)(2,1)} %get-tuple-element.85.share, bf16[256,2048]{1,0:T(8,128)(2,1)} %get-tuple-element.86.w_ref, bf16[4,2,336,256]{3,2,1,0:T(8,128)(2,1)} %bitcast.27, ...), custom_call_target="tpu_custom_call" | custom-call | flops 1048576 | bytes 65536 | tf_op jit(solution)/shard_map/out_back/pallas_call | solution.py:1579
  521.4 32.8 %attention_back.1 = (bf16[3,2688,256]{2,1,0:T(8,128)(2,1)}, f32[4,2048]{1,0:T(4,128)}, f32[256,512]{1,0:T(8,128)}) custom-call(bf16[2688,256]{1,0:T(8,128)(2,1)} %get-tuple-element.67.q_ref, bf16[2688,256]{1,0:T(8,128)(2,1)} %get-tuple-element.68.k_ref, bf16[2688,256]{1,0:T(8,128)(2,1)} %get-tuple-element.69.v_ref, ...), custom_call_target="tpu_custom_call" | custom-call | flops 1048576 | bytes 65536 | tf_op jit(solution)/shard_map/attention_back/pallas_call | solution.py:1195
  554.3 76.6 %input_back.1 = (bf16[336,2048]{1,0:T(8,128)(2,1)}, f32[3,512,256]{2,1,0:T(8,128)}, f32[2,112,512]{2,1,0:T(8,128)}) custom-call(bf16[3,4,2,336,256]{4,3,2,1,0:T(8,128)(2,1)} %bitcast.28, bf16[3,2048,256]{2,1,0:T(8,128)(2,1)} %get-tuple-element.94.w_ref, bf16[4,2,336,2048]{3,2,1,0:T(8,128)(2,1)} %bitcast.24, ...), custom_call_target="tpu_custom_call" | custom-call | flops 1048576 | bytes 65536 | tf_op jit(solution)/shard_map/input_back/pallas_call | solution.py:1665
  631.0 2.9 multiply_subtract_fusion.3
  634.7 4.9 multiply_subtract_fusion.1
  639.7 1.2 copy-done.5
  641.3 4.9 multiply_subtract_fusion
  646.2 5.1 multiply_subtract_fusion.2
  651.3 1.1 copy.56
  652.4 0.8 copy-done.10
  653.1 1.1 copy.57
  654.2 1.1 copy.58
  655.6 0.8 copy.59
  (53 shorter events, 3.7 us)
Async XLA Ops:
  7.2 4.0 copy-start.6
  7.2 639.0 %reduce-scatter.2.cloned.1.call-start = ((), (), s32[]{:S(2)}) async-start(), calls=%async_computation.1 | async-start | bytes 3604480 | tf_op jit(solution)/shard_map/reduce_scatter | solution.py:1757
  8.7 3.2 copy-start.21
  8.7 4.4 copy-start.3
  463.1 57.6 %copy-start.19 = (f32[2,2048]{1,0:T(2,128)S(1)}, f32[2,2048]{1,0:T(2,128)}, u32[]{:S(2)}) copy-start(f32[2,2048]{1,0:T(2,128)} %get-tuple-element.91) | copy-start | bytes 49156
  463.1 57.6 %copy-start.20 = (f32[2,2048]{1,0:T(2,128)S(1)}, f32[2,2048]{1,0:T(2,128)}, u32[]{:S(2)}) copy-start(f32[2,2048]{1,0:T(2,128)} %get-tuple-element.90) | copy-start | bytes 49156
  630.9 3.0 copy-start.14
  631.0 3.0 copy-start.15
  631.0 3.0 copy-start.17
  631.0 3.0 copy-start.18
  631.0 3.7 copy-start.1
  631.0 3.6 copy-start.2
  631.0 8.6 %copy-start.13 = (f32[2,96,512]{2,1,0:T(8,128)S(1)}, f32[2,96,512]{2,1,0:T(8,128)}, u32[]{:S(2)}) copy-start(f32[2,96,512]{2,1,0:T(8,128)} %get-tuple-element.99) | copy-start | bytes 1179652
  634.0 5.7 copy-start.12
  634.7 5.0 copy-start
  634.7 5.0 copy-start.4
  634.7 6.2 copy-start.5
  634.7 6.6 copy-start.8
  634.7 6.6 copy-start.11
  646.2 5.1 copy-start.9
  651.3 1.8 copy-start.10
  654.2 1.4 copy-start.7
  654.2 2.2 copy-start.16
Sparse Core Ops, SparseCore 0:
  374.7 82.9 reduce-scatter.1

commit v6 on v5

--- a/solution.py
+++ b/solution.py
@@ -350,7 +350,7 @@
 VMEM_BYTES = 61 * 1024 * 1024
 BF16 = jnp.bfloat16
 F32 = jnp.float32
-EMIT = 48
+EMIT = 112
 NT = (((1,), (1,)), ((), ()))
 ANY = pl.BlockSpec(memory_space=pl.ANY)
 VM = pl.BlockSpec(memory_space=pltpu.VMEM)
@@ -451,11 +451,22 @@
             self.minus_sum,
         )
 
-    def start(self):
-        for copy in self.remote[:4]:
-            copy.start()
+    def start_far(self):
+        self.plus_far.start()
+        self.minus_far.start()
+
+    def start_near(self):
+        self.plus_near.start()
+        self.minus_near.start()
+
+    def load(self):
         for copy in self.loads:
             copy.start()
+
+    def start(self):
+        self.start_far()
+        self.start_near()
+        self.load()
 
     def forward(self):
         for copy in self.loads:
@@ -608,6 +619,7 @@
     later=nothing,
     between=nothing,
     halfway=nothing,
+    half=4,
     middle=nothing,
     end=nothing,
     near_first=False,
@@ -719,7 +731,7 @@
             rel = (t // 2 + 1) % 4
             chip, which = place(rel, turn)
 
-            @pl.when(t == 4)
+            @pl.when(t == half)
             def _():
                 halfway()
 
@@ -1096,6 +1108,7 @@
 
 
 BLOCK = 128
+BACK_BLOCK = 448
 TN = (((0,), (0,)), ((), ()))
 
 
@@ -1113,7 +1126,7 @@
     def kernel(
         q_ref, k_ref, v_ref, p_ref, o_ref, do_ref, cos_ref, sin_ref, nt_ref, go_ref,
         da_ref, norm_ref, red_o,
-        dk_acc, dv_acc, sums, got, nsend, nrecv, buf_o, send, recv, local,
+        ds_buf, sums, got, nsend, nrecv, buf_o, send, recv, local,
     ):
         step = pl.program_id(0) * heads + pl.program_id(1)
         ring = Ring(send, recv, local)
@@ -1163,28 +1176,20 @@
         def _():
             side.forward()
 
-        for i in range(LEN // BLOCK):
-            rows = slice(i * BLOCK, (i + 1) * BLOCK)
+        for i in range(LEN // BACK_BLOCK):
+            rows = slice(i * BACK_BLOCK, (i + 1) * BACK_BLOCK)
             do = do_ref[rows, :]
-            p = p_ref[0, 0, rows, :]
             delta = jnp.sum(do.astype(F32) * o_ref[rows, :].astype(F32), axis=-1, keepdims=True)
             dp = nt_dot(do, v_ref[...])
-            ds = (p.astype(F32) * (dp - delta)).astype(BF16)
-            dv = lax.dot_general(p, do, TN, preferred_element_type=F32)
-            dk = lax.dot_general(ds, q_ref[rows, :], TN, preferred_element_type=F32)
-            if i == 0:
-                dv_acc[...] = dv
-                dk_acc[...] = dk
-            else:
-                dv_acc[...] += dv
-                dk_acc[...] += dk
+            ds = (p_ref[0, 0, rows, :].astype(F32) * (dp - delta)).astype(BF16)
+            ds_buf[rows, :] = ds
             dq = jnp.dot(ds, k_ref[...], preferred_element_type=F32)
             turned = dq * cos_ref[rows, :] - pltpu.roll(dq, HEAD_DIM // 2, 1) * sin_ref[rows, :]
             da_ref[0, rows, :] = (turned * scale).astype(BF16)
-        dk = dk_acc[...]
+        da_ref[2] = lax.dot_general(p_ref[0, 0], do_ref[...], TN, preferred_element_type=F32).astype(BF16)
+        dk = lax.dot_general(ds_buf[...], q_ref[...], TN, preferred_element_type=F32)
         turned = dk * cos_ref[...] - pltpu.roll(dk, HEAD_DIM // 2, 1) * sin_ref[...]
         da_ref[1] = turned.astype(BF16)
-        da_ref[2] = dv_acc[...].astype(BF16)
 
         @pl.when(step == last)
         def _():
@@ -1209,8 +1214,7 @@
             jax.ShapeDtypeStruct((cols, depth), F32),
         ],
         scratch_shapes=[
-            pltpu.VMEM((LEN, HEAD_DIM), F32),
-            pltpu.VMEM((LEN, HEAD_DIM), F32),
+            pltpu.VMEM((LEN, LEN), BF16),
             pltpu.VMEM((5,) + norm_terms.shape, F32),
             pltpu.VMEM((5,) + norm_terms.shape, F32),
             pltpu.SemaphoreType.DMA((5,)),
@@ -1623,21 +1627,27 @@
         load.start()
         weight.start()
 
-        def product(n, carry):
+        def product(n):
             depths = pl.ds(pl.multiple_of(n * depth, depth), depth)
             left = x_buf[:, :, :, depths].reshape(tokens, depth)
             for j in range(3):
                 right = da_ref[j].reshape(tokens, cols)
                 gq_buf[j, depths, :] = lax.dot_general(left, right, TN, preferred_element_type=F32).astype(BF16)
-            return carry
 
         def start():
             side_g.start()
             load.wait()
-            lax.fori_loop(0, 4, product, 0)
+            product(ring.far)
+            side_q.start_far()
+            weight.wait()
+
+        def halfway():
+            product(ring.right)
+            product(ring.left)
+            side_q.start_near()
             side_g.forward()
-            side_q.start()
-            weight.wait()
+            product(ring.here)
+            side_q.load()
 
         def compute(t, chip, which):
             part = nt_dot(da_ref[0, chip, which], w_buf[0])
@@ -1658,6 +1668,8 @@
             scatter=(compute, pbuf, (rcore, rxd, ryd, rx, ry), emit),
             ring=ring,
             start=start,
+            halfway=halfway,
+            half=2,
             middle=side_q.forward,
             end=end,
         )

time: 673 us -> 670 us (level)
  no operation moved by 1% of the time
where the time goes in v6:
time: 670 us; the launch traced here: 661 us
  Pallas kernels  575 us (86%)
  matrix products  36.6 us (5%)
  other arithmetic  25.1 us (4%)
  between operations  15.2 us (2%)
  local copies, waits for them, and re-layouts  8.23 us (1%)
    pallas_call x1, Pallas kernels, front_call(): pl.pallas_call(kernel, out_shape=[jax.ShapeDtypeStruct((tokens, cols), BF...  171 us
    pallas_call x1, Pallas kernels, ffn_call(): pl.pallas_call(kernel, out_shape=[jax.ShapeDtypeStruct((rows, D), BF16),...  120 us
    pallas_call x1, Pallas kernels, input_back_call(): pl.pallas_call(kernel, out_shape=[jax.ShapeDtypeStruct((rows, D), BF16),...  74.4 us
    pallas_call x1, Pallas kernels, middle_back_call(): pl.pallas_call(kernel, out_shape=[jax.ShapeDtypeStruct((rows, D), F32), j...  64.8 us
    pallas_call x1, Pallas kernels, out_back_call(): pl.pallas_call(kernel, out_shape=[jax.ShapeDtypeStruct((4, 2, rows, cols)...  57.8 us
    pallas_call x1, Pallas kernels, ffn_back_call(): pl.pallas_call(kernel, out_shape=[jax.ShapeDtypeStruct((4, 2, rows, D), B...  55.1 us
    pallas_call x1, Pallas kernels, attention_back_call(): pl.pallas_call(kernel, grid=(proteins, heads), in_specs=[tile] * 3 + [pl....  32.1 us
    dot_general x1, matrix products, body_ring(): jnp.einsum('jtf,td->jfd', gateup_rows, middle_low, preferred_element_type...  23.1 us
  transfers between devices with their start and end apart: 1, of which 0 were waited for; matrix products, arithmetic and copies ran while one was open for 6% of the time, Pallas kernels for 35%

profile of v6, /device:TPU:0, one launch (start us, length us, event | category | flops | bytes accessed | tf_op | source)
XLA Modules:
  0.0 660.6 jit_solution(15341310920853987894)
XLA Ops:
  7.3 0.8 convert_element_type.34
  8.7 2.5 convert_element_type.32.low_ref
  11.2 0.7 convert_element_type.33.lo_ref
  12.3 0.8 broadcast_in_dim.3.rw_ref
  13.1 0.9 convert_element_type.36.ld_ref
  14.0 170.9 %front.1 = (bf16[2688,256]{1,0:T(8,128)(2,1)}, bf16[2688,256]{1,0:T(8,128)(2,1)}, bf16[2688,256]{1,0:T(8,128)(2,1)}, bf16[2688,256]{1,0:T(8,128)(2,1)}, bf16[3,2...) custom-call(s32[3]{0:T(128)} %pre_ref.1, ...), custom_call_target="tpu_custom_call" | custom-call | flops 1048576 | bytes 65536 | tf_op jit(solution)/shard_map/front/pallas_call | solution.py:1058
  184.9 120.3 %ffn.1 = (bf16[336,2048]{1,0:T(8,128)(2,1)}, f32[336,2048]{1,0:T(8,128)}, bf16[336,2048]{1,0:T(8,128)(2,1)}, f32[2,2048]{1,0:T(2,128)}, bf16[4,2,336,2048]{3,2,1...) custom-call(bf16[336,2048]{1,0:T(8,128)(2,1)} %get-tuple-element.63., ...), custom_call_target="tpu_custom_call" | custom-call | flops 1048576 | bytes 65536 | tf_op jit(solution)/shard_map/ffn/pallas_call | solution.py:1333
  305.2 55.1 %ffn_back.1 = (bf16[4,2,336,2048]{3,2,1,0:T(8,128)(2,1)}, bf16[2,4,2,336,704]{4,3,2,1,0:T(8,128)(2,1)}) custom-call(bf16[336,2048]{1,0:T(8,128)(2,1)} %get-tuple-element.72.share, bf16[4,2,336,704]{3,2,1,0:T(8,128)(2,1)} %get-tuple-element.73.act_ref, bf16[4,2,336,704]{3,2,1,0:T(8,128)(2,1)} %get-tuple-element.74.pull_ref, ...), custom_call_target="tpu_custom_call" | custom-call | flops 1048576 | bytes 65536 | tf_op jit(solution)/shard_map/ffn_back/pallas_call | solution.py:1418
  360.3 13.6 %bitcast_convert_fusion = bf16[704,2048]{1,0:T(8,128)(2,1)} fusion(bf16[4,2,336,704]{3,2,1,0:T(8,128)(2,1)} %get-tuple-element.77, bf16[4,2,336,2048]{3,2,1,0:T(8,128)(2,1)} %get-tuple-element.78), kind=kOutput, calls=%fused_computation | convolution fusion | flops 7752515584 | bytes 17678336 | tf_op jit(solution)/shard_map/tf,td->fd/dot_general | solution.py:1768
  374.6 23.1 %convolution_convert_fusion.gg_ref = bf16[2,704,2048]{2,1,0:T(8,128)(2,1)} fusion(bf16[2,2688,704]{2,1,0:T(8,128)(2,1)} %bitcast.26, bf16[2688,2048,1]{1,0,2:T(8,128)(2,1)} %bitcast.31), kind=kOutput, calls=%fused_computation.1 | convolution fusion | flops 15505031168 | bytes 24346624 | tf_op jit(solution)/shard_map/jtf,td->jfd/dot_general | solution.py:1773
  397.6 64.8 %middle_back.1 = (f32[336,2048]{1,0:T(8,128)}, bf16[336,2048]{1,0:T(8,128)(2,1)}, f32[2,2048]{1,0:T(2,128)}, f32[2,96,512]{2,1,0:T(8,128)}, f32[2,112,512]{2,1,0:T(8,128)}) custom-call(bf16[2,4,2,336,704]{4,3,2,1,0:T(8,128)(2,1)} %get-tuple-element.79.dg_ref, bf16[2,704,2048]{2,1,0:T(8,128)(2,1)} %get-tuple-element.65.wg_ref, ...), custom_call_target="tpu_custom_call" | custom-call | flops 1048576 | bytes 65536 | tf_op jit(solution)/shard_map/middle_back/pallas_call | solution.py:1512
  462.5 57.8 %out_back.1 = (bf16[4,2,336,256]{3,2,1,0:T(8,128)(2,1)}, bf16[256,2048]{1,0:T(8,128)(2,1)}, f32[2,384,512]{2,1,0:T(8,128)}) custom-call(bf16[336,2048]{1,0:T(8,128)(2,1)} %get-tuple-element.85.share, bf16[256,2048]{1,0:T(8,128)(2,1)} %get-tuple-element.86.w_ref, bf16[4,2,336,256]{3,2,1,0:T(8,128)(2,1)} %bitcast.27, ...), custom_call_target="tpu_custom_call" | custom-call | flops 1048576 | bytes 65536 | tf_op jit(solution)/shard_map/out_back/pallas_call | solution.py:1583
  521.0 32.1 %attention_back.1 = (bf16[3,2688,256]{2,1,0:T(8,128)(2,1)}, f32[4,2048]{1,0:T(4,128)}, f32[256,512]{1,0:T(8,128)}) custom-call(bf16[2688,256]{1,0:T(8,128)(2,1)} %get-tuple-element.67.q_ref, bf16[2688,256]{1,0:T(8,128)(2,1)} %get-tuple-element.68.k_ref, bf16[2688,256]{1,0:T(8,128)(2,1)} %get-tuple-element.69.v_ref, ...), custom_call_target="tpu_custom_call" | custom-call | flops 1048576 | bytes 65536 | tf_op jit(solution)/shard_map/attention_back/pallas_call | solution.py:1200
  553.1 74.4 %input_back.1 = (bf16[336,2048]{1,0:T(8,128)(2,1)}, f32[3,512,256]{2,1,0:T(8,128)}, f32[2,112,512]{2,1,0:T(8,128)}) custom-call(bf16[3,4,2,336,256]{4,3,2,1,0:T(8,128)(2,1)} %bitcast.28, bf16[3,2048,256]{2,1,0:T(8,128)(2,1)} %get-tuple-element.94.w_ref, bf16[4,2,336,2048]{3,2,1,0:T(8,128)(2,1)} %bitcast.24, ...), custom_call_target="tpu_custom_call" | custom-call | flops 1048576 | bytes 65536 | tf_op jit(solution)/shard_map/input_back/pallas_call | solution.py:1677
  627.6 2.9 multiply_subtract_fusion.3
  631.3 4.9 multiply_subtract_fusion.1
  636.2 1.2 copy-done.5
  637.9 4.9 multiply_subtract_fusion
  642.8 5.1 multiply_subtract_fusion.2
  647.9 1.1 copy.56
  648.9 0.8 copy-done.10
  649.7 1.1 copy.57
  650.8 1.1 copy.58
  652.2 0.8 copy.59
  (53 shorter events, 3.7 us)
Async XLA Ops:
  7.2 4.0 copy-start.6
  7.2 635.6 %reduce-scatter.2.cloned.1.call-start = ((), (), s32[]{:S(2)}) async-start(), calls=%async_computation.1 | async-start | bytes 3604480 | tf_op jit(solution)/shard_map/reduce_scatter | solution.py:1769
  8.7 3.2 copy-start.21
  8.7 4.4 copy-start.3
  462.5 57.9 %copy-start.19 = (f32[2,2048]{1,0:T(2,128)S(1)}, f32[2,2048]{1,0:T(2,128)}, u32[]{:S(2)}) copy-start(f32[2,2048]{1,0:T(2,128)} %get-tuple-element.91) | copy-start | bytes 49156
  462.5 57.9 %copy-start.20 = (f32[2,2048]{1,0:T(2,128)S(1)}, f32[2,2048]{1,0:T(2,128)}, u32[]{:S(2)}) copy-start(f32[2,2048]{1,0:T(2,128)} %get-tuple-element.90) | copy-start | bytes 49156
  627.5 3.0 copy-start.14
  627.5 3.0 copy-start.15
  627.5 3.0 copy-start.17
  627.5 3.0 copy-start.18
  627.5 3.7 copy-start.1
  627.6 3.6 copy-start.2
  627.6 8.6 %copy-start.13 = (f32[2,96,512]{2,1,0:T(8,128)S(1)}, f32[2,96,512]{2,1,0:T(8,128)}, u32[]{:S(2)}) copy-start(f32[2,96,512]{2,1,0:T(8,128)} %get-tuple-element.99) | copy-start | bytes 1179652
  630.5 5.7 copy-start.12
  631.2 5.0 copy-start
  631.2 5.0 copy-start.4
  631.2 6.2 copy-start.5
  631.2 6.6 copy-start.8
  631.2 6.6 %copy-start.11 = (f32[2,112,512]{2,1,0:T(8,128)S(1)}, f32[2,112,512]{2,1,0:T(8,128)}, u32[]{:S(2)}) copy-start(f32[2,112,512]{2,1,0:T(8,128)} %get-tuple-element.100) | copy-start | bytes 1376260
  642.8 5.1 copy-start.9
  647.9 1.8 copy-start.10
  650.8 1.4 copy-start.7
  650.8 2.2 copy-start.16
Sparse Core Ops, SparseCore 0:
  374.0 81.8 reduce-scatter.1

commit v7 on v6

--- a/solution.py
+++ b/solution.py
@@ -1707,7 +1707,7 @@
 
 
 FRONT_SPANS = ((0, 240), (240, 464))
-SPANS = ((0, 96), (96, 112), (208, 384), (592, 112))
+SPANS = ((0, 96), (96, 128), (224, 400), (624, 80))
 
 
 def body_ring(

time: 670 us -> 667 us (level)
  transfers between devices with their start and end apart: 1 -> 1, of which waited for: 0 -> 0; matrix products, arithmetic and copies ran while one was open for 6% -> 6% of each run, Pallas kernels for 35% -> 34%
where the time goes in v7:
time: 667 us; the launch traced here: 658 us
  Pallas kernels  573 us (86%)
  matrix products  36.6 us (5%)
  other arithmetic  25.1 us (4%)
  between operations  15.2 us (2%)
  local copies, waits for them, and re-layouts  8.26 us (1%)
    pallas_call x1, Pallas kernels, front_call(): pl.pallas_call(kernel, out_shape=[jax.ShapeDtypeStruct((tokens, cols), BF...  171 us
    pallas_call x1, Pallas kernels, ffn_call(): pl.pallas_call(kernel, out_shape=[jax.ShapeDtypeStruct((rows, D), BF16),...  120 us
    pallas_call x1, Pallas kernels, input_back_call(): pl.pallas_call(kernel, out_shape=[jax.ShapeDtypeStruct((rows, D), BF16),...  70.1 us
    pallas_call x1, Pallas kernels, middle_back_call(): pl.pallas_call(kernel, out_shape=[jax.ShapeDtypeStruct((rows, D), F32), j...  64.8 us
    pallas_call x1, Pallas kernels, out_back_call(): pl.pallas_call(kernel, out_shape=[jax.ShapeDtypeStruct((4, 2, rows, cols)...  61 us
    pallas_call x1, Pallas kernels, ffn_back_call(): pl.pallas_call(kernel, out_shape=[jax.ShapeDtypeStruct((4, 2, rows, D), B...  55.1 us
    pallas_call x1, Pallas kernels, attention_back_call(): pl.pallas_call(kernel, grid=(proteins, heads), in_specs=[tile] * 3 + [pl....  30.5 us
    dot_general x1, matrix products, body_ring(): jnp.einsum('jtf,td->jfd', gateup_rows, middle_low, preferred_element_type...  23.1 us
  transfers between devices with their start and end apart: 1, of which 0 were waited for; matrix products, arithmetic and copies ran while one was open for 6% of the time, Pallas kernels for 34%

profile of v7, /device:TPU:0, one launch (start us, length us, event | category | flops | bytes accessed | tf_op | source)
XLA Modules:
  0.0 658.0 jit_solution(12937025947954261973)
XLA Ops:
  7.3 0.8 convert_element_type.34
  8.7 2.5 convert_element_type.32.low_ref
  11.2 0.7 convert_element_type.33.lo_ref
  12.3 0.8 broadcast_in_dim.3.rw_ref
  13.1 0.9 convert_element_type.36.ld_ref
  14.0 170.9 %front.1 = (bf16[2688,256]{1,0:T(8,128)(2,1)}, bf16[2688,256]{1,0:T(8,128)(2,1)}, bf16[2688,256]{1,0:T(8,128)(2,1)}, bf16[2688,256]{1,0:T(8,128)(2,1)}, bf16[3,2...) custom-call(s32[3]{0:T(128)} %pre_ref.1, ...), custom_call_target="tpu_custom_call" | custom-call | flops 1048576 | bytes 65536 | tf_op jit(solution)/shard_map/front/pallas_call | solution.py:1058
  184.9 120.3 %ffn.1 = (bf16[336,2048]{1,0:T(8,128)(2,1)}, f32[336,2048]{1,0:T(8,128)}, bf16[336,2048]{1,0:T(8,128)(2,1)}, f32[2,2048]{1,0:T(2,128)}, bf16[4,2,336,2048]{3,2,1...) custom-call(bf16[336,2048]{1,0:T(8,128)(2,1)} %get-tuple-element.63., ...), custom_call_target="tpu_custom_call" | custom-call | flops 1048576 | bytes 65536 | tf_op jit(solution)/shard_map/ffn/pallas_call | solution.py:1333
  305.2 55.1 %ffn_back.1 = (bf16[4,2,336,2048]{3,2,1,0:T(8,128)(2,1)}, bf16[2,4,2,336,704]{4,3,2,1,0:T(8,128)(2,1)}) custom-call(bf16[336,2048]{1,0:T(8,128)(2,1)} %get-tuple-element.72.share, bf16[4,2,336,704]{3,2,1,0:T(8,128)(2,1)} %get-tuple-element.73.act_ref, bf16[4,2,336,704]{3,2,1,0:T(8,128)(2,1)} %get-tuple-element.74.pull_ref, ...), custom_call_target="tpu_custom_call" | custom-call | flops 1048576 | bytes 65536 | tf_op jit(solution)/shard_map/ffn_back/pallas_call | solution.py:1418
  360.3 13.6 %bitcast_convert_fusion = bf16[704,2048]{1,0:T(8,128)(2,1)} fusion(bf16[4,2,336,704]{3,2,1,0:T(8,128)(2,1)} %get-tuple-element.77, bf16[4,2,336,2048]{3,2,1,0:T(8,128)(2,1)} %get-tuple-element.78), kind=kOutput, calls=%fused_computation | convolution fusion | flops 7752515584 | bytes 17678336 | tf_op jit(solution)/shard_map/tf,td->fd/dot_general | solution.py:1768
  374.6 23.1 %convolution_convert_fusion.gg_ref = bf16[2,704,2048]{2,1,0:T(8,128)(2,1)} fusion(bf16[2,2688,704]{2,1,0:T(8,128)(2,1)} %bitcast.26, bf16[2688,2048,1]{1,0,2:T(8,128)(2,1)} %bitcast.31), kind=kOutput, calls=%fused_computation.1 | convolution fusion | flops 15505031168 | bytes 24346624 | tf_op jit(solution)/shard_map/jtf,td->jfd/dot_general | solution.py:1773
  397.6 64.8 %middle_back.1 = (f32[336,2048]{1,0:T(8,128)}, bf16[336,2048]{1,0:T(8,128)(2,1)}, f32[2,2048]{1,0:T(2,128)}, f32[2,96,512]{2,1,0:T(8,128)}, f32[2,128,512]{2,1,0:T(8,128)}) custom-call(bf16[2,4,2,336,704]{4,3,2,1,0:T(8,128)(2,1)} %get-tuple-element.79.dg_ref, bf16[2,704,2048]{2,1,0:T(8,128)(2,1)} %get-tuple-element.65.wg_ref, ...), custom_call_target="tpu_custom_call" | custom-call | flops 1048576 | bytes 65536 | tf_op jit(solution)/shard_map/middle_back/pallas_call | solution.py:1512
  462.5 61.0 %out_back.1 = (bf16[4,2,336,256]{3,2,1,0:T(8,128)(2,1)}, bf16[256,2048]{1,0:T(8,128)(2,1)}, f32[2,400,512]{2,1,0:T(8,128)}) custom-call(bf16[336,2048]{1,0:T(8,128)(2,1)} %get-tuple-element.85.share, bf16[256,2048]{1,0:T(8,128)(2,1)} %get-tuple-element.86.w_ref, bf16[4,2,336,256]{3,2,1,0:T(8,128)(2,1)} %bitcast.27, ...), custom_call_target="tpu_custom_call" | custom-call | flops 1048576 | bytes 65536 | tf_op jit(solution)/shard_map/out_back/pallas_call | solution.py:1583
  524.1 30.5 %attention_back.1 = (bf16[3,2688,256]{2,1,0:T(8,128)(2,1)}, f32[4,2048]{1,0:T(4,128)}, f32[256,512]{1,0:T(8,128)}) custom-call(bf16[2688,256]{1,0:T(8,128)(2,1)} %get-tuple-element.67.q_ref, bf16[2688,256]{1,0:T(8,128)(2,1)} %get-tuple-element.68.k_ref, bf16[2688,256]{1,0:T(8,128)(2,1)} %get-tuple-element.69.v_ref, ...), custom_call_target="tpu_custom_call" | custom-call | flops 1048576 | bytes 65536 | tf_op jit(solution)/shard_map/attention_back/pallas_call | solution.py:1200
  554.7 70.1 %input_back.1 = (bf16[336,2048]{1,0:T(8,128)(2,1)}, f32[3,512,256]{2,1,0:T(8,128)}, f32[2,80,512]{2,1,0:T(8,128)}) custom-call(bf16[3,4,2,336,256]{4,3,2,1,0:T(8,128)(2,1)} %bitcast.28, bf16[3,2048,256]{2,1,0:T(8,128)(2,1)} %get-tuple-element.94.w_ref, bf16[4,2,336,2048]{3,2,1,0:T(8,128)(2,1)} %bitcast.24, ...), custom_call_target="tpu_custom_call" | custom-call | flops 1048576 | bytes 65536 | tf_op jit(solution)/shard_map/input_back/pallas_call | solution.py:1677
  624.9 2.9 multiply_subtract_fusion.3
  628.6 4.9 multiply_subtract_fusion.1
  633.5 1.2 copy-done.5
  635.2 4.9 multiply_subtract_fusion
  640.1 5.1 multiply_subtract_fusion.2
  645.2 1.1 copy.56
  646.3 0.8 copy-done.10
  647.1 1.1 copy.57
  648.1 1.1 copy.58
  649.5 0.8 copy.59
  (53 shorter events, 3.8 us)
Async XLA Ops:
  7.2 4.0 copy-start.6
  7.2 632.9 %reduce-scatter.2.cloned.1.call-start = ((), (), s32[]{:S(2)}) async-start(), calls=%async_computation.1 | async-start | bytes 3604480 | tf_op jit(solution)/shard_map/reduce_scatter | solution.py:1769
  8.7 3.2 copy-start.21
  8.7 4.4 copy-start.3
  462.5 61.0 %copy-start.19 = (f32[2,2048]{1,0:T(2,128)S(1)}, f32[2,2048]{1,0:T(2,128)}, u32[]{:S(2)}) copy-start(f32[2,2048]{1,0:T(2,128)} %get-tuple-element.91) | copy-start | bytes 49156
  462.5 61.0 %copy-start.20 = (f32[2,2048]{1,0:T(2,128)S(1)}, f32[2,2048]{1,0:T(2,128)}, u32[]{:S(2)}) copy-start(f32[2,2048]{1,0:T(2,128)} %get-tuple-element.90) | copy-start | bytes 49156
  624.8 3.0 copy-start.14
  624.8 3.0 copy-start.15
  624.8 3.0 copy-start.17
  624.9 3.0 copy-start.18
  624.9 3.7 copy-start.1
  624.9 3.6 copy-start.2
  624.9 8.6 %copy-start.12 = (f32[2,96,512]{2,1,0:T(8,128)S(1)}, f32[2,96,512]{2,1,0:T(8,128)}, u32[]{:S(2)}) copy-start(f32[2,96,512]{2,1,0:T(8,128)} %get-tuple-element.99) | copy-start | bytes 1179652
  627.8 5.7 copy-start.13
  628.5 5.0 copy-start
  628.5 5.0 copy-start.4
  628.5 6.2 copy-start.5
  628.6 6.6 %copy-start.8 = (f32[2,400,512]{2,1,0:T(8,128)S(1)}, f32[2,400,512]{2,1,0:T(8,128)}, u32[]{:S(2)}) copy-start(f32[2,400,512]{2,1,0:T(8,128)} %get-tuple-element.101) | copy-start | bytes 4915204
  628.6 6.7 %copy-start.11 = (f32[2,128,512]{2,1,0:T(8,128)S(1)}, f32[2,128,512]{2,1,0:T(8,128)}, u32[]{:S(2)}) copy-start(f32[2,128,512]{2,1,0:T(8,128)} %get-tuple-element.100) | copy-start | bytes 1572868
  640.1 5.1 copy-start.9
  645.2 1.8 copy-start.10
  648.1 1.4 copy-start.7
  648.1 2.2 copy-start.16
Sparse Core Ops, SparseCore 0:
  374.0 80.9 reduce-scatter.1
